TPU v7x, 256 devices: a whole 4x4x8 slice. The times are simulated.
256 devices in a mesh: ty: 16 (over y, z_lo), tx: 16 (over z_hi, x, core).
Axes of the slice: x: 4, y: 4, z: 8 (z_hi: 2, z_lo: 4; z = z_hi * 4 + z_lo), core: 2. Of those that a mesh axis runs over, the one named last changes fastest.
Arguments:
- object_field: float32 [3, 2, 2048, 2048], P(None, None, 'ty', 'tx'), may hold values from -6 to 6
- probe: float32 [2, 256, 256], replicated, may hold values from -6 to 6
- propagator_phase: float32 [256, 256], replicated, may hold values from -3.140625 to 3.140625
- patterns: float32 [16, 16, 1, 256, 256], P('ty', 'tx'), may hold values from 0 to 2
- scan_positions: int32 [16, 16, 1, 2], P('ty', 'tx'), may hold values from 0 to 255
Outputs:
- updated_object: float32 [3, 2, 2048, 2048], P(None, None, 'ty', 'tx')
All inputs are finite; a program needn't handle non-finite values.
Results may differ from a plain program's by a relative error of at most 0.0003.
Values sent between devices are 32-bit elements; how exact they have to be, the bound alone decides.
No kernel may reach another device: no remote copies, remote signals or barrier semaphores. Data moves between devices by JAX's collectives and lax.ppermute only.
A program may use at most 64 MiB of HBM per device.

v0:
```python
import functools
import math

import jax
import jax.numpy as jnp
import numpy as np
from jax import lax
from jax.experimental import pallas as pl
from jax.experimental.pallas import tpu as pltpu
from jax.sharding import PartitionSpec as P

MARGIN = 64
CORE = 128
TILE = 256
SLICES = 3
STEPS = 2
STEP_SIZE = 0.05


def half_tables():
    index = np.arange(CORE)
    tables = []
    for parity in range(2):
        freq = 2 * index + parity
        angle = 2.0 * math.pi * ((freq[:, None] * index[None, :]) % TILE) / TILE
        real, imag = np.cos(angle) / 16.0, -np.sin(angle) / 16.0
        block = np.block([[real, -imag], [imag, real]]).astype(np.float32)
        for table in (block, block.T):
            high = table.astype(jnp.bfloat16)
            low = (table - high.astype(np.float32)).astype(jnp.bfloat16)
            tables.append(np.stack([high, low]))
    return np.stack(tables)


def order_table():
    table = np.zeros((TILE, TILE), np.float32)
    index = np.arange(CORE)
    table[index, 2 * index] = 1.0
    table[CORE + index, 2 * index + 1] = 1.0
    return np.stack([table, table.T]).astype(jnp.bfloat16)


def dot(left, right):
    return jnp.dot(left, right, preferred_element_type=jnp.float32)


def split(value):
    high = value.astype(jnp.bfloat16)
    low = (value - high.astype(jnp.float32)).astype(jnp.bfloat16)
    return high, low


def from_left(tables, which, value):
    high, low = split(value)
    t_high, t_low = tables[which, 0], tables[which, 1]
    return dot(t_high, high) + (dot(t_high, low) + dot(t_low, high))


def from_right(tables, which, value):
    high, low = split(value)
    t_high, t_low = tables[which, 0], tables[which, 1]
    return dot(high, t_high) + (dot(high, t_low) + dot(low, t_high))


def stack(*rows):
    return jnp.concatenate(rows, axis=0)


def beside(*cols):
    return jnp.concatenate(cols, axis=1)


def forward(tables, real, imag):
    half = []
    for parity in range(2):
        if parity == 0:
            mixed = stack(real[:CORE] + real[CORE:], imag[:CORE] + imag[CORE:])
        else:
            mixed = stack(real[:CORE] - real[CORE:], imag[:CORE] - imag[CORE:])
        half.append(from_left(tables, 2 * parity, mixed))
    out = []
    for parity in range(2):
        rows = []
        for value in half:
            parts = []
            for part in (value[:CORE], value[CORE:]):
                first, second = part[:, :CORE], part[:, CORE:]
                parts.append(first + second if parity == 0 else first - second)
            rows.append(beside(*parts))
        out.append(from_right(tables, 2 * parity + 1, stack(*rows)))
    return out


def backward(tables, freq):
    even = from_right(tables, 0, freq[0])
    odd = from_right(tables, 2, freq[1])
    first, second = even + odd, even - odd
    half = []
    for parity in range(2):
        rows = slice(parity * CORE, (parity + 1) * CORE)
        mixed = stack(
            beside(first[rows, :CORE], second[rows, :CORE]),
            beside(first[rows, CORE:], second[rows, CORE:]),
        )
        half.append(from_left(tables, 2 * parity + 1, mixed))
    even, odd = half
    real = stack(even[:CORE] + odd[:CORE], even[:CORE] - odd[:CORE])
    imag = stack(even[CORE:] + odd[CORE:], even[CORE:] - odd[CORE:])
    return real, imag


def propagate(tables, real, imag, wave, sign):
    freq = forward(tables, real, imag)
    out = []
    for parity in range(2):
        real, imag = freq[parity][:, :CORE], freq[parity][:, CORE:]
        cols = pl.ds(parity * CORE, CORE)
        h_real, h_imag = wave[0, :, cols], wave[1, :, cols]
        if sign < 0:
            out.append(beside(real * h_real + imag * h_imag, imag * h_real - real * h_imag))
        else:
            out.append(beside(real * h_real - imag * h_imag, imag * h_real + real * h_imag))
    return backward(tables, out)


def low_lanes(shape):
    return lax.broadcasted_iota(jnp.int32, shape, len(shape) - 1) < MARGIN


def turned(value):
    return pltpu.roll(value, MARGIN, 1)


def step_kernel(
    par, mid, near, far, lit, wave, patterns, tables, part, send_near, send_far, tile, field, up
):
    even = par[1] == 0
    low = low_lanes((TILE, CORE)) == even
    for layer in range(SLICES):
        e, o = near[layer], far[layer]
        tile[layer, 0, :, :CORE] = mid[layer, 0]
        tile[layer, 1, :, :CORE] = mid[layer, 1]
        tile[layer, 0, :, CORE:] = jnp.where(low, e, o)
        tile[layer, 1, :, CORE:] = turned(jnp.where(low, o, e))
    field[0, 0] = lit[0]
    field[0, 1] = lit[1]

    def ahead(layer, carry):
        f_real, f_imag = field[layer, 0], field[layer, 1]
        t_real, t_imag = tile[layer, 0], tile[layer, 1]
        real, imag = propagate(
            tables, f_real * t_real - f_imag * t_imag, f_real * t_imag + f_imag * t_real, wave, 1
        )
        field[layer + 1, 0] = real
        field[layer + 1, 1] = imag
        return carry

    lax.fori_loop(0, SLICES - 1, ahead, 0)
    f_real, f_imag = field[SLICES - 1, 0], field[SLICES - 1, 1]
    t_real, t_imag = tile[SLICES - 1, 0], tile[SLICES - 1, 1]
    freq = forward(tables, f_real * t_real - f_imag * t_imag, f_real * t_imag + f_imag * t_real)
    out = []
    for parity in range(2):
        real, imag = freq[parity][:, :CORE], freq[parity][:, CORE:]
        residue = real * real + imag * imag - patterns[:, pl.ds(parity * CORE, CORE)]
        out.append(beside(residue * real, residue * imag))
    real, imag = backward(tables, out)
    up[0] = real
    up[1] = imag

    def gradient(layer):
        f_real, f_imag = field[layer, 0], field[layer, 1]
        u_real, u_imag = up[0], up[1]
        real = f_real * u_real + f_imag * u_imag
        imag = f_real * u_imag - f_imag * u_real
        part[layer, 0] = real[:, :CORE]
        part[layer, 1] = imag[:, :CORE]
        straight, other = real[:, CORE:], turned(imag[:, CORE:])
        send_near[layer] = jnp.where(low, straight, other)
        send_far[layer] = jnp.where(low, other, straight)

    def behind(turn, carry):
        layer = SLICES - 1 - turn
        gradient(layer)
        t_real, t_imag = tile[layer, 0], tile[layer, 1]
        u_real, u_imag = up[0], up[1]
        real, imag = propagate(
            tables, t_real * u_real + t_imag * u_imag, t_real * u_imag - t_imag * u_real, wave, -1
        )
        up[0] = real
        up[1] = imag
        return carry

    lax.fori_loop(0, SLICES - 1, behind, 0)
    gradient(0)


def call(body, outs, scratch=(), smem=1, count=0):
    return pl.pallas_call(
        body,
        out_shape=[jax.ShapeDtypeStruct(shape, jnp.float32) for shape in outs],
        in_specs=[pl.BlockSpec(memory_space=pltpu.SMEM)] * smem
        + [pl.BlockSpec(memory_space=pltpu.VMEM)] * count,
        out_specs=[pl.BlockSpec(memory_space=pltpu.VMEM)] * len(outs),
        scratch_shapes=list(scratch),
        name=body.__name__,
    )


PART = (SLICES, 2, TILE, CORE)
PACK = (SLICES, TILE, CORE)


def step(*args):
    return call(
        step_kernel,
        (PART, PACK, PACK),
        (
            pltpu.VMEM((SLICES, 2, TILE, TILE), jnp.float32),
            pltpu.VMEM((SLICES, 2, TILE, TILE), jnp.float32),
            pltpu.VMEM((2, TILE, TILE), jnp.float32),
        ),
        count=7,
    )(*args)


def three(value):
    high = value.astype(jnp.bfloat16)
    rest = value - high.astype(jnp.float32)
    middle = rest.astype(jnp.bfloat16)
    low = (rest - middle.astype(jnp.float32)).astype(jnp.bfloat16)
    return high, middle, low


def reorder(order, value):
    high, middle, low = three(value)
    rows = (dot(order[0], high) + dot(order[0], middle)) + dot(order[0], low)
    high, middle, low = three(rows)
    return (dot(high, order[1]) + dot(middle, order[1])) + dot(low, order[1])


def setup_kernel(positions, probe, phase, patterns, order, lit, ordered_phase, ordered_patterns):
    rows = lax.rem(positions[0] + (TILE - MARGIN), TILE)
    cols = lax.rem(positions[1] + (TILE - MARGIN), TILE)
    for part in range(2):
        lit[part] = pltpu.roll(pltpu.roll(probe[part], rows, 0), cols, 1)
    ordered_phase[...] = reorder(order, phase[...])
    ordered_patterns[...] = reorder(order, patterns[...])


def setup(positions, probe, phase, patterns, order):
    shapes = ((2, TILE, TILE), (TILE, TILE), (TILE, TILE))
    return call(setup_kernel, shapes, count=4)(positions, probe, phase, patterns, order)


def pack_columns(even, mid, send_near, send_far):
    low = low_lanes((TILE, CORE)) == even
    for layer in range(SLICES):
        straight, other = mid[layer, 0], turned(mid[layer, 1])
        send_near[layer] = jnp.where(low, other, straight)
        send_far[layer] = jnp.where(low, straight, other)


def assemble_kernel(par, core, near, far, mid, send_near, send_far):
    even = par[0] == 0
    for layer in range(SLICES):
        for part in range(2):
            e, o = near[layer, part], far[layer, part]
            mid[layer, part, :CORE] = core[layer, part]
            mid[layer, part, CORE : CORE + MARGIN] = jnp.where(even, e, o)
            mid[layer, part, CORE + MARGIN :] = jnp.where(even, o, e)
    pack_columns(par[1] == 0, mid, send_near, send_far)


def assemble(*args):
    return call(assemble_kernel, (PART, PACK, PACK), count=3)(*args)


def add_columns(even, part, near, far):
    low = low_lanes((TILE, CORE)) == even
    out = []
    for layer in range(SLICES):
        e, o = near[layer], far[layer]
        out.append(
            (
                part[layer, 0] + jnp.where(low, o, e),
                part[layer, 1] + turned(jnp.where(low, e, o)),
            )
        )
    return out


def share_kernel(par, part, near, far, total, send_near, send_far):
    even = par[0] == 0
    sums = add_columns(par[1] == 0, part, near, far)
    for layer in range(SLICES):
        for c in range(2):
            value = sums[layer][c]
            total[layer, c] = value
            a, b, d, e = (value[k * MARGIN : (k + 1) * MARGIN] for k in range(4))
            send_near[layer, c, :MARGIN] = jnp.where(even, b, e)
            send_near[layer, c, MARGIN:] = jnp.where(even, d, a)
            send_far[layer, c, :MARGIN] = jnp.where(even, e, b)
            send_far[layer, c, MARGIN:] = jnp.where(even, a, d)


def share(*args):
    half = (SLICES, 2, CORE, CORE)
    return call(share_kernel, (PART, half, half), count=3)(*args)


def update_kernel(par, mid, total, near, far, new, send_near, send_far):
    even = par[0] == 0
    above = jnp.where(par[2] == 0, 0.0, STEP_SIZE)
    below = jnp.where(par[3] == 0, 0.0, STEP_SIZE)
    for layer in range(SLICES):
        for c in range(2):
            e, o = near[layer, c], far[layer, c]
            down = jnp.where(even, e, o)
            up = jnp.where(even, o, e)
            for k, (added, scale) in enumerate(
                (
                    (up[MARGIN:], STEP_SIZE),
                    (down[:MARGIN], STEP_SIZE),
                    (down[MARGIN:], below),
                    (up[:MARGIN], above),
                )
            ):
                rows = pl.ds(k * MARGIN, MARGIN)
                new[layer, c, rows] = mid[layer, c, rows] - scale * (total[layer, c, rows] + added)
    pack_columns(par[1] == 0, new, send_near, send_far)


def update(*args):
    return call(update_kernel, (PART, PACK, PACK), count=4)(*args)


def close_kernel(par, part, near, far, total, send_near, send_far):
    even = par[0] == 0
    sums = add_columns(par[1] == 0, part, near, far)
    for layer in range(SLICES):
        for c in range(2):
            value = sums[layer][c]
            total[layer, c] = value[:CORE]
            below, above = value[CORE : CORE + MARGIN], value[CORE + MARGIN :]
            send_near[layer, c] = jnp.where(even, below, above)
            send_far[layer, c] = jnp.where(even, above, below)


def close(*args):
    rim = (SLICES, 2, MARGIN, CORE)
    return call(close_kernel, ((SLICES, 2, CORE, CORE), rim, rim), count=3)(*args)


def finish_kernel(par, mid, total, near, far, out):
    even = par[0] == 0
    for layer in range(SLICES):
        for c in range(2):
            e, o = near[layer, c], far[layer, c]
            for k, added in enumerate((jnp.where(even, o, e), jnp.where(even, e, o))):
                rows = pl.ds(k * MARGIN, MARGIN)
                out[layer, c, rows] = mid[layer, c, rows] - STEP_SIZE * (
                    total[layer, c, rows] + added
                )


def finish(*args):
    return call(finish_kernel, ((SLICES, 2, CORE, CORE),), count=4)(*args)[0]


def swap(axis, near, far):
    count = lax.axis_size(axis)

    def route(first):
        pairs = [(i, i + 1) for i in range(first, count - 1, 2)]
        return pairs + [(j, i) for i, j in pairs]

    far = lax.ppermute(far, axis, route(1))
    near = lax.ppermute(near, axis, route(0))
    return near, far


def shards(object_field, probe, propagator_phase, patterns, scan_positions):
    row, col = lax.axis_index("ty"), lax.axis_index("tx")
    par = jnp.stack([row % 2, col % 2, row, lax.axis_size("ty") - 1 - row]).astype(jnp.int32)
    even = row % 2 == 0
    top, bottom = object_field[:, :, :MARGIN], object_field[:, :, MARGIN:]
    near, far = swap("ty", jnp.where(even, bottom, top), jnp.where(even, top, bottom))
    lit, phase, ordered = setup(
        scan_positions[0, 0, 0], probe, propagator_phase, patterns[0, 0, 0], order_table()
    )
    wave = jnp.stack([jnp.cos(phase), jnp.sin(phase)])
    tables = jnp.asarray(half_tables())
    mid, near, far = assemble(par, object_field, near, far)
    for turn in range(STEPS):
        near, far = swap("tx", near, far)
        part, near, far = step(par, mid, near, far, lit, wave, ordered, tables)
        near, far = swap("tx", near, far)
        if turn < STEPS - 1:
            total, near, far = share(par, part, near, far)
            near, far = swap("ty", near, far)
            mid, near, far = update(par, mid, total, near, far)
    total, near, far = close(par, part, near, far)
    near, far = swap("ty", near, far)
    return finish(par, mid, total, near, far)


def solution(mesh):
    placed = (
        P(None, None, "ty", "tx"),
        P(),
        P(),
        P("ty", "tx", None, None, None),
        P("ty", "tx", None, None),
    )
    return jax.shard_map(
        shards, mesh=mesh, in_specs=placed, out_specs=P(None, None, "ty", "tx"), check_vma=False
    )
```

profile of v0, /device:TPU:232, one launch (start us, length us, event | category | flops | bytes accessed | tf_op | source)
XLA Modules:
  0.0 151.6 jit_solution(12133810602842018485)
XLA Ops:
  0.0 1.1 slice_select_fusion
  1.1 4.8 %collective-permute-start.1 = (f32[3,2,64,128]{3,2,1,0:T(8,128)S(1)}, f32[3,2,64,128]{3,2,1,0:T(8,128)S(1)}, u32[]{:S(2)}, u32[]{:S(2)}) collective-permute-start(f32[3,2,64,128]{3,2,1,0:T(8,128)S(1)} %get-tuple-element.47), channel_id=1, source_target_pairs={{16,32},{48,64},{80,96},{112,128},{144,160},{176,192},{208,224},{3... | collective-permute-start | bytes 589832 | tf_op jit(solution)/shard_map/ppermute | solution.py:378
  5.9 0.1 collective-permute-start
  6.0 0.6 pad_add_fusion.par
  6.6 6.8 %collective-permute-done.1.far = f32[3,2,64,128]{3,2,1,0:T(8,128)S(1)} collective-permute-done((f32[3,2,64,128]{3,2,1,0:T(8,128)S(1)}, f32[3,2,64,128]{3,2,1,0:T(8,128)S(1)}, u32[]{:S(2)}, u32[]{:S(2)}) %collective-permute-start.1) | collective-permute-done | bytes 196640 | tf_op jit(solution)/shard_map/ppermute | solution.py:378
  13.4 0.0 copy-start.12
  13.4 2.2 %collective-permute-done.near = f32[3,2,64,128]{3,2,1,0:T(8,128)S(1)} collective-permute-done((f32[3,2,64,128]{3,2,1,0:T(8,128)S(1)}, f32[3,2,64,128]{3,2,1,0:T(8,128)S(1)}, u32[]{:S(2)}, u32[]{:S(2)}) %collective-permute-start) | collective-permute-done | bytes 196640 | tf_op jit(solution)/shard_map/ppermute | solution.py:379
  15.6 0.0 copy-done.12
  15.6 0.0 copy-start.13
  15.6 0.7 copy-done.13
  16.3 2.4 %assemble_kernel.1 = (f32[3,2,256,128]{3,2,1,0:T(8,128)}, f32[3,256,128]{2,1,0:T(8,128)}, f32[3,256,128]{2,1,0:T(8,128)}) custom-call(s32[4]{0:T(128)} %pad_add_fusion.par, f32[3,2,128,128]{3,2,1,0:T(8,128)} %core.1, f32[3,2,64,128]{3,2,1,0:T(8,128)} %copy-done.13, f32[3,2,64,128]{3,2,1,0:T(8,128)} %copy-done.12), custom_call_target="tpu_custom_call" | custom-call | tf_op jit(solution)/shard_map/assemble_kernel/pallas_call | solution.py:276
  18.7 0.0 collective-permute-start.2
  18.7 4.1 %collective-permute-start.3 = (f32[3,256,128]{2,1,0:T(8,128)}, f32[3,256,128]{2,1,0:T(8,128)S(1)}, u32[]{:S(2)}, u32[]{:S(2)}) collective-permute-start(f32[3,256,128]{2,1,0:T(8,128)} %get-tuple-element.28), channel_id=1, source_target_pairs={{1,2},{3,4},{5,6},{7,8},{9,10},{11,12},{13,14},{2,1},{4,3},{6,5},{... | collective-permute-start | bytes 1179656 | tf_op jit(solution)/shard_map/ppermute | solution.py:378
  22.8 3.0 %setup_kernel.1 = (f32[2,256,256]{2,1,0:T(8,128)}, f32[256,256]{1,0:T(8,128)}, f32[256,256]{1,0:T(8,128)}) custom-call(s32[2]{0:T(128)} %bitcast.11, f32[2,256,256]{2,1,0:T(8,128)} %probe.1, f32[256,256]{1,0:T(8,128)} %phase.1, f32[256,256]{1,0:T(8,128)} %bitcast.10, bf16[2,256,256]{2,1,0:T(8,128)(2,1)} %constant.33.clone.order), custom_call_target="tpu_custom_call" | custom-call | tf_op jit(solution)/shard_map/setup_kernel/pallas_call | solution.py:253
  25.8 1.9 %cosine_bitcast_fusion = (f32[1,256,256]{2,1,0:T(8,128)S(1)}, f32[1,256,256]{2,1,0:T(8,128)S(1)}) fusion(f32[256,256]{1,0:T(8,128)} %get-tuple-element.30), kind=kLoop, calls=%fused_computation.2 | loop fusion | bytes 786432 | tf_op jit(solution)/shard_map/stack | solution.py:392
  27.7 0.8 pad_maximum_fusion.wave
  28.5 0.0 collective-permute-done.2.near
  28.5 0.0 copy-start
  28.5 5.6 %collective-permute-done.3.far = f32[3,256,128]{2,1,0:T(8,128)S(1)} collective-permute-done((f32[3,256,128]{2,1,0:T(8,128)}, f32[3,256,128]{2,1,0:T(8,128)S(1)}, u32[]{:S(2)}, u32[]{:S(2)}) %collective-permute-start.3) | collective-permute-done | bytes 393248 | tf_op jit(solution)/shard_map/ppermute | solution.py:378
  34.1 0.0 copy-start.1
  34.1 0.0 copy-done
  34.1 0.7 copy-done.1
  34.9 10.6 %step_kernel.2 = (f32[3,2,256,128]{3,2,1,0:T(8,128)}, f32[3,256,128]{2,1,0:T(8,128)}, f32[3,256,128]{2,1,0:T(8,128)}) custom-call(s32[4]{0:T(128)} %pad_add_fusion.par, f32[3,2,256,128]{3,2,1,0:T(8,128)} %get-tuple-element.26.mid, f32[3,256,128]{2,1,0:T(8,128)} %copy-done, f32[3,256,128]{2,1,0:T(8,128)} %copy-done.1, f32[2,256,256]{2,1,0:T(8,128)} %get-tuple-element.29.lit, ...), custom_call_target="tpu_custom_call" | custom-call | tf_op jit(solution)/shard_map/step_kernel/pallas_call | solution.py:215
  45.5 0.0 collective-permute-start.4
  45.5 4.1 %collective-permute-start.5 = (f32[3,256,128]{2,1,0:T(8,128)}, f32[3,256,128]{2,1,0:T(8,128)S(1)}, u32[]{:S(2)}, u32[]{:S(2)}) collective-permute-start(f32[3,256,128]{2,1,0:T(8,128)} %get-tuple-element.34), channel_id=1, source_target_pairs={{1,2},{3,4},{5,6},{7,8},{9,10},{11,12},{13,14},{2,1},{4,3},{6,5},{... | collective-permute-start | bytes 1179656 | tf_op jit(solution)/shard_map/ppermute | solution.py:378
  49.6 0.0 collective-permute-done.4.near
  49.7 0.0 copy-start.6
  49.7 11.2 %collective-permute-done.5.far = f32[3,256,128]{2,1,0:T(8,128)S(1)} collective-permute-done((f32[3,256,128]{2,1,0:T(8,128)}, f32[3,256,128]{2,1,0:T(8,128)S(1)}, u32[]{:S(2)}, u32[]{:S(2)}) %collective-permute-start.5) | collective-permute-done | bytes 393248 | tf_op jit(solution)/shard_map/ppermute | solution.py:378
  60.9 0.0 copy-start.8
  60.9 0.0 copy-done.6
  60.9 0.7 copy-done.8
  61.7 2.7 %share_kernel.1 = (f32[3,2,256,128]{3,2,1,0:T(8,128)}, f32[3,2,128,128]{3,2,1,0:T(8,128)}, f32[3,2,128,128]{3,2,1,0:T(8,128)}) custom-call(s32[4]{0:T(128)} %pad_add_fusion.par, f32[3,2,256,128]{3,2,1,0:T(8,128)} %get-tuple-element.32.part, f32[3,256,128]{2,1,0:T(8,128)} %copy-done.6, f32[3,256,128]{2,1,0:T(8,128)} %copy-done.8), custom_call_target="tpu_custom_call" | custom-call | tf_op jit(solution)/shard_map/share_kernel/pallas_call | solution.py:309
  64.4 6.0 %collective-permute-start.6 = (f32[3,2,128,128]{3,2,1,0:T(8,128)}, f32[3,2,128,128]{3,2,1,0:T(8,128)S(1)}, u32[]{:S(2)}, u32[]{:S(2)}) collective-permute-start(f32[3,2,128,128]{3,2,1,0:T(8,128)} %get-tuple-element.36), channel_id=1, source_target_pairs={{0,16},{32,48},{64,80},{96,112},{128,144},{160,176},{192,208},{224... | collective-permute-start | bytes 1179656 | tf_op jit(solution)/shard_map/ppermute | solution.py:379
  70.3 5.0 %collective-permute-start.7 = (f32[3,2,128,128]{3,2,1,0:T(8,128)}, f32[3,2,128,128]{3,2,1,0:T(8,128)S(1)}, u32[]{:S(2)}, u32[]{:S(2)}) collective-permute-start(f32[3,2,128,128]{3,2,1,0:T(8,128)} %get-tuple-element.37), channel_id=1, source_target_pairs={{16,32},{48,64},{80,96},{112,128},{144,160},{176,192},{208,224},{3... | collective-permute-start | bytes 1179656 | tf_op jit(solution)/shard_map/ppermute | solution.py:378
  75.3 3.0 %collective-permute-done.6.near = f32[3,2,128,128]{3,2,1,0:T(8,128)S(1)} collective-permute-done((f32[3,2,128,128]{3,2,1,0:T(8,128)}, f32[3,2,128,128]{3,2,1,0:T(8,128)S(1)}, u32[]{:S(2)}, u32[]{:S(2)}) %collective-permute-start.6) | collective-permute-done | bytes 393248 | tf_op jit(solution)/shard_map/ppermute | solution.py:379
  78.3 0.0 copy-start.3
  78.3 5.6 %collective-permute-done.7.far = f32[3,2,128,128]{3,2,1,0:T(8,128)S(1)} collective-permute-done((f32[3,2,128,128]{3,2,1,0:T(8,128)}, f32[3,2,128,128]{3,2,1,0:T(8,128)S(1)}, u32[]{:S(2)}, u32[]{:S(2)}) %collective-permute-start.7) | collective-permute-done | bytes 393248 | tf_op jit(solution)/shard_map/ppermute | solution.py:378
  83.9 0.0 copy-done.3
  83.9 0.7 copy-done.5
  84.7 3.0 %update_kernel.1 = (f32[3,2,256,128]{3,2,1,0:T(8,128)}, f32[3,256,128]{2,1,0:T(8,128)}, f32[3,256,128]{2,1,0:T(8,128)}) custom-call(s32[4]{0:T(128)} %pad_add_fusion.par, f32[3,2,256,128]{3,2,1,0:T(8,128)} %get-tuple-element.26.mid, f32[3,2,256,128]{3,2,1,0:T(8,128)} %get-tuple-element.35.total, f32[3,2,128,128]{3,2,1,0:T(8,128)} %copy-done.3, ...), custom_call_target="tpu_custom_call" | custom-call | tf_op jit(solution)/shard_map/update_kernel/pallas_call | solution.py:335
  87.6 0.0 collective-permute-start.8
  87.6 5.6 %collective-permute-start.9 = (f32[3,256,128]{2,1,0:T(8,128)}, f32[3,256,128]{2,1,0:T(8,128)S(1)}, u32[]{:S(2)}, u32[]{:S(2)}) collective-permute-start(f32[3,256,128]{2,1,0:T(8,128)} %get-tuple-element.40), channel_id=1, source_target_pairs={{1,2},{3,4},{5,6},{7,8},{9,10},{11,12},{13,14},{2,1},{4,3},{6,5},{... | collective-permute-start | bytes 1179656 | tf_op jit(solution)/shard_map/ppermute | solution.py:378
  93.2 0.0 collective-permute-done.8.near
  93.3 0.0 copy-start.2
  93.3 9.8 %collective-permute-done.9.far = f32[3,256,128]{2,1,0:T(8,128)S(1)} collective-permute-done((f32[3,256,128]{2,1,0:T(8,128)}, f32[3,256,128]{2,1,0:T(8,128)S(1)}, u32[]{:S(2)}, u32[]{:S(2)}) %collective-permute-start.9) | collective-permute-done | bytes 393248 | tf_op jit(solution)/shard_map/ppermute | solution.py:378
  103.0 0.0 copy-done.2
  103.0 0.7 copy-done.4
  103.8 10.6 %step_kernel.3 = (f32[3,2,256,128]{3,2,1,0:T(8,128)}, f32[3,256,128]{2,1,0:T(8,128)}, f32[3,256,128]{2,1,0:T(8,128)}) custom-call(s32[4]{0:T(128)} %pad_add_fusion.par, f32[3,2,256,128]{3,2,1,0:T(8,128)} %get-tuple-element.38.mid, f32[3,256,128]{2,1,0:T(8,128)} %copy-done.2, f32[3,256,128]{2,1,0:T(8,128)} %copy-done.4, ...), custom_call_target="tpu_custom_call" | custom-call | tf_op jit(solution)/shard_map/step_kernel/pallas_call | solution.py:215
  114.4 0.0 collective-permute-start.10
  114.4 5.6 %collective-permute-start.11 = (f32[3,256,128]{2,1,0:T(8,128)}, f32[3,256,128]{2,1,0:T(8,128)S(1)}, u32[]{:S(2)}, u32[]{:S(2)}) collective-permute-start(f32[3,256,128]{2,1,0:T(8,128)} %get-tuple-element.43), channel_id=1, source_target_pairs={{1,2},{3,4},{5,6},{7,8},{9,10},{11,12},{13,14},{2,1},{4,3},{6,5},{... | collective-permute-start | bytes 1179656 | tf_op jit(solution)/shard_map/ppermute | solution.py:378
  120.0 0.0 collective-permute-done.10.near
  120.0 0.0 copy-start.7
  120.1 9.8 %collective-permute-done.11.far = f32[3,256,128]{2,1,0:T(8,128)S(1)} collective-permute-done((f32[3,256,128]{2,1,0:T(8,128)}, f32[3,256,128]{2,1,0:T(8,128)S(1)}, u32[]{:S(2)}, u32[]{:S(2)}) %collective-permute-start.11) | collective-permute-done | bytes 393248 | tf_op jit(solution)/shard_map/ppermute | solution.py:378
  129.8 0.0 copy-done.7
  129.8 0.7 copy-done.9
  130.5 2.4 %close_kernel.1 = (f32[3,2,128,128]{3,2,1,0:T(8,128)}, f32[3,2,64,128]{3,2,1,0:T(8,128)}, f32[3,2,64,128]{3,2,1,0:T(8,128)}) custom-call(s32[4]{0:T(128)} %pad_add_fusion.par, f32[3,2,256,128]{3,2,1,0:T(8,128)} %get-tuple-element.41.part, f32[3,256,128]{2,1,0:T(8,128)} %copy-done.7, f32[3,256,128]{2,1,0:T(8,128)} %copy-done.9), custom_call_target="tpu_custom_call" | custom-call | tf_op jit(solution)/shard_map/close_kernel/pallas_call | solution.py:352
  133.0 5.3 %collective-permute-start.12 = (f32[3,2,64,128]{3,2,1,0:T(8,128)}, f32[3,2,64,128]{3,2,1,0:T(8,128)S(1)}, u32[]{:S(2)}, u32[]{:S(2)}) collective-permute-start(f32[3,2,64,128]{3,2,1,0:T(8,128)} %get-tuple-element.45), channel_id=1, source_target_pairs={{0,16},{32,48},{64,80},{96,112},{128,144},{160,176},{192,208},{224... | collective-permute-start | bytes 589832 | tf_op jit(solution)/shard_map/ppermute | solution.py:379
  138.3 5.3 %collective-permute-start.13 = (f32[3,2,64,128]{3,2,1,0:T(8,128)}, f32[3,2,64,128]{3,2,1,0:T(8,128)S(1)}, u32[]{:S(2)}, u32[]{:S(2)}) collective-permute-start(f32[3,2,64,128]{3,2,1,0:T(8,128)} %get-tuple-element.46), channel_id=1, source_target_pairs={{16,32},{48,64},{80,96},{112,128},{144,160},{176,192},{208,224},{3... | collective-permute-start | bytes 589832 | tf_op jit(solution)/shard_map/ppermute | solution.py:378
  143.5 0.0 collective-permute-done.12.near
  143.6 0.0 copy-start.10
  143.6 5.2 %collective-permute-done.13.far = f32[3,2,64,128]{3,2,1,0:T(8,128)S(1)} collective-permute-done((f32[3,2,64,128]{3,2,1,0:T(8,128)}, f32[3,2,64,128]{3,2,1,0:T(8,128)S(1)}, u32[]{:S(2)}, u32[]{:S(2)}) %collective-permute-start.13) | collective-permute-done | bytes 196640 | tf_op jit(solution)/shard_map/ppermute | solution.py:378
  148.8 0.0 copy-done.10
  148.8 0.7 copy-done.11
  149.5 2.2 %finish_kernel.1 = f32[3,2,128,128]{3,2,1,0:T(8,128)} custom-call(s32[4]{0:T(128)} %pad_add_fusion.par, f32[3,2,256,128]{3,2,1,0:T(8,128)} %get-tuple-element.38.mid, f32[3,2,128,128]{3,2,1,0:T(8,128)} %get-tuple-element.44.total, f32[3,2,64,128]{3,2,1,0:T(8,128)} %copy-done.10, f32[3,2,64,128]{3,2,1,0:T(8,128)} %copy-done.11), custom_call_target="tpu_custom_call" | custom-call | tf_op jit(solution)/shard_map/finish_kernel/pallas_call | solution.py:368
  (4 shorter events, 0.0 us)
Async XLA Ops:
  1.1 12.4 %collective-permute-start.1 = (f32[3,2,64,128]{3,2,1,0:T(8,128)S(1)}, f32[3,2,64,128]{3,2,1,0:T(8,128)S(1)}, u32[]{:S(2)}, u32[]{:S(2)}) collective-permute-start(f32[3,2,64,128]{3,2,1,0:T(8,128)S(1)} %get-tuple-element.47), channel_id=1, source_target_pairs={{16,32},{48,64},{80,96},{112,128},{144,160},{176,192},{208,224},{3... | collective-permute-start | bytes 589832 | tf_op jit(solution)/shard_map/ppermute | solution.py:378
  5.9 9.7 %collective-permute-start = (f32[3,2,64,128]{3,2,1,0:T(8,128)S(1)}, f32[3,2,64,128]{3,2,1,0:T(8,128)S(1)}, u32[]{:S(2)}, u32[]{:S(2)}) collective-permute-start(f32[3,2,64,128]{3,2,1,0:T(8,128)S(1)} %get-tuple-element.48), channel_id=1, source_target_pairs={{0,16},{32,48},{64,80},{96,112},{128,144},{160,176},{192,208},{224... | collective-permute-start | bytes 589832 | tf_op jit(solution)/shard_map/ppermute | solution.py:379
  13.4 2.2 %copy-start.12 = (f32[3,2,64,128]{3,2,1,0:T(8,128)}, f32[3,2,64,128]{3,2,1,0:T(8,128)S(1)}, u32[]{:S(2)}) copy-start(f32[3,2,64,128]{3,2,1,0:T(8,128)S(1)} %collective-permute-done.1.far) | copy-start | bytes 589828
  15.6 0.7 copy-start.13
  18.7 9.8 %collective-permute-start.2 = (f32[3,256,128]{2,1,0:T(8,128)}, f32[3,256,128]{2,1,0:T(8,128)S(1)}, u32[]{:S(2)}, u32[]{:S(2)}) collective-permute-start(f32[3,256,128]{2,1,0:T(8,128)} %get-tuple-element.27), channel_id=1, source_target_pairs={{0,1},{2,3},{4,5},{6,7},{8,9},{10,11},{12,13},{14,15},{1,0},{3,2},... | collective-permute-start | bytes 1179656 | tf_op jit(solution)/shard_map/ppermute | solution.py:379
  18.7 15.4 %collective-permute-start.3 = (f32[3,256,128]{2,1,0:T(8,128)}, f32[3,256,128]{2,1,0:T(8,128)S(1)}, u32[]{:S(2)}, u32[]{:S(2)}) collective-permute-start(f32[3,256,128]{2,1,0:T(8,128)} %get-tuple-element.28), channel_id=1, source_target_pairs={{1,2},{3,4},{5,6},{7,8},{9,10},{11,12},{13,14},{2,1},{4,3},{6,5},{... | collective-permute-start | bytes 1179656 | tf_op jit(solution)/shard_map/ppermute | solution.py:378
  28.5 5.6 %copy-start = (f32[3,256,128]{2,1,0:T(8,128)}, f32[3,256,128]{2,1,0:T(8,128)S(1)}, u32[]{:S(2)}) copy-start(f32[3,256,128]{2,1,0:T(8,128)S(1)} %collective-permute-done.2.near) | copy-start | bytes 1179652
  34.1 0.7 copy-start.1
  45.5 4.2 %collective-permute-start.4 = (f32[3,256,128]{2,1,0:T(8,128)}, f32[3,256,128]{2,1,0:T(8,128)S(1)}, u32[]{:S(2)}, u32[]{:S(2)}) collective-permute-start(f32[3,256,128]{2,1,0:T(8,128)} %get-tuple-element.33), channel_id=1, source_target_pairs={{0,1},{2,3},{4,5},{6,7},{8,9},{10,11},{12,13},{14,15},{1,0},{3,2},... | collective-permute-start | bytes 1179656 | tf_op jit(solution)/shard_map/ppermute | solution.py:379
  45.5 15.4 %collective-permute-start.5 = (f32[3,256,128]{2,1,0:T(8,128)}, f32[3,256,128]{2,1,0:T(8,128)S(1)}, u32[]{:S(2)}, u32[]{:S(2)}) collective-permute-start(f32[3,256,128]{2,1,0:T(8,128)} %get-tuple-element.34), channel_id=1, source_target_pairs={{1,2},{3,4},{5,6},{7,8},{9,10},{11,12},{13,14},{2,1},{4,3},{6,5},{... | collective-permute-start | bytes 1179656 | tf_op jit(solution)/shard_map/ppermute | solution.py:378
  49.7 11.3 %copy-start.6 = (f32[3,256,128]{2,1,0:T(8,128)}, f32[3,256,128]{2,1,0:T(8,128)S(1)}, u32[]{:S(2)}) copy-start(f32[3,256,128]{2,1,0:T(8,128)S(1)} %collective-permute-done.4.near) | copy-start | bytes 1179652
  60.9 0.7 copy-start.8
  64.4 14.0 %collective-permute-start.6 = (f32[3,2,128,128]{3,2,1,0:T(8,128)}, f32[3,2,128,128]{3,2,1,0:T(8,128)S(1)}, u32[]{:S(2)}, u32[]{:S(2)}) collective-permute-start(f32[3,2,128,128]{3,2,1,0:T(8,128)} %get-tuple-element.36), channel_id=1, source_target_pairs={{0,16},{32,48},{64,80},{96,112},{128,144},{160,176},{192,208},{224... | collective-permute-start | bytes 1179656 | tf_op jit(solution)/shard_map/ppermute | solution.py:379
  70.3 13.6 %collective-permute-start.7 = (f32[3,2,128,128]{3,2,1,0:T(8,128)}, f32[3,2,128,128]{3,2,1,0:T(8,128)S(1)}, u32[]{:S(2)}, u32[]{:S(2)}) collective-permute-start(f32[3,2,128,128]{3,2,1,0:T(8,128)} %get-tuple-element.37), channel_id=1, source_target_pairs={{16,32},{48,64},{80,96},{112,128},{144,160},{176,192},{208,224},{3... | collective-permute-start | bytes 1179656 | tf_op jit(solution)/shard_map/ppermute | solution.py:378
  78.3 5.6 %copy-start.3 = (f32[3,2,128,128]{3,2,1,0:T(8,128)}, f32[3,2,128,128]{3,2,1,0:T(8,128)S(1)}, u32[]{:S(2)}) copy-start(f32[3,2,128,128]{3,2,1,0:T(8,128)S(1)} %collective-permute-done.6.near) | copy-start | bytes 1179652
  83.9 0.7 copy-start.5
  87.6 5.6 %collective-permute-start.8 = (f32[3,256,128]{2,1,0:T(8,128)}, f32[3,256,128]{2,1,0:T(8,128)S(1)}, u32[]{:S(2)}, u32[]{:S(2)}) collective-permute-start(f32[3,256,128]{2,1,0:T(8,128)} %get-tuple-element.39), channel_id=1, source_target_pairs={{0,1},{2,3},{4,5},{6,7},{8,9},{10,11},{12,13},{14,15},{1,0},{3,2},... | collective-permute-start | bytes 1179656 | tf_op jit(solution)/shard_map/ppermute | solution.py:379
  87.6 15.4 %collective-permute-start.9 = (f32[3,256,128]{2,1,0:T(8,128)}, f32[3,256,128]{2,1,0:T(8,128)S(1)}, u32[]{:S(2)}, u32[]{:S(2)}) collective-permute-start(f32[3,256,128]{2,1,0:T(8,128)} %get-tuple-element.40), channel_id=1, source_target_pairs={{1,2},{3,4},{5,6},{7,8},{9,10},{11,12},{13,14},{2,1},{4,3},{6,5},{... | collective-permute-start | bytes 1179656 | tf_op jit(solution)/shard_map/ppermute | solution.py:378
  93.3 9.8 %copy-start.2 = (f32[3,256,128]{2,1,0:T(8,128)}, f32[3,256,128]{2,1,0:T(8,128)S(1)}, u32[]{:S(2)}) copy-start(f32[3,256,128]{2,1,0:T(8,128)S(1)} %collective-permute-done.8.near) | copy-start | bytes 1179652
  103.0 0.7 copy-start.4
  114.4 5.6 %collective-permute-start.10 = (f32[3,256,128]{2,1,0:T(8,128)}, f32[3,256,128]{2,1,0:T(8,128)S(1)}, u32[]{:S(2)}, u32[]{:S(2)}) collective-permute-start(f32[3,256,128]{2,1,0:T(8,128)} %get-tuple-element.42), channel_id=1, source_target_pairs={{0,1},{2,3},{4,5},{6,7},{8,9},{10,11},{12,13},{14,15},{1,0},{3,2},... | collective-permute-start | bytes 1179656 | tf_op jit(solution)/shard_map/ppermute | solution.py:379
  114.4 15.4 %collective-permute-start.11 = (f32[3,256,128]{2,1,0:T(8,128)}, f32[3,256,128]{2,1,0:T(8,128)S(1)}, u32[]{:S(2)}, u32[]{:S(2)}) collective-permute-start(f32[3,256,128]{2,1,0:T(8,128)} %get-tuple-element.43), channel_id=1, source_target_pairs={{1,2},{3,4},{5,6},{7,8},{9,10},{11,12},{13,14},{2,1},{4,3},{6,5},{... | collective-permute-start | bytes 1179656 | tf_op jit(solution)/shard_map/ppermute | solution.py:378
  120.0 9.8 %copy-start.7 = (f32[3,256,128]{2,1,0:T(8,128)}, f32[3,256,128]{2,1,0:T(8,128)S(1)}, u32[]{:S(2)}) copy-start(f32[3,256,128]{2,1,0:T(8,128)S(1)} %collective-permute-done.10.near) | copy-start | bytes 1179652
  129.8 0.7 copy-start.9
  133.0 10.6 %collective-permute-start.12 = (f32[3,2,64,128]{3,2,1,0:T(8,128)}, f32[3,2,64,128]{3,2,1,0:T(8,128)S(1)}, u32[]{:S(2)}, u32[]{:S(2)}) collective-permute-start(f32[3,2,64,128]{3,2,1,0:T(8,128)} %get-tuple-element.45), channel_id=1, source_target_pairs={{0,16},{32,48},{64,80},{96,112},{128,144},{160,176},{192,208},{224... | collective-permute-start | bytes 589832 | tf_op jit(solution)/shard_map/ppermute | solution.py:379
  138.3 10.6 %collective-permute-start.13 = (f32[3,2,64,128]{3,2,1,0:T(8,128)}, f32[3,2,64,128]{3,2,1,0:T(8,128)S(1)}, u32[]{:S(2)}, u32[]{:S(2)}) collective-permute-start(f32[3,2,64,128]{3,2,1,0:T(8,128)} %get-tuple-element.46), channel_id=1, source_target_pairs={{16,32},{48,64},{80,96},{112,128},{144,160},{176,192},{208,224},{3... | collective-permute-start | bytes 589832 | tf_op jit(solution)/shard_map/ppermute | solution.py:378
  143.6 5.3 %copy-start.10 = (f32[3,2,64,128]{3,2,1,0:T(8,128)}, f32[3,2,64,128]{3,2,1,0:T(8,128)S(1)}, u32[]{:S(2)}) copy-start(f32[3,2,64,128]{3,2,1,0:T(8,128)S(1)} %collective-permute-done.12.near) | copy-start | bytes 589828
  148.8 0.7 copy-start.11
where the time goes:
time: 155 us; the launch traced here: 152 us
  waiting for transfers between devices  59.2 us (38%)
  starting transfers between devices  46 us (30%)
  Pallas kernels  36.9 us (24%)
  local copies, waits for them, and re-layouts  6.92 us (4%)
  other arithmetic  2.49 us (2%)
    ppermute x7, waiting for transfers between devices, swap(): far = lax.ppermute(far, axis, route(1))  54 us
    ppermute x7, starting transfers between devices, swap(): far = lax.ppermute(far, axis, route(1))  34.6 us
    pallas_call x2, Pallas kernels, step(): call(step_kernel, (PART, PACK, PACK), (pltpu.VMEM((SLICES, 2, TILE, TILE)...  21.3 us
    ppermute x7, starting transfers between devices, swap(): near = lax.ppermute(near, axis, route(0))  11.3 us
    ppermute x7, waiting for transfers between devices, swap(): near = lax.ppermute(near, axis, route(0))  5.19 us
    unnamed x28, local copies, waits for them, and re-layouts  5.06 us
  transfers between devices with their start and end apart: 14, of which 9 were waited for; matrix products, arithmetic and copies ran while one was open for 2% of the time, Pallas kernels for 2%

commit v1 on v0

--- a/solution.py
+++ b/solution.py
@@ -195,7 +195,7 @@
     gradient(0)
 
 
-def call(body, outs, scratch=(), smem=1, count=0):
+def call(body, outs, scratch=(), smem=1, count=0, limit=8):
     return pl.pallas_call(
         body,
         out_shape=[jax.ShapeDtypeStruct(shape, jnp.float32) for shape in outs],
@@ -203,6 +203,7 @@
         + [pl.BlockSpec(memory_space=pltpu.VMEM)] * count,
         out_specs=[pl.BlockSpec(memory_space=pltpu.VMEM)] * len(outs),
         scratch_shapes=list(scratch),
+        compiler_params=pltpu.CompilerParams(vmem_limit_bytes=limit << 20),
         name=body.__name__,
     )
 
@@ -221,6 +222,7 @@
             pltpu.VMEM((2, TILE, TILE), jnp.float32),
         ),
         count=7,
+        limit=24,
     )(*args)
 
 

time: 155 us -> 140 us (0.903)
  Pallas kernels: 36.9 us -> 21.8 us
  local copies, waits for them, and re-layouts: 6.92 us -> 2.56 us
  waiting for transfers between devices: 59.2 us -> 63.5 us
  starting transfers between devices: 46 us -> 48.4 us
    ppermute x7, waiting for transfers between devices: 54 us -> 59.3 us  [swap(): far = lax.ppermute(far, axis, route(1))]
    pallas_call x2, Pallas kernels: 21.3 us -> 16.1 us  [step(): call(step_kernel, (PART, PACK, PACK), (pltpu.VMEM((SLICES, 2, TILE, TILE)...]
    ppermute x7, starting transfers between devices: 11.3 us -> 16.5 us  [swap(): near = lax.ppermute(near, axis, route(0))]
    unnamed x28 -> x14, local copies, waits for them, and re-layouts: 5.06 us -> 1.59 us
    ppermute x7, starting transfers between devices: 34.6 us -> 32 us  [swap(): far = lax.ppermute(far, axis, route(1))]
    pallas_call x1, Pallas kernels: 2.95 us -> 0.77 us  [update(): return call(update_kernel, (PART, PACK, PACK), count=4)(*args)]
    pallas_call x1, Pallas kernels: 2.7 us -> 0.74 us  [share(): return call(share_kernel, (PART, half, half), count=3)(*args)]
    pallas_call x1, Pallas kernels: 2.43 us -> 0.73 us  [close(): call(close_kernel, ((SLICES, 2, CORE, CORE), rim, rim), count=3)(*args)]
  transfers between devices with their start and end apart: 14 -> 14, of which waited for: 9 -> 9; matrix products, arithmetic and copies ran while one was open for 2% -> 1% of each run, Pallas kernels for 2% -> 1%
where the time goes in v1:
time: 140 us; the launch traced here: 138 us
  waiting for transfers between devices  63.5 us (45%)
  starting transfers between devices  48.4 us (35%)
  Pallas kernels  21.8 us (16%)
  local copies, waits for them, and re-layouts  2.56 us (2%)
    ppermute x7, waiting for transfers between devices, swap(): far = lax.ppermute(far, axis, route(1))  59.3 us
    ppermute x7, starting transfers between devices, swap(): far = lax.ppermute(far, axis, route(1))  32 us
    ppermute x7, starting transfers between devices, swap(): near = lax.ppermute(near, axis, route(0))  16.5 us
    pallas_call x2, Pallas kernels, step(): call(step_kernel, (PART, PACK, PACK), (pltpu.VMEM((SLICES, 2, TILE, TILE)...  16.1 us
    ppermute x7, waiting for transfers between devices, swap(): near = lax.ppermute(near, axis, route(0))  4.23 us
  transfers between devices with their start and end apart: 14, of which 9 were waited for; matrix products, arithmetic and copies ran while one was open for 1% of the time, Pallas kernels for 1%

profile of v1, /device:TPU:232, one launch (start us, length us, event | category | flops | bytes accessed | tf_op | source)
XLA Modules:
  0.0 137.7 jit_solution(6122185160215173400)
XLA Ops:
  0.0 0.0 copy-start.1
  0.0 0.0 copy-start.4
  0.0 1.1 slice_select_fusion
  1.1 0.0 copy-start.2
  1.1 4.9 %collective-permute-start.1 = (f32[3,2,64,128]{3,2,1,0:T(8,128)S(1)}, f32[3,2,64,128]{3,2,1,0:T(8,128)S(1)}, u32[]{:S(2)}, u32[]{:S(2)}) collective-permute-start(f32[3,2,64,128]{3,2,1,0:T(8,128)S(1)} %get-tuple-element.47), channel_id=1, source_target_pairs={{16,32},{48,64},{80,96},{112,128},{144,160},{176,192},{208,224},{3... | collective-permute-start | bytes 589832 | tf_op jit(solution)/shard_map/ppermute | solution.py:380
  6.1 0.1 collective-permute-start
  6.2 0.1 pad_add_fusion.par
  6.3 0.0 copy-start.3
  6.3 7.4 %collective-permute-done.1.far = f32[3,2,64,128]{3,2,1,0:T(8,128)S(1)} collective-permute-done((f32[3,2,64,128]{3,2,1,0:T(8,128)S(1)}, f32[3,2,64,128]{3,2,1,0:T(8,128)S(1)}, u32[]{:S(2)}, u32[]{:S(2)}) %collective-permute-start.1) | collective-permute-done | bytes 196640 | tf_op jit(solution)/shard_map/ppermute | solution.py:380
  13.6 2.2 %collective-permute-done.near = f32[3,2,64,128]{3,2,1,0:T(8,128)S(1)} collective-permute-done((f32[3,2,64,128]{3,2,1,0:T(8,128)S(1)}, f32[3,2,64,128]{3,2,1,0:T(8,128)S(1)}, u32[]{:S(2)}, u32[]{:S(2)}) %collective-permute-start) | collective-permute-done | bytes 196640 | tf_op jit(solution)/shard_map/ppermute | solution.py:381
  15.8 0.0 copy-done.1
  15.8 0.7 assemble_kernel.1
  16.5 0.1 collective-permute-start.2
  16.6 4.0 %collective-permute-start.3 = (f32[3,256,128]{2,1,0:T(8,128)S(1)}, f32[3,256,128]{2,1,0:T(8,128)S(1)}, u32[]{:S(2)}, u32[]{:S(2)}) collective-permute-start(f32[3,256,128]{2,1,0:T(8,128)S(1)} %get-tuple-element.28), channel_id=1, source_target_pairs={{1,2},{3,4},{5,6},{7,8},{9,10},{11,12},{13,14},{2,1},{4,3},{6,5},{... | collective-permute-start | bytes 1179656 | tf_op jit(solution)/shard_map/ppermute | solution.py:380
  20.6 0.0 copy-start.6
  20.6 0.0 copy-done.4
  20.6 0.0 copy-done.2
  20.6 0.0 copy-done.3
  20.6 0.6 copy-done.6
  21.3 0.0 copy-start.5
  21.3 0.9 copy-done.5
  22.2 1.4 %setup_kernel.1 = (f32[2,256,256]{2,1,0:T(8,128)S(1)}, f32[256,256]{1,0:T(8,128)S(1)}, f32[256,256]{1,0:T(8,128)S(1)}) custom-call(s32[2]{0:T(128)S(1)} %bitcast.11, f32[2,256,256]{2,1,0:T(8,128)S(1)} %copy-done.2, f32[256,256]{1,0:T(8,128)S(1)} %copy-done.3, f32[256,256]{1,0:T(8,128)S(1)} %bitcast.10, bf16[2,256,256]{2,1,0:T(8,128)(2,1)S(1)} %copy-done.5), custom_call_target="tpu_custom_call" | custom-call | tf_op jit(solution)/shard_map/setup_kernel/pallas_call | solution.py:255
  23.6 0.0 copy-start
  23.6 1.0 cosine_bitcast_fusion
  24.6 0.0 collective-permute-done.2.near
  24.7 7.2 %collective-permute-done.3.far = f32[3,256,128]{2,1,0:T(8,128)S(1)} collective-permute-done((f32[3,256,128]{2,1,0:T(8,128)S(1)}, f32[3,256,128]{2,1,0:T(8,128)S(1)}, u32[]{:S(2)}, u32[]{:S(2)}) %collective-permute-start.3) | collective-permute-done | bytes 393248 | tf_op jit(solution)/shard_map/ppermute | solution.py:380
  31.8 0.0 copy-done
  31.8 8.0 %step_kernel.2 = (f32[3,2,256,128]{3,2,1,0:T(8,128)S(1)}, f32[3,256,128]{2,1,0:T(8,128)S(1)}, f32[3,256,128]{2,1,0:T(8,128)S(1)}) custom-call(s32[4]{0:T(128)S(1)} %pad_add_fusion.par, f32[3,2,256,128]{3,2,1,0:T(8,128)S(1)} %get-tuple-element.26.mid, f32[3,256,128]{2,1,0:T(8,128)S(1)} %collective-permute-done.2.near, ...), custom_call_target="tpu_custom_call" | custom-call | tf_op jit(solution)/shard_map/step_kernel/pallas_call | solution.py:216
  39.9 0.1 collective-permute-start.4
  40.0 4.0 %collective-permute-start.5 = (f32[3,256,128]{2,1,0:T(8,128)S(1)}, f32[3,256,128]{2,1,0:T(8,128)S(1)}, u32[]{:S(2)}, u32[]{:S(2)}) collective-permute-start(f32[3,256,128]{2,1,0:T(8,128)S(1)} %get-tuple-element.34), channel_id=1, source_target_pairs={{1,2},{3,4},{5,6},{7,8},{9,10},{11,12},{13,14},{2,1},{4,3},{6,5},{... | collective-permute-start | bytes 1179656 | tf_op jit(solution)/shard_map/ppermute | solution.py:380
  44.0 0.0 collective-permute-done.4.near
  44.0 11.2 %collective-permute-done.5.far = f32[3,256,128]{2,1,0:T(8,128)S(1)} collective-permute-done((f32[3,256,128]{2,1,0:T(8,128)S(1)}, f32[3,256,128]{2,1,0:T(8,128)S(1)}, u32[]{:S(2)}, u32[]{:S(2)}) %collective-permute-start.5) | collective-permute-done | bytes 393248 | tf_op jit(solution)/shard_map/ppermute | solution.py:380
  55.2 0.7 share_kernel.1
  56.0 8.8 %collective-permute-start.6 = (f32[3,2,128,128]{3,2,1,0:T(8,128)S(1)}, f32[3,2,128,128]{3,2,1,0:T(8,128)S(1)}, u32[]{:S(2)}, u32[]{:S(2)}) collective-permute-start(f32[3,2,128,128]{3,2,1,0:T(8,128)S(1)} %get-tuple-element.36), channel_id=1, source_target_pairs={{0,16},{32,48},{64,80},{96,112},{128,144},{160,176},{192,208},{224... | collective-permute-start | bytes 1179656 | tf_op jit(solution)/shard_map/ppermute | solution.py:381
  64.8 3.7 %collective-permute-start.7 = (f32[3,2,128,128]{3,2,1,0:T(8,128)S(1)}, f32[3,2,128,128]{3,2,1,0:T(8,128)S(1)}, u32[]{:S(2)}, u32[]{:S(2)}) collective-permute-start(f32[3,2,128,128]{3,2,1,0:T(8,128)S(1)} %get-tuple-element.37), channel_id=1, source_target_pairs={{16,32},{48,64},{80,96},{112,128},{144,160},{176,192},{208,224},{3... | collective-permute-start | bytes 1179656 | tf_op jit(solution)/shard_map/ppermute | solution.py:380
  68.5 2.1 %collective-permute-done.6.near = f32[3,2,128,128]{3,2,1,0:T(8,128)S(1)} collective-permute-done((f32[3,2,128,128]{3,2,1,0:T(8,128)S(1)}, f32[3,2,128,128]{3,2,1,0:T(8,128)S(1)}, u32[]{:S(2)}, u32[]{:S(2)}) %collective-permute-start.6) | collective-permute-done | bytes 393248 | tf_op jit(solution)/shard_map/ppermute | solution.py:381
  70.5 6.7 %collective-permute-done.7.far = f32[3,2,128,128]{3,2,1,0:T(8,128)S(1)} collective-permute-done((f32[3,2,128,128]{3,2,1,0:T(8,128)S(1)}, f32[3,2,128,128]{3,2,1,0:T(8,128)S(1)}, u32[]{:S(2)}, u32[]{:S(2)}) %collective-permute-start.7) | collective-permute-done | bytes 393248 | tf_op jit(solution)/shard_map/ppermute | solution.py:380
  77.2 0.8 update_kernel.1
  78.0 0.1 collective-permute-start.8
  78.1 3.8 %collective-permute-start.9 = (f32[3,256,128]{2,1,0:T(8,128)S(1)}, f32[3,256,128]{2,1,0:T(8,128)S(1)}, u32[]{:S(2)}, u32[]{:S(2)}) collective-permute-start(f32[3,256,128]{2,1,0:T(8,128)S(1)} %get-tuple-element.40), channel_id=1, source_target_pairs={{1,2},{3,4},{5,6},{7,8},{9,10},{11,12},{13,14},{2,1},{4,3},{6,5},{... | collective-permute-start | bytes 1179656 | tf_op jit(solution)/shard_map/ppermute | solution.py:380
  81.9 0.0 collective-permute-done.8.near
  81.9 11.4 %collective-permute-done.9.far = f32[3,256,128]{2,1,0:T(8,128)S(1)} collective-permute-done((f32[3,256,128]{2,1,0:T(8,128)S(1)}, f32[3,256,128]{2,1,0:T(8,128)S(1)}, u32[]{:S(2)}, u32[]{:S(2)}) %collective-permute-start.9) | collective-permute-done | bytes 393248 | tf_op jit(solution)/shard_map/ppermute | solution.py:380
  93.3 8.0 %step_kernel.3 = (f32[3,2,256,128]{3,2,1,0:T(8,128)S(1)}, f32[3,256,128]{2,1,0:T(8,128)S(1)}, f32[3,256,128]{2,1,0:T(8,128)S(1)}) custom-call(s32[4]{0:T(128)S(1)} %pad_add_fusion.par, f32[3,2,256,128]{3,2,1,0:T(8,128)S(1)} %get-tuple-element.38.mid, f32[3,256,128]{2,1,0:T(8,128)S(1)} %collective-permute-done.8.near, ...), custom_call_target="tpu_custom_call" | custom-call | tf_op jit(solution)/shard_map/step_kernel/pallas_call | solution.py:216
  101.4 0.1 collective-permute-start.10
  101.5 3.8 %collective-permute-start.11 = (f32[3,256,128]{2,1,0:T(8,128)S(1)}, f32[3,256,128]{2,1,0:T(8,128)S(1)}, u32[]{:S(2)}, u32[]{:S(2)}) collective-permute-start(f32[3,256,128]{2,1,0:T(8,128)S(1)} %get-tuple-element.43), channel_id=1, source_target_pairs={{1,2},{3,4},{5,6},{7,8},{9,10},{11,12},{13,14},{2,1},{4,3},{6,5},{... | collective-permute-start | bytes 1179656 | tf_op jit(solution)/shard_map/ppermute | solution.py:380
  105.2 0.0 collective-permute-done.10.near
  105.2 11.4 %collective-permute-done.11.far = f32[3,256,128]{2,1,0:T(8,128)S(1)} collective-permute-done((f32[3,256,128]{2,1,0:T(8,128)S(1)}, f32[3,256,128]{2,1,0:T(8,128)S(1)}, u32[]{:S(2)}, u32[]{:S(2)}) %collective-permute-start.11) | collective-permute-done | bytes 393248 | tf_op jit(solution)/shard_map/ppermute | solution.py:380
  116.7 0.7 close_kernel.1
  117.4 7.2 %collective-permute-start.12 = (f32[3,2,64,128]{3,2,1,0:T(8,128)S(1)}, f32[3,2,64,128]{3,2,1,0:T(8,128)S(1)}, u32[]{:S(2)}, u32[]{:S(2)}) collective-permute-start(f32[3,2,64,128]{3,2,1,0:T(8,128)S(1)} %get-tuple-element.45), channel_id=1, source_target_pairs={{0,16},{32,48},{64,80},{96,112},{128,144},{160,176},{192,208},{224... | collective-permute-start | bytes 589832 | tf_op jit(solution)/shard_map/ppermute | solution.py:381
  124.6 7.8 %collective-permute-start.13 = (f32[3,2,64,128]{3,2,1,0:T(8,128)S(1)}, f32[3,2,64,128]{3,2,1,0:T(8,128)S(1)}, u32[]{:S(2)}, u32[]{:S(2)}) collective-permute-start(f32[3,2,64,128]{3,2,1,0:T(8,128)S(1)} %get-tuple-element.46), channel_id=1, source_target_pairs={{16,32},{48,64},{80,96},{112,128},{144,160},{176,192},{208,224},{3... | collective-permute-start | bytes 589832 | tf_op jit(solution)/shard_map/ppermute | solution.py:380
  132.4 0.0 collective-permute-done.12.near
  132.5 3.9 %collective-permute-done.13.far = f32[3,2,64,128]{3,2,1,0:T(8,128)S(1)} collective-permute-done((f32[3,2,64,128]{3,2,1,0:T(8,128)S(1)}, f32[3,2,64,128]{3,2,1,0:T(8,128)S(1)}, u32[]{:S(2)}, u32[]{:S(2)}) %collective-permute-start.13) | collective-permute-done | bytes 196640 | tf_op jit(solution)/shard_map/ppermute | solution.py:380
  136.4 1.3 finish_kernel.1
  (1 shorter events, 0.0 us)
Async XLA Ops:
  0.0 15.8 %copy-start.1 = (f32[3,2,128,128]{3,2,1,0:T(8,128)S(1)}, f32[3,2,128,128]{3,2,1,0:T(8,128)}, u32[]{:S(2)}) copy-start(f32[3,2,128,128]{3,2,1,0:T(8,128)} %core.1) | copy-start | bytes 1179652
  0.0 20.6 %copy-start.4 = (f32[1,1,1,256,256]{4,3,2,1,0:T(8,128)S(1)}, f32[1,1,1,256,256]{4,3,2,1,0:T(8,128)}, u32[]{:S(2)}) copy-start(f32[1,1,1,256,256]{4,3,2,1,0:T(8,128)} %param.10) | copy-start | bytes 786436
  1.1 19.5 %copy-start.2 = (f32[2,256,256]{2,1,0:T(8,128)S(1)}, f32[2,256,256]{2,1,0:T(8,128)}, u32[]{:S(2)}) copy-start(f32[2,256,256]{2,1,0:T(8,128)} %probe.1) | copy-start | bytes 1572868
  1.1 12.5 %collective-permute-start.1 = (f32[3,2,64,128]{3,2,1,0:T(8,128)S(1)}, f32[3,2,64,128]{3,2,1,0:T(8,128)S(1)}, u32[]{:S(2)}, u32[]{:S(2)}) collective-permute-start(f32[3,2,64,128]{3,2,1,0:T(8,128)S(1)} %get-tuple-element.47), channel_id=1, source_target_pairs={{16,32},{48,64},{80,96},{112,128},{144,160},{176,192},{208,224},{3... | collective-permute-start | bytes 589832 | tf_op jit(solution)/shard_map/ppermute | solution.py:380
  6.1 9.7 %collective-permute-start = (f32[3,2,64,128]{3,2,1,0:T(8,128)S(1)}, f32[3,2,64,128]{3,2,1,0:T(8,128)S(1)}, u32[]{:S(2)}, u32[]{:S(2)}) collective-permute-start(f32[3,2,64,128]{3,2,1,0:T(8,128)S(1)} %get-tuple-element.48), channel_id=1, source_target_pairs={{0,16},{32,48},{64,80},{96,112},{128,144},{160,176},{192,208},{224... | collective-permute-start | bytes 589832 | tf_op jit(solution)/shard_map/ppermute | solution.py:381
  6.3 14.4 %copy-start.3 = (f32[256,256]{1,0:T(8,128)S(1)}, f32[256,256]{1,0:T(8,128)}, u32[]{:S(2)}) copy-start(f32[256,256]{1,0:T(8,128)} %phase.1) | copy-start | bytes 786436
  16.5 8.1 %collective-permute-start.2 = (f32[3,256,128]{2,1,0:T(8,128)S(1)}, f32[3,256,128]{2,1,0:T(8,128)S(1)}, u32[]{:S(2)}, u32[]{:S(2)}) collective-permute-start(f32[3,256,128]{2,1,0:T(8,128)S(1)} %get-tuple-element.27), channel_id=1, source_target_pairs={{0,1},{2,3},{4,5},{6,7},{8,9},{10,11},{12,13},{14,15},{1,0},{3,2},... | collective-permute-start | bytes 1179656 | tf_op jit(solution)/shard_map/ppermute | solution.py:381
  16.6 15.2 %collective-permute-start.3 = (f32[3,256,128]{2,1,0:T(8,128)S(1)}, f32[3,256,128]{2,1,0:T(8,128)S(1)}, u32[]{:S(2)}, u32[]{:S(2)}) collective-permute-start(f32[3,256,128]{2,1,0:T(8,128)S(1)} %get-tuple-element.28), channel_id=1, source_target_pairs={{1,2},{3,4},{5,6},{7,8},{9,10},{11,12},{13,14},{2,1},{4,3},{6,5},{... | collective-permute-start | bytes 1179656 | tf_op jit(solution)/shard_map/ppermute | solution.py:380
  20.6 0.7 copy-start.6
  21.3 0.9 copy-start.5
  23.6 8.2 %copy-start = (bf16[4,2,256,256]{3,2,1,0:T(8,128)(2,1)S(1)}, bf16[4,2,256,256]{3,2,1,0:T(8,128)(2,1)}, u32[]{:S(2)}) copy-start(bf16[4,2,256,256]{3,2,1,0:T(8,128)(2,1)} %constant.34.clone.tables) | copy-start | bytes 3145732
  39.9 4.1 %collective-permute-start.4 = (f32[3,256,128]{2,1,0:T(8,128)S(1)}, f32[3,256,128]{2,1,0:T(8,128)S(1)}, u32[]{:S(2)}, u32[]{:S(2)}) collective-permute-start(f32[3,256,128]{2,1,0:T(8,128)S(1)} %get-tuple-element.33), channel_id=1, source_target_pairs={{0,1},{2,3},{4,5},{6,7},{8,9},{10,11},{12,13},{14,15},{1,0},{3,2},... | collective-permute-start | bytes 1179656 | tf_op jit(solution)/shard_map/ppermute | solution.py:381
  40.0 15.2 %collective-permute-start.5 = (f32[3,256,128]{2,1,0:T(8,128)S(1)}, f32[3,256,128]{2,1,0:T(8,128)S(1)}, u32[]{:S(2)}, u32[]{:S(2)}) collective-permute-start(f32[3,256,128]{2,1,0:T(8,128)S(1)} %get-tuple-element.34), channel_id=1, source_target_pairs={{1,2},{3,4},{5,6},{7,8},{9,10},{11,12},{13,14},{2,1},{4,3},{6,5},{... | collective-permute-start | bytes 1179656 | tf_op jit(solution)/shard_map/ppermute | solution.py:380
  56.0 14.6 %collective-permute-start.6 = (f32[3,2,128,128]{3,2,1,0:T(8,128)S(1)}, f32[3,2,128,128]{3,2,1,0:T(8,128)S(1)}, u32[]{:S(2)}, u32[]{:S(2)}) collective-permute-start(f32[3,2,128,128]{3,2,1,0:T(8,128)S(1)} %get-tuple-element.36), channel_id=1, source_target_pairs={{0,16},{32,48},{64,80},{96,112},{128,144},{160,176},{192,208},{224... | collective-permute-start | bytes 1179656 | tf_op jit(solution)/shard_map/ppermute | solution.py:381
  64.8 12.5 %collective-permute-start.7 = (f32[3,2,128,128]{3,2,1,0:T(8,128)S(1)}, f32[3,2,128,128]{3,2,1,0:T(8,128)S(1)}, u32[]{:S(2)}, u32[]{:S(2)}) collective-permute-start(f32[3,2,128,128]{3,2,1,0:T(8,128)S(1)} %get-tuple-element.37), channel_id=1, source_target_pairs={{16,32},{48,64},{80,96},{112,128},{144,160},{176,192},{208,224},{3... | collective-permute-start | bytes 1179656 | tf_op jit(solution)/shard_map/ppermute | solution.py:380
  78.0 3.9 %collective-permute-start.8 = (f32[3,256,128]{2,1,0:T(8,128)S(1)}, f32[3,256,128]{2,1,0:T(8,128)S(1)}, u32[]{:S(2)}, u32[]{:S(2)}) collective-permute-start(f32[3,256,128]{2,1,0:T(8,128)S(1)} %get-tuple-element.39), channel_id=1, source_target_pairs={{0,1},{2,3},{4,5},{6,7},{8,9},{10,11},{12,13},{14,15},{1,0},{3,2},... | collective-permute-start | bytes 1179656 | tf_op jit(solution)/shard_map/ppermute | solution.py:381
  78.1 15.2 %collective-permute-start.9 = (f32[3,256,128]{2,1,0:T(8,128)S(1)}, f32[3,256,128]{2,1,0:T(8,128)S(1)}, u32[]{:S(2)}, u32[]{:S(2)}) collective-permute-start(f32[3,256,128]{2,1,0:T(8,128)S(1)} %get-tuple-element.40), channel_id=1, source_target_pairs={{1,2},{3,4},{5,6},{7,8},{9,10},{11,12},{13,14},{2,1},{4,3},{6,5},{... | collective-permute-start | bytes 1179656 | tf_op jit(solution)/shard_map/ppermute | solution.py:380
  101.4 3.9 %collective-permute-start.10 = (f32[3,256,128]{2,1,0:T(8,128)S(1)}, f32[3,256,128]{2,1,0:T(8,128)S(1)}, u32[]{:S(2)}, u32[]{:S(2)}) collective-permute-start(f32[3,256,128]{2,1,0:T(8,128)S(1)} %get-tuple-element.42), channel_id=1, source_target_pairs={{0,1},{2,3},{4,5},{6,7},{8,9},{10,11},{12,13},{14,15},{1,0},{3,2},... | collective-permute-start | bytes 1179656 | tf_op jit(solution)/shard_map/ppermute | solution.py:381
  101.5 15.2 %collective-permute-start.11 = (f32[3,256,128]{2,1,0:T(8,128)S(1)}, f32[3,256,128]{2,1,0:T(8,128)S(1)}, u32[]{:S(2)}, u32[]{:S(2)}) collective-permute-start(f32[3,256,128]{2,1,0:T(8,128)S(1)} %get-tuple-element.43), channel_id=1, source_target_pairs={{1,2},{3,4},{5,6},{7,8},{9,10},{11,12},{13,14},{2,1},{4,3},{6,5},{... | collective-permute-start | bytes 1179656 | tf_op jit(solution)/shard_map/ppermute | solution.py:380
  117.4 15.1 %collective-permute-start.12 = (f32[3,2,64,128]{3,2,1,0:T(8,128)S(1)}, f32[3,2,64,128]{3,2,1,0:T(8,128)S(1)}, u32[]{:S(2)}, u32[]{:S(2)}) collective-permute-start(f32[3,2,64,128]{3,2,1,0:T(8,128)S(1)} %get-tuple-element.45), channel_id=1, source_target_pairs={{0,16},{32,48},{64,80},{96,112},{128,144},{160,176},{192,208},{224... | collective-permute-start | bytes 589832 | tf_op jit(solution)/shard_map/ppermute | solution.py:381
  124.6 11.8 %collective-permute-start.13 = (f32[3,2,64,128]{3,2,1,0:T(8,128)S(1)}, f32[3,2,64,128]{3,2,1,0:T(8,128)S(1)}, u32[]{:S(2)}, u32[]{:S(2)}) collective-permute-start(f32[3,2,64,128]{3,2,1,0:T(8,128)S(1)} %get-tuple-element.46), channel_id=1, source_target_pairs={{16,32},{48,64},{80,96},{112,128},{144,160},{176,192},{208,224},{3... | collective-permute-start | bytes 589832 | tf_op jit(solution)/shard_map/ppermute | solution.py:380

commit v2 on v1

--- a/solution.py
+++ b/solution.py
@@ -131,17 +131,45 @@
     return pltpu.roll(value, MARGIN, 1)
 
 
+def near_lanes(par, rows):
+    return low_lanes((rows, CORE)) != (par[1] == 0)
+
+
+def pack(nearby, real, imag):
+    other = turned(imag)
+    return jnp.where(nearby, real, other), jnp.where(nearby, other, real)
+
+
+def unpack(nearby, first, second):
+    return jnp.where(nearby, first, second), turned(jnp.where(nearby, second, first))
+
+
 def step_kernel(
-    par, mid, near, far, lit, wave, patterns, tables, part, send_near, send_far, tile, field, up
+    par,
+    first,
+    second,
+    near,
+    far,
+    lit,
+    wave,
+    patterns,
+    tables,
+    part_first,
+    part_second,
+    send_near,
+    send_far,
+    tile,
+    field,
+    up,
 ):
-    even = par[1] == 0
-    low = low_lanes((TILE, CORE)) == even
+    nearby = near_lanes(par, TILE)
     for layer in range(SLICES):
-        e, o = near[layer], far[layer]
-        tile[layer, 0, :, :CORE] = mid[layer, 0]
-        tile[layer, 1, :, :CORE] = mid[layer, 1]
-        tile[layer, 0, :, CORE:] = jnp.where(low, e, o)
-        tile[layer, 1, :, CORE:] = turned(jnp.where(low, o, e))
+        real, imag = unpack(nearby, first[layer], second[layer])
+        tile[layer, 0, :, :CORE] = real
+        tile[layer, 1, :, :CORE] = imag
+        real, imag = unpack(nearby, far[layer], near[layer])
+        tile[layer, 0, :, CORE:] = real
+        tile[layer, 1, :, CORE:] = imag
     field[0, 0] = lit[0]
     field[0, 1] = lit[1]
 
@@ -173,11 +201,8 @@
         u_real, u_imag = up[0], up[1]
         real = f_real * u_real + f_imag * u_imag
         imag = f_real * u_imag - f_imag * u_real
-        part[layer, 0] = real[:, :CORE]
-        part[layer, 1] = imag[:, :CORE]
-        straight, other = real[:, CORE:], turned(imag[:, CORE:])
-        send_near[layer] = jnp.where(low, straight, other)
-        send_far[layer] = jnp.where(low, other, straight)
+        part_first[layer], part_second[layer] = pack(nearby, real[:, :CORE], imag[:, :CORE])
+        send_far[layer], send_near[layer] = pack(nearby, real[:, CORE:], imag[:, CORE:])
 
     def behind(turn, carry):
         layer = SLICES - 1 - turn
@@ -208,20 +233,21 @@
     )
 
 
-PART = (SLICES, 2, TILE, CORE)
 PACK = (SLICES, TILE, CORE)
+HALF = (SLICES, CORE, CORE)
+RIMS = (2, SLICES, MARGIN, CORE)
 
 
 def step(*args):
     return call(
         step_kernel,
-        (PART, PACK, PACK),
+        (PACK, PACK, PACK, PACK),
         (
             pltpu.VMEM((SLICES, 2, TILE, TILE), jnp.float32),
             pltpu.VMEM((SLICES, 2, TILE, TILE), jnp.float32),
             pltpu.VMEM((2, TILE, TILE), jnp.float32),
         ),
-        count=7,
+        count=8,
         limit=24,
     )(*args)
 
@@ -255,156 +281,147 @@
     return call(setup_kernel, shapes, count=4)(positions, probe, phase, patterns, order)
 
 
-def pack_columns(even, mid, send_near, send_far):
-    low = low_lanes((TILE, CORE)) == even
+def open_kernel(par, core, first, second, near, far):
+    even = par[0] == 0
+    nearby = near_lanes(par, CORE)
     for layer in range(SLICES):
-        straight, other = mid[layer, 0], turned(mid[layer, 1])
-        send_near[layer] = jnp.where(low, other, straight)
-        send_far[layer] = jnp.where(low, straight, other)
-
-
-def assemble_kernel(par, core, near, far, mid, send_near, send_far):
+        packs = pack(nearby, core[layer, 0], core[layer, 1])
+        for k, (value, whole) in enumerate(zip(packs, (first, second))):
+            whole[layer] = value
+            near[k, layer] = jnp.where(even, value[MARGIN:], value[:MARGIN])
+            far[k, layer] = jnp.where(even, value[:MARGIN], value[MARGIN:])
+
+
+def begin(par, core):
+    return call(open_kernel, (HALF, HALF, RIMS, RIMS), count=1)(par, core)
+
+
+def assemble_kernel(par, core_1, core_2, near, far, first, second):
+    even = par[0] == 0
+    for k, (core, mid) in enumerate(((core_1, first), (core_2, second))):
+        for layer in range(SLICES):
+            mid[layer, :CORE] = core[layer]
+            mid[layer, CORE : CORE + MARGIN] = jnp.where(even, near[k, layer], far[k, layer])
+            mid[layer, CORE + MARGIN :] = jnp.where(even, far[k, layer], near[k, layer])
+
+
+def assemble(*args):
+    return call(assemble_kernel, (PACK, PACK), count=4)(*args)
+
+
+def share_kernel(par, part, came, total, send_near, send_far):
     even = par[0] == 0
     for layer in range(SLICES):
-        for part in range(2):
-            e, o = near[layer, part], far[layer, part]
-            mid[layer, part, :CORE] = core[layer, part]
-            mid[layer, part, CORE : CORE + MARGIN] = jnp.where(even, e, o)
-            mid[layer, part, CORE + MARGIN :] = jnp.where(even, o, e)
-    pack_columns(par[1] == 0, mid, send_near, send_far)
-
-
-def assemble(*args):
-    return call(assemble_kernel, (PART, PACK, PACK), count=3)(*args)
-
-
-def add_columns(even, part, near, far):
-    low = low_lanes((TILE, CORE)) == even
-    out = []
-    for layer in range(SLICES):
-        e, o = near[layer], far[layer]
-        out.append(
-            (
-                part[layer, 0] + jnp.where(low, o, e),
-                part[layer, 1] + turned(jnp.where(low, e, o)),
-            )
-        )
-    return out
-
-
-def share_kernel(par, part, near, far, total, send_near, send_far):
-    even = par[0] == 0
-    sums = add_columns(par[1] == 0, part, near, far)
-    for layer in range(SLICES):
-        for c in range(2):
-            value = sums[layer][c]
-            total[layer, c] = value
-            a, b, d, e = (value[k * MARGIN : (k + 1) * MARGIN] for k in range(4))
-            send_near[layer, c, :MARGIN] = jnp.where(even, b, e)
-            send_near[layer, c, MARGIN:] = jnp.where(even, d, a)
-            send_far[layer, c, :MARGIN] = jnp.where(even, e, b)
-            send_far[layer, c, MARGIN:] = jnp.where(even, a, d)
+        value = part[layer] + came[layer]
+        total[layer] = value
+        a, b, d, e = (value[k * MARGIN : (k + 1) * MARGIN] for k in range(4))
+        send_near[layer, :MARGIN] = jnp.where(even, b, e)
+        send_near[layer, MARGIN:] = jnp.where(even, d, a)
+        send_far[layer, :MARGIN] = jnp.where(even, e, b)
+        send_far[layer, MARGIN:] = jnp.where(even, a, d)
 
 
 def share(*args):
-    half = (SLICES, 2, CORE, CORE)
-    return call(share_kernel, (PART, half, half), count=3)(*args)
-
-
-def update_kernel(par, mid, total, near, far, new, send_near, send_far):
+    return call(share_kernel, (PACK, HALF, HALF), count=2)(*args)
+
+
+def update_kernel(par, mid, total, near, far, new):
     even = par[0] == 0
     above = jnp.where(par[2] == 0, 0.0, STEP_SIZE)
     below = jnp.where(par[3] == 0, 0.0, STEP_SIZE)
     for layer in range(SLICES):
-        for c in range(2):
-            e, o = near[layer, c], far[layer, c]
-            down = jnp.where(even, e, o)
-            up = jnp.where(even, o, e)
-            for k, (added, scale) in enumerate(
-                (
-                    (up[MARGIN:], STEP_SIZE),
-                    (down[:MARGIN], STEP_SIZE),
-                    (down[MARGIN:], below),
-                    (up[:MARGIN], above),
-                )
-            ):
-                rows = pl.ds(k * MARGIN, MARGIN)
-                new[layer, c, rows] = mid[layer, c, rows] - scale * (total[layer, c, rows] + added)
-    pack_columns(par[1] == 0, new, send_near, send_far)
+        e, o = near[layer], far[layer]
+        down = jnp.where(even, e, o)
+        up = jnp.where(even, o, e)
+        for k, (added, scale) in enumerate(
+            (
+                (up[MARGIN:], STEP_SIZE),
+                (down[:MARGIN], STEP_SIZE),
+                (down[MARGIN:], below),
+                (up[:MARGIN], above),
+            )
+        ):
+            rows = pl.ds(k * MARGIN, MARGIN)
+            new[layer, rows] = mid[layer, rows] - scale * (total[layer, rows] + added)
 
 
 def update(*args):
-    return call(update_kernel, (PART, PACK, PACK), count=4)(*args)
-
-
-def close_kernel(par, part, near, far, total, send_near, send_far):
-    even = par[0] == 0
-    sums = add_columns(par[1] == 0, part, near, far)
+    return call(update_kernel, (PACK,), count=4)(*args)[0]
+
+
+def close_kernel(par, part_1, part_2, came_1, came_2, total, send_near, send_far):
+    even = par[0] == 0
+    for k, (part, came) in enumerate(((part_1, came_1), (part_2, came_2))):
+        for layer in range(SLICES):
+            value = part[layer] + came[layer]
+            total[k, layer] = value[:CORE]
+            below, above = value[CORE : CORE + MARGIN], value[CORE + MARGIN :]
+            send_near[k, layer] = jnp.where(even, below, above)
+            send_far[k, layer] = jnp.where(even, above, below)
+
+
+def close(*args):
+    return call(close_kernel, ((2, *HALF), RIMS, RIMS), count=4)(*args)
+
+
+def finish_kernel(par, mid_1, mid_2, total, near, far, out):
+    even = par[0] == 0
+    nearby = near_lanes(par, MARGIN)
     for layer in range(SLICES):
-        for c in range(2):
-            value = sums[layer][c]
-            total[layer, c] = value[:CORE]
-            below, above = value[CORE : CORE + MARGIN], value[CORE + MARGIN :]
-            send_near[layer, c] = jnp.where(even, below, above)
-            send_far[layer, c] = jnp.where(even, above, below)
-
-
-def close(*args):
-    rim = (SLICES, 2, MARGIN, CORE)
-    return call(close_kernel, ((SLICES, 2, CORE, CORE), rim, rim), count=3)(*args)
-
-
-def finish_kernel(par, mid, total, near, far, out):
-    even = par[0] == 0
-    for layer in range(SLICES):
-        for c in range(2):
-            e, o = near[layer, c], far[layer, c]
-            for k, added in enumerate((jnp.where(even, o, e), jnp.where(even, e, o))):
-                rows = pl.ds(k * MARGIN, MARGIN)
-                out[layer, c, rows] = mid[layer, c, rows] - STEP_SIZE * (
-                    total[layer, c, rows] + added
-                )
+        for half in range(2):
+            rows = pl.ds(half * MARGIN, MARGIN)
+            packs = []
+            for k, mid in enumerate((mid_1, mid_2)):
+                e, o = near[k, layer], far[k, layer]
+                added = jnp.where(even, o, e) if half == 0 else jnp.where(even, e, o)
+                packs.append(mid[layer, rows] - STEP_SIZE * (total[k, layer, rows] + added))
+            out[layer, 0, rows], out[layer, 1, rows] = unpack(nearby, *packs)
 
 
 def finish(*args):
-    return call(finish_kernel, ((SLICES, 2, CORE, CORE),), count=4)(*args)[0]
-
-
-def swap(axis, near, far):
+    return call(finish_kernel, ((SLICES, 2, CORE, CORE),), count=5)(*args)[0]
+
+
+def swap(axis, first, block):
     count = lax.axis_size(axis)
-
-    def route(first):
-        pairs = [(i, i + 1) for i in range(first, count - 1, 2)]
-        return pairs + [(j, i) for i, j in pairs]
-
-    far = lax.ppermute(far, axis, route(1))
-    near = lax.ppermute(near, axis, route(0))
-    return near, far
+    pairs = [(i, i + 1) for i in range(first, count - 1, 2)]
+    return lax.ppermute(block, axis, pairs + [(j, i) for i, j in pairs])
+
+
+def swap_rows(near, far):
+    far = swap("ty", 1, far)
+    return swap("ty", 0, near), far
 
 
 def shards(object_field, probe, propagator_phase, patterns, scan_positions):
     row, col = lax.axis_index("ty"), lax.axis_index("tx")
     par = jnp.stack([row % 2, col % 2, row, lax.axis_size("ty") - 1 - row]).astype(jnp.int32)
-    even = row % 2 == 0
-    top, bottom = object_field[:, :, :MARGIN], object_field[:, :, MARGIN:]
-    near, far = swap("ty", jnp.where(even, bottom, top), jnp.where(even, top, bottom))
+    first, second, near, far = begin(par, object_field)
+    near, far = swap_rows(near, far)
     lit, phase, ordered = setup(
         scan_positions[0, 0, 0], probe, propagator_phase, patterns[0, 0, 0], order_table()
     )
     wave = jnp.stack([jnp.cos(phase), jnp.sin(phase)])
     tables = jnp.asarray(half_tables())
-    mid, near, far = assemble(par, object_field, near, far)
+    first, second = assemble(par, first, second, near, far)
     for turn in range(STEPS):
-        near, far = swap("tx", near, far)
-        part, near, far = step(par, mid, near, far, lit, wave, ordered, tables)
-        near, far = swap("tx", near, far)
+        far = swap("tx", 1, second)
+        near = swap("tx", 0, first)
+        part_1, part_2, near, far = step(
+            par, first, second, near, far, lit, wave, ordered, tables
+        )
+        far = swap("tx", 1, far)
+        near = swap("tx", 0, near)
         if turn < STEPS - 1:
-            total, near, far = share(par, part, near, far)
-            near, far = swap("ty", near, far)
-            mid, near, far = update(par, mid, total, near, far)
-    total, near, far = close(par, part, near, far)
-    near, far = swap("ty", near, far)
-    return finish(par, mid, total, near, far)
+            total_1, near_1, far_1 = share(par, part_1, near)
+            near_1, far_1 = swap_rows(near_1, far_1)
+            total_2, near_2, far_2 = share(par, part_2, far)
+            near_2, far_2 = swap_rows(near_2, far_2)
+            first = update(par, first, total_1, near_1, far_1)
+            second = update(par, second, total_2, near_2, far_2)
+    total, near, far = close(par, part_1, part_2, near, far)
+    near, far = swap_rows(near, far)
+    return finish(par, first, second, total, near, far)
 
 
 def solution(mesh):

time: 140 us -> 144 us (1.029); the launches traced: 138 us -> 144 us
  starting transfers between devices: 48.4 us -> 66.3 us
  waiting for transfers between devices: 63.5 us -> 49.8 us
  Pallas kernels: 21.8 us -> 23.5 us
    ppermute x14 -> x16, starting transfers between devices: 48.4 us -> 66.3 us  [swap(): return lax.ppermute(block, axis, pairs + [(j, i) for i, j in pairs])]
    ppermute x14 -> x16, waiting for transfers between devices: 63.5 us -> 49.8 us  [swap(): return lax.ppermute(block, axis, pairs + [(j, i) for i, j in pairs])]
    pallas_call x7 -> x10, Pallas kernels: 20.4 us -> 22.1 us  [the longest x2 16.4 us: step(): call(step_kernel, (PACK, PACK, PACK, PACK), (pltpu.VMEM((SLICES, 2, TILE,...]
  transfers between devices with their start and end apart: 14 -> 16, of which waited for: 9 -> 9; matrix products, arithmetic and copies ran while one was open for 1% -> 1% of each run, Pallas kernels for 1% -> 3%
where the time goes in v2:
time: 144 us
  starting transfers between devices  66.3 us (46%)
  waiting for transfers between devices  49.8 us (35%)
  Pallas kernels  23.5 us (16%)
  local copies, waits for them, and re-layouts  3.55 us (2%)
    ppermute x16, starting transfers between devices, swap(): return lax.ppermute(block, axis, pairs + [(j, i) for i, j in pairs])  66.3 us
    ppermute x16, waiting for transfers between devices, swap(): return lax.ppermute(block, axis, pairs + [(j, i) for i, j in pairs])  49.8 us
    pallas_call x2, Pallas kernels, step(): call(step_kernel, (PACK, PACK, PACK, PACK), (pltpu.VMEM((SLICES, 2, TILE,...  16.4 us
  transfers between devices with their start and end apart: 16, of which 9 were waited for; matrix products, arithmetic and copies ran while one was open for 1% of the time, Pallas kernels for 3%

profile of v2, /device:TPU:232, one launch (start us, length us, event | category | flops | bytes accessed | tf_op | source)
XLA Modules:
  0.0 143.6 jit_solution(4070326029324225395)
XLA Ops:
  0.0 0.1 pad_add_fusion.par
  0.1 0.0 copy-start.2
  0.1 1.0 copy-done.2
  1.1 0.0 copy-start.1
  1.1 0.7 open_kernel.1
  1.7 1.1 collective-permute-start
  2.8 4.8 %collective-permute-start.1 = (f32[2,3,64,128]{3,2,1,0:T(8,128)S(1)}, f32[2,3,64,128]{3,2,1,0:T(8,128)S(1)}, u32[]{:S(2)}, u32[]{:S(2)}) collective-permute-start(f32[2,3,64,128]{3,2,1,0:T(8,128)S(1)} %get-tuple-element.34), channel_id=1, source_target_pairs={{16,32},{48,64},{80,96},{112,128},{144,160},{176,192},{208,224},{3... | collective-permute-start | bytes 589832 | tf_op jit(solution)/shard_map/ppermute | solution.py:388
  7.7 0.8 collective-permute-done.near
  8.5 6.2 %collective-permute-done.1.far = f32[2,3,64,128]{3,2,1,0:T(8,128)S(1)} collective-permute-done((f32[2,3,64,128]{3,2,1,0:T(8,128)S(1)}, f32[2,3,64,128]{3,2,1,0:T(8,128)S(1)}, u32[]{:S(2)}, u32[]{:S(2)}) %collective-permute-start.1) | collective-permute-done | bytes 196640 | tf_op jit(solution)/shard_map/ppermute | solution.py:388
  14.7 0.0 copy-start.3
  14.7 0.0 copy-start.4
  14.7 0.6 assemble_kernel.1
  15.3 0.1 collective-permute-start.2
  15.4 4.1 %collective-permute-start.3 = (f32[3,256,128]{2,1,0:T(8,128)S(1)}, f32[3,256,128]{2,1,0:T(8,128)S(1)}, u32[]{:S(2)}, u32[]{:S(2)}) collective-permute-start(f32[3,256,128]{2,1,0:T(8,128)S(1)} %get-tuple-element.36.second.mid), channel_id=1, source_target_pairs={{1,2},{3,4},{5,6},{7,8},{9,10},{11,12},{13,14},{2,1},{4,3},{6,5},{... | collective-permute-start | bytes 1179656 | tf_op jit(solution)/shard_map/ppermute | solution.py:388
  19.5 0.0 copy-start.6
  19.5 0.0 copy-done.1
  19.6 0.0 copy-done.3
  19.6 0.0 copy-done.4
  19.6 0.6 copy-done.6
  20.2 0.0 copy-start.5
  20.2 0.9 copy-done.5
  21.1 1.4 setup_kernel.1
  22.5 0.0 copy-start
  22.6 1.0 cosine_bitcast_fusion
  23.6 0.0 collective-permute-done.2.near
  23.6 7.0 %collective-permute-done.3.far = f32[3,256,128]{2,1,0:T(8,128)S(1)} collective-permute-done((f32[3,256,128]{2,1,0:T(8,128)S(1)}, f32[3,256,128]{2,1,0:T(8,128)S(1)}, u32[]{:S(2)}, u32[]{:S(2)}) %collective-permute-start.3) | collective-permute-done | bytes 393248 | tf_op jit(solution)/shard_map/ppermute | solution.py:388
  30.6 0.0 copy-done
  30.6 8.2 %step_kernel.2 = (f32[3,256,128]{2,1,0:T(8,128)S(1)}, f32[3,256,128]{2,1,0:T(8,128)S(1)}, f32[3,256,128]{2,1,0:T(8,128)S(1)}, f32[3,256,128]{2,1,0:T(8,128)S(1)}) custom-call(s32[4]{0:T(128)S(1)} %pad_add_fusion.par, f32[3,256,128]{2,1,0:T(8,128)S(1)} %get-tuple-element.35.first.mid, f32[3,256,128]{2,1,0:T(8,128)S(1)} %get-tuple-element.36.second.mid, ...), custom_call_target="tpu_custom_call" | custom-call | tf_op jit(solution)/shard_map/step_kernel/pallas_call | solution.py:242
  38.8 0.1 collective-permute-start.4
  38.9 4.1 %collective-permute-start.7 = (f32[3,256,128]{2,1,0:T(8,128)S(1)}, f32[3,256,128]{2,1,0:T(8,128)S(1)}, u32[]{:S(2)}, u32[]{:S(2)}) collective-permute-start(f32[3,256,128]{2,1,0:T(8,128)S(1)} %get-tuple-element.46), channel_id=1, source_target_pairs={{1,2},{3,4},{5,6},{7,8},{9,10},{11,12},{13,14},{2,1},{4,3},{6,5},{... | collective-permute-start | bytes 1179656 | tf_op jit(solution)/shard_map/ppermute | solution.py:388
  43.1 0.0 collective-permute-done.4.came
  43.1 0.6 share_kernel.2
  43.7 5.8 %collective-permute-start.5 = (f32[3,128,128]{2,1,0:T(8,128)S(1)}, f32[3,128,128]{2,1,0:T(8,128)S(1)}, u32[]{:S(2)}, u32[]{:S(2)}) collective-permute-start(f32[3,128,128]{2,1,0:T(8,128)S(1)} %get-tuple-element.43), channel_id=1, source_target_pairs={{0,16},{32,48},{64,80},{96,112},{128,144},{160,176},{192,208},{224... | collective-permute-start | bytes 589832 | tf_op jit(solution)/shard_map/ppermute | solution.py:388
  49.5 5.2 %collective-permute-start.6 = (f32[3,128,128]{2,1,0:T(8,128)S(1)}, f32[3,128,128]{2,1,0:T(8,128)S(1)}, u32[]{:S(2)}, u32[]{:S(2)}) collective-permute-start(f32[3,128,128]{2,1,0:T(8,128)S(1)} %get-tuple-element.44), channel_id=1, source_target_pairs={{16,32},{48,64},{80,96},{112,128},{144,160},{176,192},{208,224},{3... | collective-permute-start | bytes 589832 | tf_op jit(solution)/shard_map/ppermute | solution.py:388
  54.6 1.6 %collective-permute-done.7.came = f32[3,256,128]{2,1,0:T(8,128)S(1)} collective-permute-done((f32[3,256,128]{2,1,0:T(8,128)S(1)}, f32[3,256,128]{2,1,0:T(8,128)S(1)}, u32[]{:S(2)}, u32[]{:S(2)}) %collective-permute-start.7) | collective-permute-done | bytes 393248 | tf_op jit(solution)/shard_map/ppermute | solution.py:388
  56.3 0.6 share_kernel.3
  56.9 13.7 %collective-permute-start.8 = (f32[3,128,128]{2,1,0:T(8,128)S(1)}, f32[3,128,128]{2,1,0:T(8,128)S(1)}, u32[]{:S(2)}, u32[]{:S(2)}) collective-permute-start(f32[3,128,128]{2,1,0:T(8,128)S(1)} %get-tuple-element.48), channel_id=1, source_target_pairs={{0,16},{32,48},{64,80},{96,112},{128,144},{160,176},{192,208},{224... | collective-permute-start | bytes 589832 | tf_op jit(solution)/shard_map/ppermute | solution.py:388
  70.6 5.3 %collective-permute-start.9 = (f32[3,128,128]{2,1,0:T(8,128)S(1)}, f32[3,128,128]{2,1,0:T(8,128)S(1)}, u32[]{:S(2)}, u32[]{:S(2)}) collective-permute-start(f32[3,128,128]{2,1,0:T(8,128)S(1)} %get-tuple-element.49), channel_id=1, source_target_pairs={{16,32},{48,64},{80,96},{112,128},{144,160},{176,192},{208,224},{3... | collective-permute-start | bytes 589832 | tf_op jit(solution)/shard_map/ppermute | solution.py:388
  75.9 0.0 collective-permute-done.5.near
  75.9 0.0 collective-permute-done.6.far
  75.9 0.6 update_kernel.2.first.mid_1
  76.6 0.1 collective-permute-start.10
  76.7 0.0 collective-permute-done.8.near
  76.7 4.2 %collective-permute-done.9.far = f32[3,128,128]{2,1,0:T(8,128)S(1)} collective-permute-done((f32[3,128,128]{2,1,0:T(8,128)S(1)}, f32[3,128,128]{2,1,0:T(8,128)S(1)}, u32[]{:S(2)}, u32[]{:S(2)}) %collective-permute-start.9) | collective-permute-done | bytes 196640 | tf_op jit(solution)/shard_map/ppermute | solution.py:388
  80.8 0.6 update_kernel.3.second.mid_2
  81.4 3.5 %collective-permute-start.11 = (f32[3,256,128]{2,1,0:T(8,128)S(1)}, f32[3,256,128]{2,1,0:T(8,128)S(1)}, u32[]{:S(2)}, u32[]{:S(2)}) collective-permute-start(f32[3,256,128]{2,1,0:T(8,128)S(1)} %update_kernel.3.second.mid_2), channel_id=1, source_target_pairs={{1,2},{3,4},{5,6},{7,8},{9,10},{11,12},{13,14},{2,1},{4,3},{6,5},{... | collective-permute-start | bytes 1179656 | tf_op jit(solution)/shard_map/ppermute | solution.py:388
  84.9 0.0 collective-permute-done.10.near
  84.9 11.8 %collective-permute-done.11.far = f32[3,256,128]{2,1,0:T(8,128)S(1)} collective-permute-done((f32[3,256,128]{2,1,0:T(8,128)S(1)}, f32[3,256,128]{2,1,0:T(8,128)S(1)}, u32[]{:S(2)}, u32[]{:S(2)}) %collective-permute-start.11) | collective-permute-done | bytes 393248 | tf_op jit(solution)/shard_map/ppermute | solution.py:388
  96.7 8.2 %step_kernel.3 = (f32[3,256,128]{2,1,0:T(8,128)S(1)}, f32[3,256,128]{2,1,0:T(8,128)S(1)}, f32[3,256,128]{2,1,0:T(8,128)S(1)}, f32[3,256,128]{2,1,0:T(8,128)S(1)}) custom-call(s32[4]{0:T(128)S(1)} %pad_add_fusion.par, f32[3,256,128]{2,1,0:T(8,128)S(1)} %update_kernel.2.first.mid_1, f32[3,256,128]{2,1,0:T(8,128)S(1)} %update_kernel.3.second.mid_2, ...), custom_call_target="tpu_custom_call" | custom-call | tf_op jit(solution)/shard_map/step_kernel/pallas_call | solution.py:242
  104.9 0.1 collective-permute-start.12
  105.0 3.3 %collective-permute-start.13 = (f32[3,256,128]{2,1,0:T(8,128)S(1)}, f32[3,256,128]{2,1,0:T(8,128)S(1)}, u32[]{:S(2)}, u32[]{:S(2)}) collective-permute-start(f32[3,256,128]{2,1,0:T(8,128)S(1)} %get-tuple-element.53), channel_id=1, source_target_pairs={{1,2},{3,4},{5,6},{7,8},{9,10},{11,12},{13,14},{2,1},{4,3},{6,5},{... | collective-permute-start | bytes 1179656 | tf_op jit(solution)/shard_map/ppermute | solution.py:388
  108.3 0.0 collective-permute-done.12.came_1
  108.3 11.9 %collective-permute-done.13.came_2 = f32[3,256,128]{2,1,0:T(8,128)S(1)} collective-permute-done((f32[3,256,128]{2,1,0:T(8,128)S(1)}, f32[3,256,128]{2,1,0:T(8,128)S(1)}, u32[]{:S(2)}, u32[]{:S(2)}) %collective-permute-start.13) | collective-permute-done | bytes 393248 | tf_op jit(solution)/shard_map/ppermute | solution.py:388
  120.2 0.6 close_kernel.1
  120.9 11.1 %collective-permute-start.14 = (f32[2,3,64,128]{3,2,1,0:T(8,128)S(1)}, f32[2,3,64,128]{3,2,1,0:T(8,128)S(1)}, u32[]{:S(2)}, u32[]{:S(2)}) collective-permute-start(f32[2,3,64,128]{3,2,1,0:T(8,128)S(1)} %get-tuple-element.55), channel_id=1, source_target_pairs={{0,16},{32,48},{64,80},{96,112},{128,144},{160,176},{192,208},{224... | collective-permute-start | bytes 589832 | tf_op jit(solution)/shard_map/ppermute | solution.py:388
  131.9 4.0 %collective-permute-start.15 = (f32[2,3,64,128]{3,2,1,0:T(8,128)S(1)}, f32[2,3,64,128]{3,2,1,0:T(8,128)S(1)}, u32[]{:S(2)}, u32[]{:S(2)}) collective-permute-start(f32[2,3,64,128]{3,2,1,0:T(8,128)S(1)} %get-tuple-element.56), channel_id=1, source_target_pairs={{16,32},{48,64},{80,96},{112,128},{144,160},{176,192},{208,224},{3... | collective-permute-start | bytes 589832 | tf_op jit(solution)/shard_map/ppermute | solution.py:388
  136.0 1.7 %collective-permute-done.14.near = f32[2,3,64,128]{3,2,1,0:T(8,128)S(1)} collective-permute-done((f32[2,3,64,128]{3,2,1,0:T(8,128)S(1)}, f32[2,3,64,128]{3,2,1,0:T(8,128)S(1)}, u32[]{:S(2)}, u32[]{:S(2)}) %collective-permute-start.14) | collective-permute-done | bytes 196640 | tf_op jit(solution)/shard_map/ppermute | solution.py:388
  137.7 4.5 %collective-permute-done.15.far = f32[2,3,64,128]{3,2,1,0:T(8,128)S(1)} collective-permute-done((f32[2,3,64,128]{3,2,1,0:T(8,128)S(1)}, f32[2,3,64,128]{3,2,1,0:T(8,128)S(1)}, u32[]{:S(2)}, u32[]{:S(2)}) %collective-permute-start.15) | collective-permute-done | bytes 196640 | tf_op jit(solution)/shard_map/ppermute | solution.py:388
  142.2 1.4 finish_kernel.1
  (1 shorter events, 0.0 us)
Async XLA Ops:
  0.1 1.0 copy-start.2
  1.1 18.5 %copy-start.1 = (f32[2,256,256]{2,1,0:T(8,128)S(1)}, f32[2,256,256]{2,1,0:T(8,128)}, u32[]{:S(2)}) copy-start(f32[2,256,256]{2,1,0:T(8,128)} %probe.1) | copy-start | bytes 1572868
  1.7 6.7 %collective-permute-start = (f32[2,3,64,128]{3,2,1,0:T(8,128)S(1)}, f32[2,3,64,128]{3,2,1,0:T(8,128)S(1)}, u32[]{:S(2)}, u32[]{:S(2)}) collective-permute-start(f32[2,3,64,128]{3,2,1,0:T(8,128)S(1)} %get-tuple-element.33), channel_id=1, source_target_pairs={{0,16},{32,48},{64,80},{96,112},{128,144},{160,176},{192,208},{224... | collective-permute-start | bytes 589832 | tf_op jit(solution)/shard_map/ppermute | solution.py:388
  2.8 11.8 %collective-permute-start.1 = (f32[2,3,64,128]{3,2,1,0:T(8,128)S(1)}, f32[2,3,64,128]{3,2,1,0:T(8,128)S(1)}, u32[]{:S(2)}, u32[]{:S(2)}) collective-permute-start(f32[2,3,64,128]{3,2,1,0:T(8,128)S(1)} %get-tuple-element.34), channel_id=1, source_target_pairs={{16,32},{48,64},{80,96},{112,128},{144,160},{176,192},{208,224},{3... | collective-permute-start | bytes 589832 | tf_op jit(solution)/shard_map/ppermute | solution.py:388
  14.7 4.9 %copy-start.3 = (f32[256,256]{1,0:T(8,128)S(1)}, f32[256,256]{1,0:T(8,128)}, u32[]{:S(2)}) copy-start(f32[256,256]{1,0:T(8,128)} %phase.1) | copy-start | bytes 786436
  14.7 4.9 %copy-start.4 = (f32[1,1,1,256,256]{4,3,2,1,0:T(8,128)S(1)}, f32[1,1,1,256,256]{4,3,2,1,0:T(8,128)}, u32[]{:S(2)}) copy-start(f32[1,1,1,256,256]{4,3,2,1,0:T(8,128)} %param.10) | copy-start | bytes 786436
  15.3 8.3 %collective-permute-start.2 = (f32[3,256,128]{2,1,0:T(8,128)S(1)}, f32[3,256,128]{2,1,0:T(8,128)S(1)}, u32[]{:S(2)}, u32[]{:S(2)}) collective-permute-start(f32[3,256,128]{2,1,0:T(8,128)S(1)} %get-tuple-element.35.first.mid), channel_id=1, source_target_pairs={{0,1},{2,3},{4,5},{6,7},{8,9},{10,11},{12,13},{14,15},{1,0},{3,2},... | collective-permute-start | bytes 1179656 | tf_op jit(solution)/shard_map/ppermute | solution.py:388
  15.4 15.2 %collective-permute-start.3 = (f32[3,256,128]{2,1,0:T(8,128)S(1)}, f32[3,256,128]{2,1,0:T(8,128)S(1)}, u32[]{:S(2)}, u32[]{:S(2)}) collective-permute-start(f32[3,256,128]{2,1,0:T(8,128)S(1)} %get-tuple-element.36.second.mid), channel_id=1, source_target_pairs={{1,2},{3,4},{5,6},{7,8},{9,10},{11,12},{13,14},{2,1},{4,3},{6,5},{... | collective-permute-start | bytes 1179656 | tf_op jit(solution)/shard_map/ppermute | solution.py:388
  19.5 0.7 copy-start.6
  20.2 0.9 copy-start.5
  22.5 8.1 %copy-start = (bf16[4,2,256,256]{3,2,1,0:T(8,128)(2,1)S(1)}, bf16[4,2,256,256]{3,2,1,0:T(8,128)(2,1)}, u32[]{:S(2)}) copy-start(bf16[4,2,256,256]{3,2,1,0:T(8,128)(2,1)} %constant.31.clone.tables) | copy-start | bytes 3145732
  38.8 4.2 %collective-permute-start.4 = (f32[3,256,128]{2,1,0:T(8,128)S(1)}, f32[3,256,128]{2,1,0:T(8,128)S(1)}, u32[]{:S(2)}, u32[]{:S(2)}) collective-permute-start(f32[3,256,128]{2,1,0:T(8,128)S(1)} %get-tuple-element.41), channel_id=1, source_target_pairs={{0,1},{2,3},{4,5},{6,7},{8,9},{10,11},{12,13},{14,15},{1,0},{3,2},... | collective-permute-start | bytes 1179656 | tf_op jit(solution)/shard_map/ppermute | solution.py:388
  38.9 17.3 %collective-permute-start.7 = (f32[3,256,128]{2,1,0:T(8,128)S(1)}, f32[3,256,128]{2,1,0:T(8,128)S(1)}, u32[]{:S(2)}, u32[]{:S(2)}) collective-permute-start(f32[3,256,128]{2,1,0:T(8,128)S(1)} %get-tuple-element.46), channel_id=1, source_target_pairs={{1,2},{3,4},{5,6},{7,8},{9,10},{11,12},{13,14},{2,1},{4,3},{6,5},{... | collective-permute-start | bytes 1179656 | tf_op jit(solution)/shard_map/ppermute | solution.py:388
  43.7 32.2 %collective-permute-start.5 = (f32[3,128,128]{2,1,0:T(8,128)S(1)}, f32[3,128,128]{2,1,0:T(8,128)S(1)}, u32[]{:S(2)}, u32[]{:S(2)}) collective-permute-start(f32[3,128,128]{2,1,0:T(8,128)S(1)} %get-tuple-element.43), channel_id=1, source_target_pairs={{0,16},{32,48},{64,80},{96,112},{128,144},{160,176},{192,208},{224... | collective-permute-start | bytes 589832 | tf_op jit(solution)/shard_map/ppermute | solution.py:388
  49.5 26.5 %collective-permute-start.6 = (f32[3,128,128]{2,1,0:T(8,128)S(1)}, f32[3,128,128]{2,1,0:T(8,128)S(1)}, u32[]{:S(2)}, u32[]{:S(2)}) collective-permute-start(f32[3,128,128]{2,1,0:T(8,128)S(1)} %get-tuple-element.44), channel_id=1, source_target_pairs={{16,32},{48,64},{80,96},{112,128},{144,160},{176,192},{208,224},{3... | collective-permute-start | bytes 589832 | tf_op jit(solution)/shard_map/ppermute | solution.py:388
  56.9 19.8 %collective-permute-start.8 = (f32[3,128,128]{2,1,0:T(8,128)S(1)}, f32[3,128,128]{2,1,0:T(8,128)S(1)}, u32[]{:S(2)}, u32[]{:S(2)}) collective-permute-start(f32[3,128,128]{2,1,0:T(8,128)S(1)} %get-tuple-element.48), channel_id=1, source_target_pairs={{0,16},{32,48},{64,80},{96,112},{128,144},{160,176},{192,208},{224... | collective-permute-start | bytes 589832 | tf_op jit(solution)/shard_map/ppermute | solution.py:388
  70.6 10.2 %collective-permute-start.9 = (f32[3,128,128]{2,1,0:T(8,128)S(1)}, f32[3,128,128]{2,1,0:T(8,128)S(1)}, u32[]{:S(2)}, u32[]{:S(2)}) collective-permute-start(f32[3,128,128]{2,1,0:T(8,128)S(1)} %get-tuple-element.49), channel_id=1, source_target_pairs={{16,32},{48,64},{80,96},{112,128},{144,160},{176,192},{208,224},{3... | collective-permute-start | bytes 589832 | tf_op jit(solution)/shard_map/ppermute | solution.py:388
  76.6 8.3 %collective-permute-start.10 = (f32[3,256,128]{2,1,0:T(8,128)S(1)}, f32[3,256,128]{2,1,0:T(8,128)S(1)}, u32[]{:S(2)}, u32[]{:S(2)}) collective-permute-start(f32[3,256,128]{2,1,0:T(8,128)S(1)} %update_kernel.2.first.mid_1), channel_id=1, source_target_pairs={{0,1},{2,3},{4,5},{6,7},{8,9},{10,11},{12,13},{14,15},{1,0},{3,2},... | collective-permute-start | bytes 1179656 | tf_op jit(solution)/shard_map/ppermute | solution.py:388
  81.4 15.3 %collective-permute-start.11 = (f32[3,256,128]{2,1,0:T(8,128)S(1)}, f32[3,256,128]{2,1,0:T(8,128)S(1)}, u32[]{:S(2)}, u32[]{:S(2)}) collective-permute-start(f32[3,256,128]{2,1,0:T(8,128)S(1)} %update_kernel.3.second.mid_2), channel_id=1, source_target_pairs={{1,2},{3,4},{5,6},{7,8},{9,10},{11,12},{13,14},{2,1},{4,3},{6,5},{... | collective-permute-start | bytes 1179656 | tf_op jit(solution)/shard_map/ppermute | solution.py:388
  104.9 3.4 %collective-permute-start.12 = (f32[3,256,128]{2,1,0:T(8,128)S(1)}, f32[3,256,128]{2,1,0:T(8,128)S(1)}, u32[]{:S(2)}, u32[]{:S(2)}) collective-permute-start(f32[3,256,128]{2,1,0:T(8,128)S(1)} %get-tuple-element.52), channel_id=1, source_target_pairs={{0,1},{2,3},{4,5},{6,7},{8,9},{10,11},{12,13},{14,15},{1,0},{3,2},... | collective-permute-start | bytes 1179656 | tf_op jit(solution)/shard_map/ppermute | solution.py:388
  105.0 15.2 %collective-permute-start.13 = (f32[3,256,128]{2,1,0:T(8,128)S(1)}, f32[3,256,128]{2,1,0:T(8,128)S(1)}, u32[]{:S(2)}, u32[]{:S(2)}) collective-permute-start(f32[3,256,128]{2,1,0:T(8,128)S(1)} %get-tuple-element.53), channel_id=1, source_target_pairs={{1,2},{3,4},{5,6},{7,8},{9,10},{11,12},{13,14},{2,1},{4,3},{6,5},{... | collective-permute-start | bytes 1179656 | tf_op jit(solution)/shard_map/ppermute | solution.py:388
  120.9 16.8 %collective-permute-start.14 = (f32[2,3,64,128]{3,2,1,0:T(8,128)S(1)}, f32[2,3,64,128]{3,2,1,0:T(8,128)S(1)}, u32[]{:S(2)}, u32[]{:S(2)}) collective-permute-start(f32[2,3,64,128]{3,2,1,0:T(8,128)S(1)} %get-tuple-element.55), channel_id=1, source_target_pairs={{0,16},{32,48},{64,80},{96,112},{128,144},{160,176},{192,208},{224... | collective-permute-start | bytes 589832 | tf_op jit(solution)/shard_map/ppermute | solution.py:388
  131.9 10.2 %collective-permute-start.15 = (f32[2,3,64,128]{3,2,1,0:T(8,128)S(1)}, f32[2,3,64,128]{3,2,1,0:T(8,128)S(1)}, u32[]{:S(2)}, u32[]{:S(2)}) collective-permute-start(f32[2,3,64,128]{3,2,1,0:T(8,128)S(1)} %get-tuple-element.56), channel_id=1, source_target_pairs={{16,32},{48,64},{80,96},{112,128},{144,160},{176,192},{208,224},{3... | collective-permute-start | bytes 589832 | tf_op jit(solution)/shard_map/ppermute | solution.py:388

commit v3 on v2

--- a/solution.py
+++ b/solution.py
@@ -1,4 +1,3 @@
-import functools
 import math
 
 import jax
@@ -8,6 +7,7 @@
 from jax.experimental import pallas as pl
 from jax.experimental.pallas import tpu as pltpu
 from jax.sharding import PartitionSpec as P
+
 
 MARGIN = 64
 CORE = 128
@@ -52,14 +52,14 @@
 
 def from_left(tables, which, value):
     high, low = split(value)
-    t_high, t_low = tables[which, 0], tables[which, 1]
-    return dot(t_high, high) + (dot(t_high, low) + dot(t_low, high))
+    both = dot(tables[which].reshape(2 * TILE, TILE), high)
+    return both[:TILE] + (both[TILE:] + dot(tables[which, 0], low))
 
 
 def from_right(tables, which, value):
     high, low = split(value)
-    t_high, t_low = tables[which, 0], tables[which, 1]
-    return dot(high, t_high) + (dot(high, t_low) + dot(low, t_high))
+    both = dot(jnp.concatenate([high, low], axis=0), tables[which, 0])
+    return both[:TILE] + (both[TILE:] + dot(high, tables[which, 1]))
 
 
 def stack(*rows):
@@ -160,7 +160,6 @@
     send_far,
     tile,
     field,
-    up,
 ):
     nearby = near_lanes(par, TILE)
     for layer in range(SLICES):
@@ -170,21 +169,14 @@
         real, imag = unpack(nearby, far[layer], near[layer])
         tile[layer, 0, :, CORE:] = real
         tile[layer, 1, :, CORE:] = imag
-    field[0, 0] = lit[0]
-    field[0, 1] = lit[1]
-
-    def ahead(layer, carry):
-        f_real, f_imag = field[layer, 0], field[layer, 1]
+    f_real, f_imag = lit[0], lit[1]
+    for layer in range(SLICES - 1):
         t_real, t_imag = tile[layer, 0], tile[layer, 1]
-        real, imag = propagate(
+        f_real, f_imag = propagate(
             tables, f_real * t_real - f_imag * t_imag, f_real * t_imag + f_imag * t_real, wave, 1
         )
-        field[layer + 1, 0] = real
-        field[layer + 1, 1] = imag
-        return carry
-
-    lax.fori_loop(0, SLICES - 1, ahead, 0)
-    f_real, f_imag = field[SLICES - 1, 0], field[SLICES - 1, 1]
+        field[layer, 0] = f_real
+        field[layer, 1] = f_imag
     t_real, t_imag = tile[SLICES - 1, 0], tile[SLICES - 1, 1]
     freq = forward(tables, f_real * t_real - f_imag * t_imag, f_real * t_imag + f_imag * t_real)
     out = []
@@ -192,32 +184,25 @@
         real, imag = freq[parity][:, :CORE], freq[parity][:, CORE:]
         residue = real * real + imag * imag - patterns[:, pl.ds(parity * CORE, CORE)]
         out.append(beside(residue * real, residue * imag))
-    real, imag = backward(tables, out)
-    up[0] = real
-    up[1] = imag
-
-    def gradient(layer):
-        f_real, f_imag = field[layer, 0], field[layer, 1]
-        u_real, u_imag = up[0], up[1]
+    u_real, u_imag = backward(tables, out)
+    for layer in reversed(range(SLICES)):
+        if layer > 0:
+            f_real, f_imag = field[layer - 1, 0], field[layer - 1, 1]
+        else:
+            f_real, f_imag = lit[0], lit[1]
         real = f_real * u_real + f_imag * u_imag
         imag = f_real * u_imag - f_imag * u_real
         part_first[layer], part_second[layer] = pack(nearby, real[:, :CORE], imag[:, :CORE])
         send_far[layer], send_near[layer] = pack(nearby, real[:, CORE:], imag[:, CORE:])
-
-    def behind(turn, carry):
-        layer = SLICES - 1 - turn
-        gradient(layer)
-        t_real, t_imag = tile[layer, 0], tile[layer, 1]
-        u_real, u_imag = up[0], up[1]
-        real, imag = propagate(
-            tables, t_real * u_real + t_imag * u_imag, t_real * u_imag - t_imag * u_real, wave, -1
-        )
-        up[0] = real
-        up[1] = imag
-        return carry
-
-    lax.fori_loop(0, SLICES - 1, behind, 0)
-    gradient(0)
+        if layer > 0:
+            t_real, t_imag = tile[layer, 0], tile[layer, 1]
+            u_real, u_imag = propagate(
+                tables,
+                t_real * u_real + t_imag * u_imag,
+                t_real * u_imag - t_imag * u_real,
+                wave,
+                -1,
+            )
 
 
 def call(body, outs, scratch=(), smem=1, count=0, limit=8):
@@ -229,7 +214,6 @@
         out_specs=[pl.BlockSpec(memory_space=pltpu.VMEM)] * len(outs),
         scratch_shapes=list(scratch),
         compiler_params=pltpu.CompilerParams(vmem_limit_bytes=limit << 20),
-        name=body.__name__,
     )
 
 
@@ -244,8 +228,7 @@
         (PACK, PACK, PACK, PACK),
         (
             pltpu.VMEM((SLICES, 2, TILE, TILE), jnp.float32),
-            pltpu.VMEM((SLICES, 2, TILE, TILE), jnp.float32),
-            pltpu.VMEM((2, TILE, TILE), jnp.float32),
+            pltpu.VMEM((SLICES - 1, 2, TILE, TILE), jnp.float32),
         ),
         count=8,
         limit=24,
@@ -309,44 +292,46 @@
     return call(assemble_kernel, (PACK, PACK), count=4)(*args)
 
 
-def share_kernel(par, part, came, total, send_near, send_far):
-    even = par[0] == 0
-    for layer in range(SLICES):
-        value = part[layer] + came[layer]
-        total[layer] = value
-        a, b, d, e = (value[k * MARGIN : (k + 1) * MARGIN] for k in range(4))
-        send_near[layer, :MARGIN] = jnp.where(even, b, e)
-        send_near[layer, MARGIN:] = jnp.where(even, d, a)
-        send_far[layer, :MARGIN] = jnp.where(even, e, b)
-        send_far[layer, MARGIN:] = jnp.where(even, a, d)
+def share_kernel(par, part_1, part_2, came_1, came_2, total, send_near, send_far):
+    even = par[0] == 0
+    for k, (part, came) in enumerate(((part_1, came_1), (part_2, came_2))):
+        for layer in range(SLICES):
+            value = part[layer] + came[layer]
+            total[k, layer] = value
+            a, b, d, e = (value[n * MARGIN : (n + 1) * MARGIN] for n in range(4))
+            send_near[k, layer, :MARGIN] = jnp.where(even, b, e)
+            send_near[k, layer, MARGIN:] = jnp.where(even, d, a)
+            send_far[k, layer, :MARGIN] = jnp.where(even, e, b)
+            send_far[k, layer, MARGIN:] = jnp.where(even, a, d)
 
 
 def share(*args):
-    return call(share_kernel, (PACK, HALF, HALF), count=2)(*args)
-
-
-def update_kernel(par, mid, total, near, far, new):
+    return call(share_kernel, ((2, *PACK), (2, *HALF), (2, *HALF)), count=4)(*args)
+
+
+def update_kernel(par, mid_1, mid_2, total, near, far, new_1, new_2):
     even = par[0] == 0
     above = jnp.where(par[2] == 0, 0.0, STEP_SIZE)
     below = jnp.where(par[3] == 0, 0.0, STEP_SIZE)
-    for layer in range(SLICES):
-        e, o = near[layer], far[layer]
-        down = jnp.where(even, e, o)
-        up = jnp.where(even, o, e)
-        for k, (added, scale) in enumerate(
-            (
-                (up[MARGIN:], STEP_SIZE),
-                (down[:MARGIN], STEP_SIZE),
-                (down[MARGIN:], below),
-                (up[:MARGIN], above),
-            )
-        ):
-            rows = pl.ds(k * MARGIN, MARGIN)
-            new[layer, rows] = mid[layer, rows] - scale * (total[layer, rows] + added)
+    for k, (mid, new) in enumerate(((mid_1, new_1), (mid_2, new_2))):
+        for layer in range(SLICES):
+            e, o = near[k, layer], far[k, layer]
+            down = jnp.where(even, e, o)
+            up = jnp.where(even, o, e)
+            for n, (added, scale) in enumerate(
+                (
+                    (up[MARGIN:], STEP_SIZE),
+                    (down[:MARGIN], STEP_SIZE),
+                    (down[MARGIN:], below),
+                    (up[:MARGIN], above),
+                )
+            ):
+                rows = pl.ds(n * MARGIN, MARGIN)
+                new[layer, rows] = mid[layer, rows] - scale * (total[k, layer, rows] + added)
 
 
 def update(*args):
-    return call(update_kernel, (PACK,), count=4)(*args)[0]
+    return call(update_kernel, (PACK, PACK), count=5)(*args)
 
 
 def close_kernel(par, part_1, part_2, came_1, came_2, total, send_near, send_far):
@@ -390,10 +375,11 @@
 
 def swap_rows(near, far):
     far = swap("ty", 1, far)
-    return swap("ty", 0, near), far
-
-
-def shards(object_field, probe, propagator_phase, patterns, scan_positions):
+    near = swap("ty", 0, near)
+    return near, far
+
+
+def exchange_and_step(object_field, probe, propagator_phase, patterns, scan_positions):
     row, col = lax.axis_index("ty"), lax.axis_index("tx")
     par = jnp.stack([row % 2, col % 2, row, lax.axis_size("ty") - 1 - row]).astype(jnp.int32)
     first, second, near, far = begin(par, object_field)
@@ -413,12 +399,9 @@
         far = swap("tx", 1, far)
         near = swap("tx", 0, near)
         if turn < STEPS - 1:
-            total_1, near_1, far_1 = share(par, part_1, near)
-            near_1, far_1 = swap_rows(near_1, far_1)
-            total_2, near_2, far_2 = share(par, part_2, far)
-            near_2, far_2 = swap_rows(near_2, far_2)
-            first = update(par, first, total_1, near_1, far_1)
-            second = update(par, second, total_2, near_2, far_2)
+            total, near, far = share(par, part_1, part_2, near, far)
+            near, far = swap_rows(near, far)
+            first, second = update(par, first, second, total, near, far)
     total, near, far = close(par, part_1, part_2, near, far)
     near, far = swap_rows(near, far)
     return finish(par, first, second, total, near, far)
@@ -433,5 +416,5 @@
         P("ty", "tx", None, None),
     )
     return jax.shard_map(
-        shards, mesh=mesh, in_specs=placed, out_specs=P(None, None, "ty", "tx"), check_vma=False
+        exchange_and_step, mesh=mesh, in_specs=placed, out_specs=P(None, None, "ty", "tx"), check_vma=False
     )

time: 144 us -> 135 us (0.938)
  starting transfers between devices: 66.3 us -> 45.6 us
  waiting for transfers between devices: 49.8 us -> 62.7 us
  Pallas kernels: 23.5 us -> 21.6 us
    ppermute x16 -> x14, starting transfers between devices: 66.3 us -> 45.6 us  [swap(): return lax.ppermute(block, axis, pairs + [(j, i) for i, j in pairs])]
    ppermute x16 -> x14, waiting for transfers between devices: 49.8 us -> 62.7 us  [swap(): return lax.ppermute(block, axis, pairs + [(j, i) for i, j in pairs])]
  transfers between devices with their start and end apart: 16 -> 14, of which waited for: 9 -> 10; matrix products, arithmetic and copies ran while one was open for 1% -> 1% of each run, Pallas kernels for 3% -> 1%
where the time goes in v3:
time: 135 us; the launch traced here: 134 us
  waiting for transfers between devices  62.7 us (46%)
  starting transfers between devices  45.6 us (34%)
  Pallas kernels  21.6 us (16%)
  local copies, waits for them, and re-layouts  3.55 us (3%)
    ppermute x14, waiting for transfers between devices, swap(): return lax.ppermute(block, axis, pairs + [(j, i) for i, j in pairs])  62.7 us
    ppermute x14, starting transfers between devices, swap(): return lax.ppermute(block, axis, pairs + [(j, i) for i, j in pairs])  45.6 us
    pallas_call x2, Pallas kernels, step(): call(step_kernel, (PACK, PACK, PACK, PACK), (pltpu.VMEM((SLICES, 2, TILE,...  15.6 us
  transfers between devices with their start and end apart: 14, of which 10 were waited for; matrix products, arithmetic and copies ran while one was open for 1% of the time, Pallas kernels for 1%

profile of v3, /device:TPU:232, one launch (start us, length us, event | category | flops | bytes accessed | tf_op | source)
XLA Modules:
  0.0 133.9 jit_solution(7037852169867878144)
XLA Ops:
  0.0 0.1 pad_add_fusion.par
  0.1 0.0 copy-start.2
  0.1 1.0 copy-done.2
  1.1 0.0 copy-start.1
  1.1 0.7 shard_map.73
  1.7 1.1 collective-permute-start
  2.8 4.8 %collective-permute-start.1 = (f32[2,3,64,128]{3,2,1,0:T(8,128)S(1)}, f32[2,3,64,128]{3,2,1,0:T(8,128)S(1)}, u32[]{:S(2)}, u32[]{:S(2)}) collective-permute-start(f32[2,3,64,128]{3,2,1,0:T(8,128)S(1)} %get-tuple-element.33), channel_id=1, source_target_pairs={{16,32},{48,64},{80,96},{112,128},{144,160},{176,192},{208,224},{3... | collective-permute-start | bytes 589832 | tf_op jit(solution)/shard_map/ppermute | solution.py:373
  7.7 0.8 collective-permute-done.near
  8.5 6.2 %collective-permute-done.1.far = f32[2,3,64,128]{3,2,1,0:T(8,128)S(1)} collective-permute-done((f32[2,3,64,128]{3,2,1,0:T(8,128)S(1)}, f32[2,3,64,128]{3,2,1,0:T(8,128)S(1)}, u32[]{:S(2)}, u32[]{:S(2)}) %collective-permute-start.1) | collective-permute-done | bytes 196640 | tf_op jit(solution)/shard_map/ppermute | solution.py:373
  14.7 0.0 copy-start.3
  14.7 0.0 copy-start.4
  14.7 0.6 shard_map.74
  15.3 0.1 collective-permute-start.2
  15.4 4.1 %collective-permute-start.3 = (f32[3,256,128]{2,1,0:T(8,128)S(1)}, f32[3,256,128]{2,1,0:T(8,128)S(1)}, u32[]{:S(2)}, u32[]{:S(2)}) collective-permute-start(f32[3,256,128]{2,1,0:T(8,128)S(1)} %get-tuple-element.35.second.mid_2), channel_id=1, source_target_pairs={{1,2},{3,4},{5,6},{7,8},{9,10},{11,12},{13,14},{2,1},{4,3},{6,5},{... | collective-permute-start | bytes 1179656 | tf_op jit(solution)/shard_map/ppermute | solution.py:373
  19.5 0.0 copy-start.6
  19.5 0.0 copy-done.1
  19.6 0.0 copy-done.3
  19.6 0.0 copy-done.4
  19.6 0.6 copy-done.6
  20.2 0.0 copy-start.5
  20.2 0.9 copy-done.5
  21.1 1.4 %shard_map.75 = (f32[2,256,256]{2,1,0:T(8,128)S(1)}, f32[256,256]{1,0:T(8,128)S(1)}, f32[256,256]{1,0:T(8,128)S(1)}) custom-call(s32[2]{0:T(128)S(1)} %bitcast.11, f32[2,256,256]{2,1,0:T(8,128)S(1)} %copy-done.1, f32[256,256]{1,0:T(8,128)S(1)} %copy-done.3, f32[256,256]{1,0:T(8,128)S(1)} %bitcast.10, bf16[2,256,256]{2,1,0:T(8,128)(2,1)S(1)} %copy-done.5), custom_call_target="tpu_custom_call" | custom-call | tf_op jit(solution)/shard_map/pallas_call | solution.py:264
  22.5 0.0 copy-start
  22.6 1.0 cosine_bitcast_fusion
  23.6 0.0 collective-permute-done.2.near
  23.6 7.0 %collective-permute-done.3.far = f32[3,256,128]{2,1,0:T(8,128)S(1)} collective-permute-done((f32[3,256,128]{2,1,0:T(8,128)S(1)}, f32[3,256,128]{2,1,0:T(8,128)S(1)}, u32[]{:S(2)}, u32[]{:S(2)}) %collective-permute-start.3) | collective-permute-done | bytes 393248 | tf_op jit(solution)/shard_map/ppermute | solution.py:373
  30.6 0.0 copy-done
  30.6 7.8 %shard_map.76 = (f32[3,256,128]{2,1,0:T(8,128)S(1)}, f32[3,256,128]{2,1,0:T(8,128)S(1)}, f32[3,256,128]{2,1,0:T(8,128)S(1)}, f32[3,256,128]{2,1,0:T(8,128)S(1)}) custom-call(s32[4]{0:T(128)S(1)} %pad_add_fusion.par, f32[3,256,128]{2,1,0:T(8,128)S(1)} %get-tuple-element.34.first.mid_1, f32[3,256,128]{2,1,0:T(8,128)S(1)} %get-tuple-element.35.second.mid_2, ...), custom_call_target="tpu_custom_call" | custom-call | tf_op jit(solution)/shard_map/pallas_call | solution.py:226
  38.4 0.1 collective-permute-start.4
  38.5 4.1 %collective-permute-start.5 = (f32[3,256,128]{2,1,0:T(8,128)S(1)}, f32[3,256,128]{2,1,0:T(8,128)S(1)}, u32[]{:S(2)}, u32[]{:S(2)}) collective-permute-start(f32[3,256,128]{2,1,0:T(8,128)S(1)} %get-tuple-element.42), channel_id=1, source_target_pairs={{1,2},{3,4},{5,6},{7,8},{9,10},{11,12},{13,14},{2,1},{4,3},{6,5},{... | collective-permute-start | bytes 1179656 | tf_op jit(solution)/shard_map/ppermute | solution.py:373
  42.7 0.0 collective-permute-done.4.came_1
  42.7 11.0 %collective-permute-done.5.came_2 = f32[3,256,128]{2,1,0:T(8,128)S(1)} collective-permute-done((f32[3,256,128]{2,1,0:T(8,128)S(1)}, f32[3,256,128]{2,1,0:T(8,128)S(1)}, u32[]{:S(2)}, u32[]{:S(2)}) %collective-permute-start.5) | collective-permute-done | bytes 393248 | tf_op jit(solution)/shard_map/ppermute | solution.py:373
  53.7 0.6 shard_map.77
  54.4 6.2 %collective-permute-start.6 = (f32[2,3,128,128]{3,2,1,0:T(8,128)S(1)}, f32[2,3,128,128]{3,2,1,0:T(8,128)S(1)}, u32[]{:S(2)}, u32[]{:S(2)}) collective-permute-start(f32[2,3,128,128]{3,2,1,0:T(8,128)S(1)} %get-tuple-element.44), channel_id=1, source_target_pairs={{0,16},{32,48},{64,80},{96,112},{128,144},{160,176},{192,208},{224... | collective-permute-start | bytes 1179656 | tf_op jit(solution)/shard_map/ppermute | solution.py:373
  60.6 5.5 %collective-permute-start.7 = (f32[2,3,128,128]{3,2,1,0:T(8,128)S(1)}, f32[2,3,128,128]{3,2,1,0:T(8,128)S(1)}, u32[]{:S(2)}, u32[]{:S(2)}) collective-permute-start(f32[2,3,128,128]{3,2,1,0:T(8,128)S(1)} %get-tuple-element.45), channel_id=1, source_target_pairs={{16,32},{48,64},{80,96},{112,128},{144,160},{176,192},{208,224},{3... | collective-permute-start | bytes 1179656 | tf_op jit(solution)/shard_map/ppermute | solution.py:373
  66.1 3.7 %collective-permute-done.6.near = f32[2,3,128,128]{3,2,1,0:T(8,128)S(1)} collective-permute-done((f32[2,3,128,128]{3,2,1,0:T(8,128)S(1)}, f32[2,3,128,128]{3,2,1,0:T(8,128)S(1)}, u32[]{:S(2)}, u32[]{:S(2)}) %collective-permute-start.6) | collective-permute-done | bytes 393248 | tf_op jit(solution)/shard_map/ppermute | solution.py:373
  69.8 5.3 %collective-permute-done.7.far = f32[2,3,128,128]{3,2,1,0:T(8,128)S(1)} collective-permute-done((f32[2,3,128,128]{3,2,1,0:T(8,128)S(1)}, f32[2,3,128,128]{3,2,1,0:T(8,128)S(1)}, u32[]{:S(2)}, u32[]{:S(2)}) %collective-permute-start.7) | collective-permute-done | bytes 393248 | tf_op jit(solution)/shard_map/ppermute | solution.py:373
  75.1 0.7 shard_map.78
  75.8 0.1 collective-permute-start.8
  75.9 4.9 %collective-permute-start.9 = (f32[3,256,128]{2,1,0:T(8,128)S(1)}, f32[3,256,128]{2,1,0:T(8,128)S(1)}, u32[]{:S(2)}, u32[]{:S(2)}) collective-permute-start(f32[3,256,128]{2,1,0:T(8,128)S(1)} %get-tuple-element.47.second.mid_2), channel_id=1, source_target_pairs={{1,2},{3,4},{5,6},{7,8},{9,10},{11,12},{13,14},{2,1},{4,3},{6,5},{... | collective-permute-start | bytes 1179656 | tf_op jit(solution)/shard_map/ppermute | solution.py:373
  80.7 0.0 collective-permute-done.8.near
  80.7 10.3 %collective-permute-done.9.far = f32[3,256,128]{2,1,0:T(8,128)S(1)} collective-permute-done((f32[3,256,128]{2,1,0:T(8,128)S(1)}, f32[3,256,128]{2,1,0:T(8,128)S(1)}, u32[]{:S(2)}, u32[]{:S(2)}) %collective-permute-start.9) | collective-permute-done | bytes 393248 | tf_op jit(solution)/shard_map/ppermute | solution.py:373
  91.1 7.8 %shard_map.79 = (f32[3,256,128]{2,1,0:T(8,128)S(1)}, f32[3,256,128]{2,1,0:T(8,128)S(1)}, f32[3,256,128]{2,1,0:T(8,128)S(1)}, f32[3,256,128]{2,1,0:T(8,128)S(1)}) custom-call(s32[4]{0:T(128)S(1)} %pad_add_fusion.par, f32[3,256,128]{2,1,0:T(8,128)S(1)} %get-tuple-element.46.first.mid_1, f32[3,256,128]{2,1,0:T(8,128)S(1)} %get-tuple-element.47.second.mid_2, ...), custom_call_target="tpu_custom_call" | custom-call | tf_op jit(solution)/shard_map/pallas_call | solution.py:226
  98.9 0.1 collective-permute-start.10
  99.0 4.7 %collective-permute-start.11 = (f32[3,256,128]{2,1,0:T(8,128)S(1)}, f32[3,256,128]{2,1,0:T(8,128)S(1)}, u32[]{:S(2)}, u32[]{:S(2)}) collective-permute-start(f32[3,256,128]{2,1,0:T(8,128)S(1)} %get-tuple-element.51), channel_id=1, source_target_pairs={{1,2},{3,4},{5,6},{7,8},{9,10},{11,12},{13,14},{2,1},{4,3},{6,5},{... | collective-permute-start | bytes 1179656 | tf_op jit(solution)/shard_map/ppermute | solution.py:373
  103.7 0.0 collective-permute-done.10.came_1
  103.7 10.5 %collective-permute-done.11.came_2 = f32[3,256,128]{2,1,0:T(8,128)S(1)} collective-permute-done((f32[3,256,128]{2,1,0:T(8,128)S(1)}, f32[3,256,128]{2,1,0:T(8,128)S(1)}, u32[]{:S(2)}, u32[]{:S(2)}) %collective-permute-start.11) | collective-permute-done | bytes 393248 | tf_op jit(solution)/shard_map/ppermute | solution.py:373
  114.2 0.6 shard_map.80
  114.8 7.4 %collective-permute-start.12 = (f32[2,3,64,128]{3,2,1,0:T(8,128)S(1)}, f32[2,3,64,128]{3,2,1,0:T(8,128)S(1)}, u32[]{:S(2)}, u32[]{:S(2)}) collective-permute-start(f32[2,3,64,128]{3,2,1,0:T(8,128)S(1)} %get-tuple-element.53), channel_id=1, source_target_pairs={{0,16},{32,48},{64,80},{96,112},{128,144},{160,176},{192,208},{224... | collective-permute-start | bytes 589832 | tf_op jit(solution)/shard_map/ppermute | solution.py:373
  122.2 2.4 %collective-permute-start.13 = (f32[2,3,64,128]{3,2,1,0:T(8,128)S(1)}, f32[2,3,64,128]{3,2,1,0:T(8,128)S(1)}, u32[]{:S(2)}, u32[]{:S(2)}) collective-permute-start(f32[2,3,64,128]{3,2,1,0:T(8,128)S(1)} %get-tuple-element.54), channel_id=1, source_target_pairs={{16,32},{48,64},{80,96},{112,128},{144,160},{176,192},{208,224},{3... | collective-permute-start | bytes 589832 | tf_op jit(solution)/shard_map/ppermute | solution.py:373
  124.7 1.2 collective-permute-done.12.near
  125.9 6.6 %collective-permute-done.13.far = f32[2,3,64,128]{3,2,1,0:T(8,128)S(1)} collective-permute-done((f32[2,3,64,128]{3,2,1,0:T(8,128)S(1)}, f32[2,3,64,128]{3,2,1,0:T(8,128)S(1)}, u32[]{:S(2)}, u32[]{:S(2)}) %collective-permute-start.13) | collective-permute-done | bytes 196640 | tf_op jit(solution)/shard_map/ppermute | solution.py:373
  132.5 1.4 %shard_map.81 = f32[3,2,128,128]{3,2,1,0:T(8,128)} custom-call(s32[4]{0:T(128)S(1)} %pad_add_fusion.par, f32[3,256,128]{2,1,0:T(8,128)S(1)} %get-tuple-element.46.first.mid_1, f32[3,256,128]{2,1,0:T(8,128)S(1)} %get-tuple-element.47.second.mid_2, f32[2,3,128,128]{3,2,1,0:T(8,128)S(1)} %get-tuple-element.52.total, ...), custom_call_target="tpu_custom_call" | custom-call | tf_op jit(solution)/shard_map/pallas_call | solution.py:367
  (1 shorter events, 0.0 us)
Async XLA Ops:
  0.1 1.0 copy-start.2
  1.1 18.5 %copy-start.1 = (f32[2,256,256]{2,1,0:T(8,128)S(1)}, f32[2,256,256]{2,1,0:T(8,128)}, u32[]{:S(2)}) copy-start(f32[2,256,256]{2,1,0:T(8,128)} %probe.1) | copy-start | bytes 1572868
  1.7 6.7 %collective-permute-start = (f32[2,3,64,128]{3,2,1,0:T(8,128)S(1)}, f32[2,3,64,128]{3,2,1,0:T(8,128)S(1)}, u32[]{:S(2)}, u32[]{:S(2)}) collective-permute-start(f32[2,3,64,128]{3,2,1,0:T(8,128)S(1)} %get-tuple-element.32), channel_id=1, source_target_pairs={{0,16},{32,48},{64,80},{96,112},{128,144},{160,176},{192,208},{224... | collective-permute-start | bytes 589832 | tf_op jit(solution)/shard_map/ppermute | solution.py:373
  2.8 11.8 %collective-permute-start.1 = (f32[2,3,64,128]{3,2,1,0:T(8,128)S(1)}, f32[2,3,64,128]{3,2,1,0:T(8,128)S(1)}, u32[]{:S(2)}, u32[]{:S(2)}) collective-permute-start(f32[2,3,64,128]{3,2,1,0:T(8,128)S(1)} %get-tuple-element.33), channel_id=1, source_target_pairs={{16,32},{48,64},{80,96},{112,128},{144,160},{176,192},{208,224},{3... | collective-permute-start | bytes 589832 | tf_op jit(solution)/shard_map/ppermute | solution.py:373
  14.7 4.9 %copy-start.3 = (f32[256,256]{1,0:T(8,128)S(1)}, f32[256,256]{1,0:T(8,128)}, u32[]{:S(2)}) copy-start(f32[256,256]{1,0:T(8,128)} %phase.1) | copy-start | bytes 786436
  14.7 4.9 %copy-start.4 = (f32[1,1,1,256,256]{4,3,2,1,0:T(8,128)S(1)}, f32[1,1,1,256,256]{4,3,2,1,0:T(8,128)}, u32[]{:S(2)}) copy-start(f32[1,1,1,256,256]{4,3,2,1,0:T(8,128)} %param.10) | copy-start | bytes 786436
  15.3 8.3 %collective-permute-start.2 = (f32[3,256,128]{2,1,0:T(8,128)S(1)}, f32[3,256,128]{2,1,0:T(8,128)S(1)}, u32[]{:S(2)}, u32[]{:S(2)}) collective-permute-start(f32[3,256,128]{2,1,0:T(8,128)S(1)} %get-tuple-element.34.first.mid_1), channel_id=1, source_target_pairs={{0,1},{2,3},{4,5},{6,7},{8,9},{10,11},{12,13},{14,15},{1,0},{3,2},... | collective-permute-start | bytes 1179656 | tf_op jit(solution)/shard_map/ppermute | solution.py:373
  15.4 15.2 %collective-permute-start.3 = (f32[3,256,128]{2,1,0:T(8,128)S(1)}, f32[3,256,128]{2,1,0:T(8,128)S(1)}, u32[]{:S(2)}, u32[]{:S(2)}) collective-permute-start(f32[3,256,128]{2,1,0:T(8,128)S(1)} %get-tuple-element.35.second.mid_2), channel_id=1, source_target_pairs={{1,2},{3,4},{5,6},{7,8},{9,10},{11,12},{13,14},{2,1},{4,3},{6,5},{... | collective-permute-start | bytes 1179656 | tf_op jit(solution)/shard_map/ppermute | solution.py:373
  19.5 0.7 copy-start.6
  20.2 0.9 copy-start.5
  22.5 8.1 %copy-start = (bf16[4,2,256,256]{3,2,1,0:T(8,128)(2,1)S(1)}, bf16[4,2,256,256]{3,2,1,0:T(8,128)(2,1)}, u32[]{:S(2)}) copy-start(bf16[4,2,256,256]{3,2,1,0:T(8,128)(2,1)} %constant.31.clone.tables) | copy-start | bytes 3145732
  38.4 4.2 %collective-permute-start.4 = (f32[3,256,128]{2,1,0:T(8,128)S(1)}, f32[3,256,128]{2,1,0:T(8,128)S(1)}, u32[]{:S(2)}, u32[]{:S(2)}) collective-permute-start(f32[3,256,128]{2,1,0:T(8,128)S(1)} %get-tuple-element.41), channel_id=1, source_target_pairs={{0,1},{2,3},{4,5},{6,7},{8,9},{10,11},{12,13},{14,15},{1,0},{3,2},... | collective-permute-start | bytes 1179656 | tf_op jit(solution)/shard_map/ppermute | solution.py:373
  38.5 15.2 %collective-permute-start.5 = (f32[3,256,128]{2,1,0:T(8,128)S(1)}, f32[3,256,128]{2,1,0:T(8,128)S(1)}, u32[]{:S(2)}, u32[]{:S(2)}) collective-permute-start(f32[3,256,128]{2,1,0:T(8,128)S(1)} %get-tuple-element.42), channel_id=1, source_target_pairs={{1,2},{3,4},{5,6},{7,8},{9,10},{11,12},{13,14},{2,1},{4,3},{6,5},{... | collective-permute-start | bytes 1179656 | tf_op jit(solution)/shard_map/ppermute | solution.py:373
  54.4 15.5 %collective-permute-start.6 = (f32[2,3,128,128]{3,2,1,0:T(8,128)S(1)}, f32[2,3,128,128]{3,2,1,0:T(8,128)S(1)}, u32[]{:S(2)}, u32[]{:S(2)}) collective-permute-start(f32[2,3,128,128]{3,2,1,0:T(8,128)S(1)} %get-tuple-element.44), channel_id=1, source_target_pairs={{0,16},{32,48},{64,80},{96,112},{128,144},{160,176},{192,208},{224... | collective-permute-start | bytes 1179656 | tf_op jit(solution)/shard_map/ppermute | solution.py:373
  60.6 14.5 %collective-permute-start.7 = (f32[2,3,128,128]{3,2,1,0:T(8,128)S(1)}, f32[2,3,128,128]{3,2,1,0:T(8,128)S(1)}, u32[]{:S(2)}, u32[]{:S(2)}) collective-permute-start(f32[2,3,128,128]{3,2,1,0:T(8,128)S(1)} %get-tuple-element.45), channel_id=1, source_target_pairs={{16,32},{48,64},{80,96},{112,128},{144,160},{176,192},{208,224},{3... | collective-permute-start | bytes 1179656 | tf_op jit(solution)/shard_map/ppermute | solution.py:373
  75.8 5.0 %collective-permute-start.8 = (f32[3,256,128]{2,1,0:T(8,128)S(1)}, f32[3,256,128]{2,1,0:T(8,128)S(1)}, u32[]{:S(2)}, u32[]{:S(2)}) collective-permute-start(f32[3,256,128]{2,1,0:T(8,128)S(1)} %get-tuple-element.46.first.mid_1), channel_id=1, source_target_pairs={{0,1},{2,3},{4,5},{6,7},{8,9},{10,11},{12,13},{14,15},{1,0},{3,2},... | collective-permute-start | bytes 1179656 | tf_op jit(solution)/shard_map/ppermute | solution.py:373
  75.9 15.2 %collective-permute-start.9 = (f32[3,256,128]{2,1,0:T(8,128)S(1)}, f32[3,256,128]{2,1,0:T(8,128)S(1)}, u32[]{:S(2)}, u32[]{:S(2)}) collective-permute-start(f32[3,256,128]{2,1,0:T(8,128)S(1)} %get-tuple-element.47.second.mid_2), channel_id=1, source_target_pairs={{1,2},{3,4},{5,6},{7,8},{9,10},{11,12},{13,14},{2,1},{4,3},{6,5},{... | collective-permute-start | bytes 1179656 | tf_op jit(solution)/shard_map/ppermute | solution.py:373
  98.9 4.8 %collective-permute-start.10 = (f32[3,256,128]{2,1,0:T(8,128)S(1)}, f32[3,256,128]{2,1,0:T(8,128)S(1)}, u32[]{:S(2)}, u32[]{:S(2)}) collective-permute-start(f32[3,256,128]{2,1,0:T(8,128)S(1)} %get-tuple-element.50), channel_id=1, source_target_pairs={{0,1},{2,3},{4,5},{6,7},{8,9},{10,11},{12,13},{14,15},{1,0},{3,2},... | collective-permute-start | bytes 1179656 | tf_op jit(solution)/shard_map/ppermute | solution.py:373
  99.0 15.2 %collective-permute-start.11 = (f32[3,256,128]{2,1,0:T(8,128)S(1)}, f32[3,256,128]{2,1,0:T(8,128)S(1)}, u32[]{:S(2)}, u32[]{:S(2)}) collective-permute-start(f32[3,256,128]{2,1,0:T(8,128)S(1)} %get-tuple-element.51), channel_id=1, source_target_pairs={{1,2},{3,4},{5,6},{7,8},{9,10},{11,12},{13,14},{2,1},{4,3},{6,5},{... | collective-permute-start | bytes 1179656 | tf_op jit(solution)/shard_map/ppermute | solution.py:373
  114.8 11.1 %collective-permute-start.12 = (f32[2,3,64,128]{3,2,1,0:T(8,128)S(1)}, f32[2,3,64,128]{3,2,1,0:T(8,128)S(1)}, u32[]{:S(2)}, u32[]{:S(2)}) collective-permute-start(f32[2,3,64,128]{3,2,1,0:T(8,128)S(1)} %get-tuple-element.53), channel_id=1, source_target_pairs={{0,16},{32,48},{64,80},{96,112},{128,144},{160,176},{192,208},{224... | collective-permute-start | bytes 589832 | tf_op jit(solution)/shard_map/ppermute | solution.py:373
  122.2 10.2 %collective-permute-start.13 = (f32[2,3,64,128]{3,2,1,0:T(8,128)S(1)}, f32[2,3,64,128]{3,2,1,0:T(8,128)S(1)}, u32[]{:S(2)}, u32[]{:S(2)}) collective-permute-start(f32[2,3,64,128]{3,2,1,0:T(8,128)S(1)} %get-tuple-element.54), channel_id=1, source_target_pairs={{16,32},{48,64},{80,96},{112,128},{144,160},{176,192},{208,224},{3... | collective-permute-start | bytes 589832 | tf_op jit(solution)/shard_map/ppermute | solution.py:373

commit v4 on v3

--- a/solution.py
+++ b/solution.py
@@ -1,3 +1,4 @@
+import functools
 import math
 
 import jax
@@ -7,7 +8,6 @@
 from jax.experimental import pallas as pl
 from jax.experimental.pallas import tpu as pltpu
 from jax.sharding import PartitionSpec as P
-
 
 MARGIN = 64
 CORE = 128
@@ -123,6 +123,10 @@
     return backward(tables, out)
 
 
+def even_row():
+    return lax.rem(lax.axis_index("ty"), 2) == 0
+
+
 def low_lanes(shape):
     return lax.broadcasted_iota(jnp.int32, shape, len(shape) - 1) < MARGIN
 
@@ -131,8 +135,8 @@
     return pltpu.roll(value, MARGIN, 1)
 
 
-def near_lanes(par, rows):
-    return low_lanes((rows, CORE)) != (par[1] == 0)
+def near_lanes(rows):
+    return low_lanes((rows, CORE)) != (lax.rem(lax.axis_index("tx"), 2) == 0)
 
 
 def pack(nearby, real, imag):
@@ -145,7 +149,6 @@
 
 
 def step_kernel(
-    par,
     first,
     second,
     near,
@@ -161,14 +164,13 @@
     tile,
     field,
 ):
-    nearby = near_lanes(par, TILE)
+    nearby = near_lanes(TILE)
+
     for layer in range(SLICES):
-        real, imag = unpack(nearby, first[layer], second[layer])
-        tile[layer, 0, :, :CORE] = real
-        tile[layer, 1, :, :CORE] = imag
-        real, imag = unpack(nearby, far[layer], near[layer])
-        tile[layer, 0, :, CORE:] = real
-        tile[layer, 1, :, CORE:] = imag
+        core = unpack(nearby, first[layer], second[layer])
+        margin = unpack(nearby, far[layer], near[layer])
+        for c in range(2):
+            tile[layer, c] = beside(core[c], margin[c])
     f_real, f_imag = lit[0], lit[1]
     for layer in range(SLICES - 1):
         t_real, t_imag = tile[layer, 0], tile[layer, 1]
@@ -205,7 +207,7 @@
             )
 
 
-def call(body, outs, scratch=(), smem=1, count=0, limit=8):
+def call(body, outs, scratch=(), smem=0, count=0, limit=8):
     return pl.pallas_call(
         body,
         out_shape=[jax.ShapeDtypeStruct(shape, jnp.float32) for shape in outs],
@@ -214,6 +216,7 @@
         out_specs=[pl.BlockSpec(memory_space=pltpu.VMEM)] * len(outs),
         scratch_shapes=list(scratch),
         compiler_params=pltpu.CompilerParams(vmem_limit_bytes=limit << 20),
+        name=body.__name__,
     )
 
 
@@ -261,12 +264,12 @@
 
 def setup(positions, probe, phase, patterns, order):
     shapes = ((2, TILE, TILE), (TILE, TILE), (TILE, TILE))
-    return call(setup_kernel, shapes, count=4)(positions, probe, phase, patterns, order)
-
-
-def open_kernel(par, core, first, second, near, far):
-    even = par[0] == 0
-    nearby = near_lanes(par, CORE)
+    return call(setup_kernel, shapes, smem=1, count=4)(positions, probe, phase, patterns, order)
+
+
+def open_kernel(core, first, second, near, far):
+    even = even_row()
+    nearby = near_lanes(CORE)
     for layer in range(SLICES):
         packs = pack(nearby, core[layer, 0], core[layer, 1])
         for k, (value, whole) in enumerate(zip(packs, (first, second))):
@@ -275,12 +278,12 @@
             far[k, layer] = jnp.where(even, value[:MARGIN], value[MARGIN:])
 
 
-def begin(par, core):
-    return call(open_kernel, (HALF, HALF, RIMS, RIMS), count=1)(par, core)
-
-
-def assemble_kernel(par, core_1, core_2, near, far, first, second):
-    even = par[0] == 0
+def begin(core):
+    return call(open_kernel, (HALF, HALF, RIMS, RIMS), count=1)(core)
+
+
+def assemble_kernel(core_1, core_2, near, far, first, second):
+    even = even_row()
     for k, (core, mid) in enumerate(((core_1, first), (core_2, second))):
         for layer in range(SLICES):
             mid[layer, :CORE] = core[layer]
@@ -292,8 +295,8 @@
     return call(assemble_kernel, (PACK, PACK), count=4)(*args)
 
 
-def share_kernel(par, part_1, part_2, came_1, came_2, total, send_near, send_far):
-    even = par[0] == 0
+def share_kernel(part_1, part_2, came_1, came_2, total, send_near, send_far):
+    even = even_row()
     for k, (part, came) in enumerate(((part_1, came_1), (part_2, came_2))):
         for layer in range(SLICES):
             value = part[layer] + came[layer]
@@ -309,10 +312,11 @@
     return call(share_kernel, ((2, *PACK), (2, *HALF), (2, *HALF)), count=4)(*args)
 
 
-def update_kernel(par, mid_1, mid_2, total, near, far, new_1, new_2):
-    even = par[0] == 0
-    above = jnp.where(par[2] == 0, 0.0, STEP_SIZE)
-    below = jnp.where(par[3] == 0, 0.0, STEP_SIZE)
+def update_kernel(mid_1, mid_2, total, near, far, new_1, new_2):
+    even = even_row()
+    row = lax.axis_index("ty")
+    above = jnp.where(row == 0, 0.0, STEP_SIZE)
+    below = jnp.where(row == lax.axis_size("ty") - 1, 0.0, STEP_SIZE)
     for k, (mid, new) in enumerate(((mid_1, new_1), (mid_2, new_2))):
         for layer in range(SLICES):
             e, o = near[k, layer], far[k, layer]
@@ -334,8 +338,8 @@
     return call(update_kernel, (PACK, PACK), count=5)(*args)
 
 
-def close_kernel(par, part_1, part_2, came_1, came_2, total, send_near, send_far):
-    even = par[0] == 0
+def close_kernel(part_1, part_2, came_1, came_2, total, send_near, send_far):
+    even = even_row()
     for k, (part, came) in enumerate(((part_1, came_1), (part_2, came_2))):
         for layer in range(SLICES):
             value = part[layer] + came[layer]
@@ -349,9 +353,9 @@
     return call(close_kernel, ((2, *HALF), RIMS, RIMS), count=4)(*args)
 
 
-def finish_kernel(par, mid_1, mid_2, total, near, far, out):
-    even = par[0] == 0
-    nearby = near_lanes(par, MARGIN)
+def finish_kernel(mid_1, mid_2, total, near, far, out):
+    even = even_row()
+    nearby = near_lanes(MARGIN)
     for layer in range(SLICES):
         for half in range(2):
             rows = pl.ds(half * MARGIN, MARGIN)
@@ -375,36 +379,33 @@
 
 def swap_rows(near, far):
     far = swap("ty", 1, far)
-    near = swap("ty", 0, near)
-    return near, far
-
-
-def exchange_and_step(object_field, probe, propagator_phase, patterns, scan_positions):
-    row, col = lax.axis_index("ty"), lax.axis_index("tx")
-    par = jnp.stack([row % 2, col % 2, row, lax.axis_size("ty") - 1 - row]).astype(jnp.int32)
-    first, second, near, far = begin(par, object_field)
+    return swap("ty", 0, near), far
+
+
+def shards(object_field, probe, propagator_phase, patterns, scan_positions):
+    first, second, near, far = begin(object_field)
     near, far = swap_rows(near, far)
     lit, phase, ordered = setup(
         scan_positions[0, 0, 0], probe, propagator_phase, patterns[0, 0, 0], order_table()
     )
     wave = jnp.stack([jnp.cos(phase), jnp.sin(phase)])
     tables = jnp.asarray(half_tables())
-    first, second = assemble(par, first, second, near, far)
+    first, second = assemble(first, second, near, far)
     for turn in range(STEPS):
         far = swap("tx", 1, second)
         near = swap("tx", 0, first)
         part_1, part_2, near, far = step(
-            par, first, second, near, far, lit, wave, ordered, tables
+            first, second, near, far, lit, wave, ordered, tables
         )
         far = swap("tx", 1, far)
         near = swap("tx", 0, near)
         if turn < STEPS - 1:
-            total, near, far = share(par, part_1, part_2, near, far)
+            total, near, far = share(part_1, part_2, near, far)
             near, far = swap_rows(near, far)
-            first, second = update(par, first, second, total, near, far)
-    total, near, far = close(par, part_1, part_2, near, far)
+            first, second = update(first, second, total, near, far)
+    total, near, far = close(part_1, part_2, near, far)
     near, far = swap_rows(near, far)
-    return finish(par, first, second, total, near, far)
+    return finish(first, second, total, near, far)
 
 
 def solution(mesh):
@@ -416,5 +417,5 @@
         P("ty", "tx", None, None),
     )
     return jax.shard_map(
-        exchange_and_step, mesh=mesh, in_specs=placed, out_specs=P(None, None, "ty", "tx"), check_vma=False
+        shards, mesh=mesh, in_specs=placed, out_specs=P(None, None, "ty", "tx"), check_vma=False
     )

time: 135 us -> 131 us (0.970)
  Pallas kernels: 21.6 us -> 17.2 us
where the time goes in v4:
time: 131 us; the launch traced here: 130 us
  waiting for transfers between devices  62 us (47%)
  starting transfers between devices  46.9 us (36%)
  Pallas kernels  17.2 us (13%)
  local copies, waits for them, and re-layouts  3.55 us (3%)
    ppermute x14, waiting for transfers between devices, swap(): return lax.ppermute(block, axis, pairs + [(j, i) for i, j in pairs])  62 us
    ppermute x14, starting transfers between devices, swap(): return lax.ppermute(block, axis, pairs + [(j, i) for i, j in pairs])  46.9 us
    pallas_call x2, Pallas kernels, step(): call(step_kernel, (PACK, PACK, PACK, PACK), (pltpu.VMEM((SLICES, 2, TILE,...  14.4 us
  transfers between devices with their start and end apart: 14, of which 10 were waited for; matrix products, arithmetic and copies ran while one was open for 1% of the time, Pallas kernels for 1%

profile of v4, /device:TPU:232, one launch (start us, length us, event | category | flops | bytes accessed | tf_op | source)
XLA Modules:
  0.0 129.9 jit_solution(12815392654456672940)
XLA Ops:
  0.0 0.0 copy-start.2
  0.0 1.0 copy-done.2
  1.0 0.0 copy-start.1
  1.0 0.1 open_kernel.1
  1.1 1.1 collective-permute-start
  2.2 4.8 %collective-permute-start.1 = (f32[2,3,64,128]{3,2,1,0:T(8,128)S(1)}, f32[2,3,64,128]{3,2,1,0:T(8,128)S(1)}, u32[]{:S(2)}, u32[]{:S(2)}) collective-permute-start(f32[2,3,64,128]{3,2,1,0:T(8,128)S(1)} %get-tuple-element.33), channel_id=1, source_target_pairs={{16,32},{48,64},{80,96},{112,128},{144,160},{176,192},{208,224},{3... | collective-permute-start | bytes 589832 | tf_op jit(solution)/shard_map/ppermute | solution.py:377
  7.0 0.8 collective-permute-done.near
  7.9 6.2 %collective-permute-done.1.far = f32[2,3,64,128]{3,2,1,0:T(8,128)S(1)} collective-permute-done((f32[2,3,64,128]{3,2,1,0:T(8,128)S(1)}, f32[2,3,64,128]{3,2,1,0:T(8,128)S(1)}, u32[]{:S(2)}, u32[]{:S(2)}) %collective-permute-start.1) | collective-permute-done | bytes 196640 | tf_op jit(solution)/shard_map/ppermute | solution.py:377
  14.1 0.0 copy-start.3
  14.1 0.0 copy-start.4
  14.1 0.1 assemble_kernel.1
  14.1 0.1 collective-permute-start.2
  14.2 4.1 %collective-permute-start.3 = (f32[3,256,128]{2,1,0:T(8,128)S(1)}, f32[3,256,128]{2,1,0:T(8,128)S(1)}, u32[]{:S(2)}, u32[]{:S(2)}) collective-permute-start(f32[3,256,128]{2,1,0:T(8,128)S(1)} %get-tuple-element.35.second.mid_2), channel_id=1, source_target_pairs={{1,2},{3,4},{5,6},{7,8},{9,10},{11,12},{13,14},{2,1},{4,3},{6,5},{... | collective-permute-start | bytes 1179656 | tf_op jit(solution)/shard_map/ppermute | solution.py:377
  18.4 0.0 copy-start.6
  18.4 0.0 copy-done.1
  18.4 0.0 copy-done.3
  18.4 0.0 copy-done.4
  18.4 0.6 copy-done.6
  19.0 0.0 copy-start.5
  19.0 0.9 copy-done.5
  20.0 1.4 %setup_kernel.1 = (f32[2,256,256]{2,1,0:T(8,128)S(1)}, f32[256,256]{1,0:T(8,128)S(1)}, f32[256,256]{1,0:T(8,128)S(1)}) custom-call(s32[2]{0:T(128)S(1)} %bitcast.7, f32[2,256,256]{2,1,0:T(8,128)S(1)} %copy-done.1, f32[256,256]{1,0:T(8,128)S(1)} %copy-done.3, f32[256,256]{1,0:T(8,128)S(1)} %bitcast.6, bf16[2,256,256]{2,1,0:T(8,128)(2,1)S(1)} %copy-done.5), custom_call_target="tpu_custom_call" | custom-call | tf_op jit(solution)/shard_map/setup_kernel/pallas_call | solution.py:267
  21.4 0.0 copy-start
  21.4 1.0 cosine_bitcast_fusion
  22.4 0.0 collective-permute-done.2.near
  22.4 7.0 %collective-permute-done.3.far = f32[3,256,128]{2,1,0:T(8,128)S(1)} collective-permute-done((f32[3,256,128]{2,1,0:T(8,128)S(1)}, f32[3,256,128]{2,1,0:T(8,128)S(1)}, u32[]{:S(2)}, u32[]{:S(2)}) %collective-permute-start.3) | collective-permute-done | bytes 393248 | tf_op jit(solution)/shard_map/ppermute | solution.py:377
  29.5 0.0 copy-done
  29.5 7.2 %step_kernel.2 = (f32[3,256,128]{2,1,0:T(8,128)S(1)}, f32[3,256,128]{2,1,0:T(8,128)S(1)}, f32[3,256,128]{2,1,0:T(8,128)S(1)}, f32[3,256,128]{2,1,0:T(8,128)S(1)}) custom-call(f32[3,256,128]{2,1,0:T(8,128)S(1)} %get-tuple-element.34.first.mid_1, f32[3,256,128]{2,1,0:T(8,128)S(1)} %get-tuple-element.35.second.mid_2, ...), custom_call_target="tpu_custom_call" | custom-call | tf_op jit(solution)/shard_map/step_kernel/pallas_call | solution.py:229
  36.7 0.1 collective-permute-start.4
  36.8 4.1 %collective-permute-start.5 = (f32[3,256,128]{2,1,0:T(8,128)S(1)}, f32[3,256,128]{2,1,0:T(8,128)S(1)}, u32[]{:S(2)}, u32[]{:S(2)}) collective-permute-start(f32[3,256,128]{2,1,0:T(8,128)S(1)} %get-tuple-element.42), channel_id=1, source_target_pairs={{1,2},{3,4},{5,6},{7,8},{9,10},{11,12},{13,14},{2,1},{4,3},{6,5},{... | collective-permute-start | bytes 1179656 | tf_op jit(solution)/shard_map/ppermute | solution.py:377
  40.9 0.0 collective-permute-done.4.came_1
  40.9 11.0 %collective-permute-done.5.came_2 = f32[3,256,128]{2,1,0:T(8,128)S(1)} collective-permute-done((f32[3,256,128]{2,1,0:T(8,128)S(1)}, f32[3,256,128]{2,1,0:T(8,128)S(1)}, u32[]{:S(2)}, u32[]{:S(2)}) %collective-permute-start.5) | collective-permute-done | bytes 393248 | tf_op jit(solution)/shard_map/ppermute | solution.py:377
  51.9 0.1 share_kernel.1
  52.0 6.8 %collective-permute-start.6 = (f32[2,3,128,128]{3,2,1,0:T(8,128)S(1)}, f32[2,3,128,128]{3,2,1,0:T(8,128)S(1)}, u32[]{:S(2)}, u32[]{:S(2)}) collective-permute-start(f32[2,3,128,128]{3,2,1,0:T(8,128)S(1)} %get-tuple-element.44), channel_id=1, source_target_pairs={{0,16},{32,48},{64,80},{96,112},{128,144},{160,176},{192,208},{224... | collective-permute-start | bytes 1179656 | tf_op jit(solution)/shard_map/ppermute | solution.py:377
  58.8 5.5 %collective-permute-start.7 = (f32[2,3,128,128]{3,2,1,0:T(8,128)S(1)}, f32[2,3,128,128]{3,2,1,0:T(8,128)S(1)}, u32[]{:S(2)}, u32[]{:S(2)}) collective-permute-start(f32[2,3,128,128]{3,2,1,0:T(8,128)S(1)} %get-tuple-element.45), channel_id=1, source_target_pairs={{16,32},{48,64},{80,96},{112,128},{144,160},{176,192},{208,224},{3... | collective-permute-start | bytes 1179656 | tf_op jit(solution)/shard_map/ppermute | solution.py:377
  64.3 3.2 %collective-permute-done.6.near = f32[2,3,128,128]{3,2,1,0:T(8,128)S(1)} collective-permute-done((f32[2,3,128,128]{3,2,1,0:T(8,128)S(1)}, f32[2,3,128,128]{3,2,1,0:T(8,128)S(1)}, u32[]{:S(2)}, u32[]{:S(2)}) %collective-permute-start.6) | collective-permute-done | bytes 393248 | tf_op jit(solution)/shard_map/ppermute | solution.py:377
  67.5 5.3 %collective-permute-done.7.far = f32[2,3,128,128]{3,2,1,0:T(8,128)S(1)} collective-permute-done((f32[2,3,128,128]{3,2,1,0:T(8,128)S(1)}, f32[2,3,128,128]{3,2,1,0:T(8,128)S(1)}, u32[]{:S(2)}, u32[]{:S(2)}) %collective-permute-start.7) | collective-permute-done | bytes 393248 | tf_op jit(solution)/shard_map/ppermute | solution.py:377
  72.8 0.1 update_kernel.1
  72.9 0.1 collective-permute-start.8
  73.0 4.9 %collective-permute-start.9 = (f32[3,256,128]{2,1,0:T(8,128)S(1)}, f32[3,256,128]{2,1,0:T(8,128)S(1)}, u32[]{:S(2)}, u32[]{:S(2)}) collective-permute-start(f32[3,256,128]{2,1,0:T(8,128)S(1)} %get-tuple-element.47.second.mid_2), channel_id=1, source_target_pairs={{1,2},{3,4},{5,6},{7,8},{9,10},{11,12},{13,14},{2,1},{4,3},{6,5},{... | collective-permute-start | bytes 1179656 | tf_op jit(solution)/shard_map/ppermute | solution.py:377
  77.9 0.0 collective-permute-done.8.near
  77.9 10.3 %collective-permute-done.9.far = f32[3,256,128]{2,1,0:T(8,128)S(1)} collective-permute-done((f32[3,256,128]{2,1,0:T(8,128)S(1)}, f32[3,256,128]{2,1,0:T(8,128)S(1)}, u32[]{:S(2)}, u32[]{:S(2)}) %collective-permute-start.9) | collective-permute-done | bytes 393248 | tf_op jit(solution)/shard_map/ppermute | solution.py:377
  88.2 7.2 %step_kernel.3 = (f32[3,256,128]{2,1,0:T(8,128)S(1)}, f32[3,256,128]{2,1,0:T(8,128)S(1)}, f32[3,256,128]{2,1,0:T(8,128)S(1)}, f32[3,256,128]{2,1,0:T(8,128)S(1)}) custom-call(f32[3,256,128]{2,1,0:T(8,128)S(1)} %get-tuple-element.46.first.mid_1, f32[3,256,128]{2,1,0:T(8,128)S(1)} %get-tuple-element.47.second.mid_2, ...), custom_call_target="tpu_custom_call" | custom-call | tf_op jit(solution)/shard_map/step_kernel/pallas_call | solution.py:229
  95.4 0.1 collective-permute-start.10
  95.5 4.7 %collective-permute-start.11 = (f32[3,256,128]{2,1,0:T(8,128)S(1)}, f32[3,256,128]{2,1,0:T(8,128)S(1)}, u32[]{:S(2)}, u32[]{:S(2)}) collective-permute-start(f32[3,256,128]{2,1,0:T(8,128)S(1)} %get-tuple-element.51), channel_id=1, source_target_pairs={{1,2},{3,4},{5,6},{7,8},{9,10},{11,12},{13,14},{2,1},{4,3},{6,5},{... | collective-permute-start | bytes 1179656 | tf_op jit(solution)/shard_map/ppermute | solution.py:377
  100.2 0.0 collective-permute-done.10.came_1
  100.2 10.5 %collective-permute-done.11.came_2 = f32[3,256,128]{2,1,0:T(8,128)S(1)} collective-permute-done((f32[3,256,128]{2,1,0:T(8,128)S(1)}, f32[3,256,128]{2,1,0:T(8,128)S(1)}, u32[]{:S(2)}, u32[]{:S(2)}) %collective-permute-start.11) | collective-permute-done | bytes 393248 | tf_op jit(solution)/shard_map/ppermute | solution.py:377
  110.7 0.1 close_kernel.1
  110.8 8.0 %collective-permute-start.12 = (f32[2,3,64,128]{3,2,1,0:T(8,128)S(1)}, f32[2,3,64,128]{3,2,1,0:T(8,128)S(1)}, u32[]{:S(2)}, u32[]{:S(2)}) collective-permute-start(f32[2,3,64,128]{3,2,1,0:T(8,128)S(1)} %get-tuple-element.53), channel_id=1, source_target_pairs={{0,16},{32,48},{64,80},{96,112},{128,144},{160,176},{192,208},{224... | collective-permute-start | bytes 589832 | tf_op jit(solution)/shard_map/ppermute | solution.py:377
  118.8 2.6 %collective-permute-start.13 = (f32[2,3,64,128]{3,2,1,0:T(8,128)S(1)}, f32[2,3,64,128]{3,2,1,0:T(8,128)S(1)}, u32[]{:S(2)}, u32[]{:S(2)}) collective-permute-start(f32[2,3,64,128]{3,2,1,0:T(8,128)S(1)} %get-tuple-element.54), channel_id=1, source_target_pairs={{16,32},{48,64},{80,96},{112,128},{144,160},{176,192},{208,224},{3... | collective-permute-start | bytes 589832 | tf_op jit(solution)/shard_map/ppermute | solution.py:377
  121.4 1.0 collective-permute-done.12.near
  122.4 6.6 %collective-permute-done.13.far = f32[2,3,64,128]{3,2,1,0:T(8,128)S(1)} collective-permute-done((f32[2,3,64,128]{3,2,1,0:T(8,128)S(1)}, f32[2,3,64,128]{3,2,1,0:T(8,128)S(1)}, u32[]{:S(2)}, u32[]{:S(2)}) %collective-permute-start.13) | collective-permute-done | bytes 196640 | tf_op jit(solution)/shard_map/ppermute | solution.py:377
  129.0 0.9 finish_kernel.1
  (1 shorter events, 0.0 us)
Async XLA Ops:
  0.0 1.0 copy-start.2
  1.0 17.4 %copy-start.1 = (f32[2,256,256]{2,1,0:T(8,128)S(1)}, f32[2,256,256]{2,1,0:T(8,128)}, u32[]{:S(2)}) copy-start(f32[2,256,256]{2,1,0:T(8,128)} %probe.1) | copy-start | bytes 1572868
  1.1 6.7 %collective-permute-start = (f32[2,3,64,128]{3,2,1,0:T(8,128)S(1)}, f32[2,3,64,128]{3,2,1,0:T(8,128)S(1)}, u32[]{:S(2)}, u32[]{:S(2)}) collective-permute-start(f32[2,3,64,128]{3,2,1,0:T(8,128)S(1)} %get-tuple-element.32), channel_id=1, source_target_pairs={{0,16},{32,48},{64,80},{96,112},{128,144},{160,176},{192,208},{224... | collective-permute-start | bytes 589832 | tf_op jit(solution)/shard_map/ppermute | solution.py:377
  2.2 11.8 %collective-permute-start.1 = (f32[2,3,64,128]{3,2,1,0:T(8,128)S(1)}, f32[2,3,64,128]{3,2,1,0:T(8,128)S(1)}, u32[]{:S(2)}, u32[]{:S(2)}) collective-permute-start(f32[2,3,64,128]{3,2,1,0:T(8,128)S(1)} %get-tuple-element.33), channel_id=1, source_target_pairs={{16,32},{48,64},{80,96},{112,128},{144,160},{176,192},{208,224},{3... | collective-permute-start | bytes 589832 | tf_op jit(solution)/shard_map/ppermute | solution.py:377
  14.1 4.3 %copy-start.3 = (f32[256,256]{1,0:T(8,128)S(1)}, f32[256,256]{1,0:T(8,128)}, u32[]{:S(2)}) copy-start(f32[256,256]{1,0:T(8,128)} %phase.1) | copy-start | bytes 786436
  14.1 4.3 %copy-start.4 = (f32[1,1,1,256,256]{4,3,2,1,0:T(8,128)S(1)}, f32[1,1,1,256,256]{4,3,2,1,0:T(8,128)}, u32[]{:S(2)}) copy-start(f32[1,1,1,256,256]{4,3,2,1,0:T(8,128)} %param.10) | copy-start | bytes 786436
  14.1 8.3 %collective-permute-start.2 = (f32[3,256,128]{2,1,0:T(8,128)S(1)}, f32[3,256,128]{2,1,0:T(8,128)S(1)}, u32[]{:S(2)}, u32[]{:S(2)}) collective-permute-start(f32[3,256,128]{2,1,0:T(8,128)S(1)} %get-tuple-element.34.first.mid_1), channel_id=1, source_target_pairs={{0,1},{2,3},{4,5},{6,7},{8,9},{10,11},{12,13},{14,15},{1,0},{3,2},... | collective-permute-start | bytes 1179656 | tf_op jit(solution)/shard_map/ppermute | solution.py:377
  14.2 15.2 %collective-permute-start.3 = (f32[3,256,128]{2,1,0:T(8,128)S(1)}, f32[3,256,128]{2,1,0:T(8,128)S(1)}, u32[]{:S(2)}, u32[]{:S(2)}) collective-permute-start(f32[3,256,128]{2,1,0:T(8,128)S(1)} %get-tuple-element.35.second.mid_2), channel_id=1, source_target_pairs={{1,2},{3,4},{5,6},{7,8},{9,10},{11,12},{13,14},{2,1},{4,3},{6,5},{... | collective-permute-start | bytes 1179656 | tf_op jit(solution)/shard_map/ppermute | solution.py:377
  18.4 0.7 copy-start.6
  19.0 0.9 copy-start.5
  21.4 8.1 %copy-start = (bf16[4,2,256,256]{3,2,1,0:T(8,128)(2,1)S(1)}, bf16[4,2,256,256]{3,2,1,0:T(8,128)(2,1)}, u32[]{:S(2)}) copy-start(bf16[4,2,256,256]{3,2,1,0:T(8,128)(2,1)} %constant.5.clone.tables) | copy-start | bytes 3145732
  36.7 4.2 %collective-permute-start.4 = (f32[3,256,128]{2,1,0:T(8,128)S(1)}, f32[3,256,128]{2,1,0:T(8,128)S(1)}, u32[]{:S(2)}, u32[]{:S(2)}) collective-permute-start(f32[3,256,128]{2,1,0:T(8,128)S(1)} %get-tuple-element.41), channel_id=1, source_target_pairs={{0,1},{2,3},{4,5},{6,7},{8,9},{10,11},{12,13},{14,15},{1,0},{3,2},... | collective-permute-start | bytes 1179656 | tf_op jit(solution)/shard_map/ppermute | solution.py:377
  36.8 15.2 %collective-permute-start.5 = (f32[3,256,128]{2,1,0:T(8,128)S(1)}, f32[3,256,128]{2,1,0:T(8,128)S(1)}, u32[]{:S(2)}, u32[]{:S(2)}) collective-permute-start(f32[3,256,128]{2,1,0:T(8,128)S(1)} %get-tuple-element.42), channel_id=1, source_target_pairs={{1,2},{3,4},{5,6},{7,8},{9,10},{11,12},{13,14},{2,1},{4,3},{6,5},{... | collective-permute-start | bytes 1179656 | tf_op jit(solution)/shard_map/ppermute | solution.py:377
  52.0 15.5 %collective-permute-start.6 = (f32[2,3,128,128]{3,2,1,0:T(8,128)S(1)}, f32[2,3,128,128]{3,2,1,0:T(8,128)S(1)}, u32[]{:S(2)}, u32[]{:S(2)}) collective-permute-start(f32[2,3,128,128]{3,2,1,0:T(8,128)S(1)} %get-tuple-element.44), channel_id=1, source_target_pairs={{0,16},{32,48},{64,80},{96,112},{128,144},{160,176},{192,208},{224... | collective-permute-start | bytes 1179656 | tf_op jit(solution)/shard_map/ppermute | solution.py:377
  58.8 14.0 %collective-permute-start.7 = (f32[2,3,128,128]{3,2,1,0:T(8,128)S(1)}, f32[2,3,128,128]{3,2,1,0:T(8,128)S(1)}, u32[]{:S(2)}, u32[]{:S(2)}) collective-permute-start(f32[2,3,128,128]{3,2,1,0:T(8,128)S(1)} %get-tuple-element.45), channel_id=1, source_target_pairs={{16,32},{48,64},{80,96},{112,128},{144,160},{176,192},{208,224},{3... | collective-permute-start | bytes 1179656 | tf_op jit(solution)/shard_map/ppermute | solution.py:377
  72.9 5.0 %collective-permute-start.8 = (f32[3,256,128]{2,1,0:T(8,128)S(1)}, f32[3,256,128]{2,1,0:T(8,128)S(1)}, u32[]{:S(2)}, u32[]{:S(2)}) collective-permute-start(f32[3,256,128]{2,1,0:T(8,128)S(1)} %get-tuple-element.46.first.mid_1), channel_id=1, source_target_pairs={{0,1},{2,3},{4,5},{6,7},{8,9},{10,11},{12,13},{14,15},{1,0},{3,2},... | collective-permute-start | bytes 1179656 | tf_op jit(solution)/shard_map/ppermute | solution.py:377
  73.0 15.2 %collective-permute-start.9 = (f32[3,256,128]{2,1,0:T(8,128)S(1)}, f32[3,256,128]{2,1,0:T(8,128)S(1)}, u32[]{:S(2)}, u32[]{:S(2)}) collective-permute-start(f32[3,256,128]{2,1,0:T(8,128)S(1)} %get-tuple-element.47.second.mid_2), channel_id=1, source_target_pairs={{1,2},{3,4},{5,6},{7,8},{9,10},{11,12},{13,14},{2,1},{4,3},{6,5},{... | collective-permute-start | bytes 1179656 | tf_op jit(solution)/shard_map/ppermute | solution.py:377
  95.4 4.8 %collective-permute-start.10 = (f32[3,256,128]{2,1,0:T(8,128)S(1)}, f32[3,256,128]{2,1,0:T(8,128)S(1)}, u32[]{:S(2)}, u32[]{:S(2)}) collective-permute-start(f32[3,256,128]{2,1,0:T(8,128)S(1)} %get-tuple-element.50), channel_id=1, source_target_pairs={{0,1},{2,3},{4,5},{6,7},{8,9},{10,11},{12,13},{14,15},{1,0},{3,2},... | collective-permute-start | bytes 1179656 | tf_op jit(solution)/shard_map/ppermute | solution.py:377
  95.5 15.2 %collective-permute-start.11 = (f32[3,256,128]{2,1,0:T(8,128)S(1)}, f32[3,256,128]{2,1,0:T(8,128)S(1)}, u32[]{:S(2)}, u32[]{:S(2)}) collective-permute-start(f32[3,256,128]{2,1,0:T(8,128)S(1)} %get-tuple-element.51), channel_id=1, source_target_pairs={{1,2},{3,4},{5,6},{7,8},{9,10},{11,12},{13,14},{2,1},{4,3},{6,5},{... | collective-permute-start | bytes 1179656 | tf_op jit(solution)/shard_map/ppermute | solution.py:377
  110.8 11.6 %collective-permute-start.12 = (f32[2,3,64,128]{3,2,1,0:T(8,128)S(1)}, f32[2,3,64,128]{3,2,1,0:T(8,128)S(1)}, u32[]{:S(2)}, u32[]{:S(2)}) collective-permute-start(f32[2,3,64,128]{3,2,1,0:T(8,128)S(1)} %get-tuple-element.53), channel_id=1, source_target_pairs={{0,16},{32,48},{64,80},{96,112},{128,144},{160,176},{192,208},{224... | collective-permute-start | bytes 589832 | tf_op jit(solution)/shard_map/ppermute | solution.py:377
  118.8 10.2 %collective-permute-start.13 = (f32[2,3,64,128]{3,2,1,0:T(8,128)S(1)}, f32[2,3,64,128]{3,2,1,0:T(8,128)S(1)}, u32[]{:S(2)}, u32[]{:S(2)}) collective-permute-start(f32[2,3,64,128]{3,2,1,0:T(8,128)S(1)} %get-tuple-element.54), channel_id=1, source_target_pairs={{16,32},{48,64},{80,96},{112,128},{144,160},{176,192},{208,224},{3... | collective-permute-start | bytes 589832 | tf_op jit(solution)/shard_map/ppermute | solution.py:377

commit v5 on v4

--- a/solution.py
+++ b/solution.py
@@ -148,27 +148,29 @@
     return jnp.where(nearby, first, second), turned(jnp.where(nearby, second, first))
 
 
-def step_kernel(
-    first,
-    second,
-    near,
-    far,
-    lit,
-    wave,
-    patterns,
-    tables,
-    part_first,
-    part_second,
-    send_near,
-    send_far,
-    tile,
-    field,
-):
+def rows_of(refs, layer):
+    return stack(*(ref[layer] for ref in refs))
+
+
+def put_rows(refs, layer, value):
+    if len(refs) == 1:
+        refs[0][layer] = value
+    else:
+        refs[0][layer] = value[:CORE]
+        refs[1][layer] = value[CORE:]
+
+
+def step_kernel(blocks, cuts, *refs):
+    taken = [refs[k * blocks : (k + 1) * blocks] for k in range(4)]
+    first, second, near, far = taken
+    lit, wave, patterns, tables, part_first, part_second = refs[4 * blocks : 4 * blocks + 6]
+    sends = refs[4 * blocks + 6 : -2]
+    send_near, send_far = sends[:cuts], sends[cuts:]
+    tile, field = refs[-2:]
     nearby = near_lanes(TILE)
-
     for layer in range(SLICES):
-        core = unpack(nearby, first[layer], second[layer])
-        margin = unpack(nearby, far[layer], near[layer])
+        core = unpack(nearby, rows_of(first, layer), rows_of(second, layer))
+        margin = unpack(nearby, rows_of(far, layer), rows_of(near, layer))
         for c in range(2):
             tile[layer, c] = beside(core[c], margin[c])
     f_real, f_imag = lit[0], lit[1]
@@ -195,7 +197,9 @@
         real = f_real * u_real + f_imag * u_imag
         imag = f_real * u_imag - f_imag * u_real
         part_first[layer], part_second[layer] = pack(nearby, real[:, :CORE], imag[:, :CORE])
-        send_far[layer], send_near[layer] = pack(nearby, real[:, CORE:], imag[:, CORE:])
+        far_pack, near_pack = pack(nearby, real[:, CORE:], imag[:, CORE:])
+        put_rows(send_far, layer, far_pack)
+        put_rows(send_near, layer, near_pack)
         if layer > 0:
             t_real, t_imag = tile[layer, 0], tile[layer, 1]
             u_real, u_imag = propagate(
@@ -207,7 +211,7 @@
             )
 
 
-def call(body, outs, scratch=(), smem=0, count=0, limit=8):
+def call(body, outs, scratch=(), smem=0, count=0, limit=8, name=None):
     return pl.pallas_call(
         body,
         out_shape=[jax.ShapeDtypeStruct(shape, jnp.float32) for shape in outs],
@@ -216,7 +220,7 @@
         out_specs=[pl.BlockSpec(memory_space=pltpu.VMEM)] * len(outs),
         scratch_shapes=list(scratch),
         compiler_params=pltpu.CompilerParams(vmem_limit_bytes=limit << 20),
-        name=body.__name__,
+        name=name or body.__name__,
     )
 
 
@@ -225,17 +229,19 @@
 RIMS = (2, SLICES, MARGIN, CORE)
 
 
-def step(*args):
-    return call(
-        step_kernel,
-        (PACK, PACK, PACK, PACK),
+def step(blocks, cuts, *args):
+    out = call(
+        functools.partial(step_kernel, blocks, cuts),
+        (PACK, PACK) + ((PACK,) * 2 if cuts == 1 else (HALF,) * 4),
         (
             pltpu.VMEM((SLICES, 2, TILE, TILE), jnp.float32),
             pltpu.VMEM((SLICES - 1, 2, TILE, TILE), jnp.float32),
         ),
-        count=8,
+        count=4 * blocks + 4,
         limit=24,
+        name="step_kernel",
     )(*args)
+    return out[:2], out[2 : 2 + cuts], out[2 + cuts :]
 
 
 def three(value):
@@ -282,17 +288,16 @@
     return call(open_kernel, (HALF, HALF, RIMS, RIMS), count=1)(core)
 
 
-def assemble_kernel(core_1, core_2, near, far, first, second):
-    even = even_row()
-    for k, (core, mid) in enumerate(((core_1, first), (core_2, second))):
+def margin_kernel(near, far, first, second):
+    even = even_row()
+    for k, margin in enumerate((first, second)):
         for layer in range(SLICES):
-            mid[layer, :CORE] = core[layer]
-            mid[layer, CORE : CORE + MARGIN] = jnp.where(even, near[k, layer], far[k, layer])
-            mid[layer, CORE + MARGIN :] = jnp.where(even, far[k, layer], near[k, layer])
-
-
-def assemble(*args):
-    return call(assemble_kernel, (PACK, PACK), count=4)(*args)
+            margin[layer, :MARGIN] = jnp.where(even, near[k, layer], far[k, layer])
+            margin[layer, MARGIN:] = jnp.where(even, far[k, layer], near[k, layer])
+
+
+def margins(*args):
+    return call(margin_kernel, (HALF, HALF), count=2)(*args)
 
 
 def share_kernel(part_1, part_2, came_1, came_2, total, send_near, send_far):
@@ -312,12 +317,12 @@
     return call(share_kernel, ((2, *PACK), (2, *HALF), (2, *HALF)), count=4)(*args)
 
 
-def update_kernel(mid_1, mid_2, total, near, far, new_1, new_2):
+def update_kernel(core_1, core_2, margin_1, margin_2, total, near, far, new_1, new_2):
     even = even_row()
     row = lax.axis_index("ty")
     above = jnp.where(row == 0, 0.0, STEP_SIZE)
     below = jnp.where(row == lax.axis_size("ty") - 1, 0.0, STEP_SIZE)
-    for k, (mid, new) in enumerate(((mid_1, new_1), (mid_2, new_2))):
+    for k, (mid, new) in enumerate((((core_1, margin_1), new_1), ((core_2, margin_2), new_2))):
         for layer in range(SLICES):
             e, o = near[k, layer], far[k, layer]
             down = jnp.where(even, e, o)
@@ -331,44 +336,47 @@
                 )
             ):
                 rows = pl.ds(n * MARGIN, MARGIN)
-                new[layer, rows] = mid[layer, rows] - scale * (total[k, layer, rows] + added)
+                old = mid[n // 2][layer, pl.ds(n % 2 * MARGIN, MARGIN)]
+                new[layer, rows] = old - scale * (total[k, layer, rows] + added)
 
 
 def update(*args):
-    return call(update_kernel, (PACK, PACK), count=5)(*args)
-
-
-def close_kernel(part_1, part_2, came_1, came_2, total, send_near, send_far):
+    return call(update_kernel, (PACK, PACK), count=7)(*args)
+
+
+def close_kernel(part_1, part_2, came_1, came_2, send_near, send_far):
     even = even_row()
     for k, (part, came) in enumerate(((part_1, came_1), (part_2, came_2))):
         for layer in range(SLICES):
-            value = part[layer] + came[layer]
-            total[k, layer] = value[:CORE]
-            below, above = value[CORE : CORE + MARGIN], value[CORE + MARGIN :]
+            value = part[layer, CORE:] + came[layer]
+            below, above = value[:MARGIN], value[MARGIN:]
             send_near[k, layer] = jnp.where(even, below, above)
             send_far[k, layer] = jnp.where(even, above, below)
 
 
 def close(*args):
-    return call(close_kernel, ((2, *HALF), RIMS, RIMS), count=4)(*args)
-
-
-def finish_kernel(mid_1, mid_2, total, near, far, out):
+    return call(close_kernel, (RIMS, RIMS), count=4)(*args)
+
+
+def finish_kernel(mid_1, mid_2, part_1, part_2, came_1, came_2, near, far, out):
     even = even_row()
     nearby = near_lanes(MARGIN)
     for layer in range(SLICES):
         for half in range(2):
             rows = pl.ds(half * MARGIN, MARGIN)
             packs = []
-            for k, mid in enumerate((mid_1, mid_2)):
+            for k, (mid, part, came) in enumerate(
+                ((mid_1, part_1, came_1), (mid_2, part_2, came_2))
+            ):
                 e, o = near[k, layer], far[k, layer]
                 added = jnp.where(even, o, e) if half == 0 else jnp.where(even, e, o)
-                packs.append(mid[layer, rows] - STEP_SIZE * (total[k, layer, rows] + added))
+                total = part[layer, rows] + came[layer, rows]
+                packs.append(mid[layer, rows] - STEP_SIZE * (total + added))
             out[layer, 0, rows], out[layer, 1, rows] = unpack(nearby, *packs)
 
 
 def finish(*args):
-    return call(finish_kernel, ((SLICES, 2, CORE, CORE),), count=5)(*args)[0]
+    return call(finish_kernel, ((SLICES, 2, CORE, CORE),), count=8)(*args)[0]
 
 
 def swap(axis, first, block):
@@ -382,30 +390,38 @@
     return swap("ty", 0, near), far
 
 
+def swap_cols(near, far):
+    far = swap("tx", 1, far)
+    near = swap("tx", 0, near)
+    return near, far
+
+
 def shards(object_field, probe, propagator_phase, patterns, scan_positions):
     first, second, near, far = begin(object_field)
     near, far = swap_rows(near, far)
+    core_near, core_far = swap_cols(first, second)
     lit, phase, ordered = setup(
         scan_positions[0, 0, 0], probe, propagator_phase, patterns[0, 0, 0], order_table()
     )
     wave = jnp.stack([jnp.cos(phase), jnp.sin(phase)])
     tables = jnp.asarray(half_tables())
-    first, second = assemble(first, second, near, far)
-    for turn in range(STEPS):
-        far = swap("tx", 1, second)
-        near = swap("tx", 0, first)
-        part_1, part_2, near, far = step(
-            first, second, near, far, lit, wave, ordered, tables
-        )
-        far = swap("tx", 1, far)
-        near = swap("tx", 0, near)
-        if turn < STEPS - 1:
-            total, near, far = share(part_1, part_2, near, far)
-            near, far = swap_rows(near, far)
-            first, second = update(first, second, total, near, far)
-    total, near, far = close(part_1, part_2, near, far)
+    shared = (lit, wave, ordered, tables)
+    margin_1, margin_2 = margins(near, far)
+    rim_near, rim_far = swap_cols(margin_1, margin_2)
+    taken = (first, margin_1, second, margin_2, core_near, rim_near, core_far, rim_far)
+    parts, (near,), (far,) = step(2, 1, *taken, *shared)
+
+    near, far = swap_cols(near, far)
+    total, near, far = share(*parts, near, far)
     near, far = swap_rows(near, far)
-    return finish(first, second, total, near, far)
+    first, second = update(first, second, margin_1, margin_2, total, near, far)
+    near, far = swap_cols(first, second)
+    parts, near, far = step(1, 2, first, second, near, far, *shared)
+
+    rim_near, rim_far = swap_cols(near[1], far[1])
+    core_near, core_far = swap_cols(near[0], far[0])
+    near, far = swap_rows(*close(*parts, rim_near, rim_far))
+    return finish(first, second, *parts, core_near, core_far, near, far)
 
 
 def solution(mesh):

time: 131 us -> 138 us (1.053)
  the two profiles are of different devices: /device:TPU:232 before, /device:TPU:31 now
where the time goes in v5:
time: 138 us; the launch traced here: 137 us
  starting transfers between devices  70.6 us (51%)
  waiting for transfers between devices  43.5 us (32%)
  Pallas kernels  17.2 us (12%)
  local copies, waits for them, and re-layouts  5.55 us (4%)
    ppermute x18, starting transfers between devices, swap(): return lax.ppermute(block, axis, pairs + [(j, i) for i, j in pairs])  70.6 us
    ppermute x18, waiting for transfers between devices, swap(): return lax.ppermute(block, axis, pairs + [(j, i) for i, j in pairs])  43.5 us
    pallas_call x2, Pallas kernels, step(): call(functools.partial(step_kernel, blocks, cuts), (PACK, PACK) + ((PACK,...  14.4 us
    unnamed x14, local copies, waits for them, and re-layouts  4.59 us
  transfers between devices with their start and end apart: 18, of which 6 were waited for; matrix products, arithmetic and copies ran while one was open for 1% of the time, Pallas kernels for 1%

profile of v5, /device:TPU:31, one launch (start us, length us, event | category | flops | bytes accessed | tf_op | source)
XLA Modules:
  0.0 137.1 jit_solution(1620745552886414845)
XLA Ops:
  0.0 0.0 copy-start.2
  0.0 1.0 copy-done.2
  1.0 0.0 copy-start.3
  1.0 0.1 open_kernel.1
  1.1 1.7 %collective-permute-start = (f32[2,3,64,128]{3,2,1,0:T(8,128)S(1)}, f32[2,3,64,128]{3,2,1,0:T(8,128)S(1)}, u32[]{:S(2)}, u32[]{:S(2)}) collective-permute-start(f32[2,3,64,128]{3,2,1,0:T(8,128)S(1)} %get-tuple-element.33), channel_id=1, source_target_pairs={{0,16},{32,48},{64,80},{96,112},{128,144},{160,176},{192,208},{224... | collective-permute-start | bytes 589832 | tf_op jit(solution)/shard_map/ppermute | solution.py:385
  2.9 4.8 %collective-permute-start.1 = (f32[2,3,64,128]{3,2,1,0:T(8,128)S(1)}, f32[2,3,64,128]{3,2,1,0:T(8,128)S(1)}, u32[]{:S(2)}, u32[]{:S(2)}) collective-permute-start(f32[2,3,64,128]{3,2,1,0:T(8,128)S(1)} %get-tuple-element.34), channel_id=1, source_target_pairs={{16,32},{48,64},{80,96},{112,128},{144,160},{176,192},{208,224},{3... | collective-permute-start | bytes 589832 | tf_op jit(solution)/shard_map/ppermute | solution.py:385
  7.7 1.1 collective-permute-start.2
  8.8 6.8 %collective-permute-start.4 = (f32[3,128,128]{2,1,0:T(8,128)S(1)}, f32[3,128,128]{2,1,0:T(8,128)S(1)}, u32[]{:S(2)}, u32[]{:S(2)}) collective-permute-start(f32[3,128,128]{2,1,0:T(8,128)S(1)} %get-tuple-element.32.refs_2_.core_2), channel_id=1, source_target_pairs={{1,2},{3,4},{5,6},{7,8},{9,10},{11,12},{13,14},{2,1},{4,3},{6,5},{... | collective-permute-start | bytes 589832 | tf_op jit(solution)/shard_map/ppermute | solution.py:385
  15.6 0.0 copy-start.6
  15.6 0.0 copy-done.3
  15.7 0.6 copy-done.6
  16.3 0.0 copy-start.1
  16.3 1.0 copy-done.1
  17.3 0.0 copy-start.4
  17.3 0.9 copy-done.4
  18.3 0.0 copy-start.5
  18.3 0.9 copy-done.5
  19.2 1.4 %setup_kernel.1 = (f32[2,256,256]{2,1,0:T(8,128)S(1)}, f32[256,256]{1,0:T(8,128)S(1)}, f32[256,256]{1,0:T(8,128)S(1)}) custom-call(s32[2]{0:T(128)S(1)} %bitcast.7, f32[2,256,256]{2,1,0:T(8,128)S(1)} %copy-done.1, f32[256,256]{1,0:T(8,128)S(1)} %copy-done.3, f32[256,256]{1,0:T(8,128)S(1)} %bitcast.6, bf16[2,256,256]{2,1,0:T(8,128)(2,1)S(1)} %copy-done.5), custom_call_target="tpu_custom_call" | custom-call | tf_op jit(solution)/shard_map/setup_kernel/pallas_call | solution.py:273
  20.6 0.0 copy-start
  20.7 0.0 collective-permute-done.near
  20.7 0.0 collective-permute-done.1.far
  20.7 0.1 margin_kernel.1
  20.7 0.1 collective-permute-start.3
  20.8 4.9 %collective-permute-start.5 = (f32[3,128,128]{2,1,0:T(8,128)S(1)}, f32[3,128,128]{2,1,0:T(8,128)S(1)}, u32[]{:S(2)}, u32[]{:S(2)}) collective-permute-start(f32[3,128,128]{2,1,0:T(8,128)S(1)} %get-tuple-element.36.refs_3_.margin_2), channel_id=1, source_target_pairs={{1,2},{3,4},{5,6},{7,8},{9,10},{11,12},{13,14},{2,1},{4,3},{6,5},{... | collective-permute-start | bytes 589832 | tf_op jit(solution)/shard_map/ppermute | solution.py:385
  25.7 1.0 cosine_bitcast_fusion
  26.7 0.0 collective-permute-done.2.refs_4_
  26.7 0.0 collective-permute-done.4.refs_6_
  26.7 0.0 collective-permute-done.3.refs_5_
  26.8 7.3 %collective-permute-done.5.refs_7_ = f32[3,128,128]{2,1,0:T(8,128)S(1)} collective-permute-done((f32[3,128,128]{2,1,0:T(8,128)S(1)}, f32[3,128,128]{2,1,0:T(8,128)S(1)}, u32[]{:S(2)}, u32[]{:S(2)}) %collective-permute-start.5) | collective-permute-done | bytes 196640 | tf_op jit(solution)/shard_map/ppermute | solution.py:385
  34.1 0.0 copy-done
  34.1 7.2 %step_kernel.2 = (f32[3,256,128]{2,1,0:T(8,128)S(1)}, f32[3,256,128]{2,1,0:T(8,128)S(1)}, f32[3,256,128]{2,1,0:T(8,128)S(1)}, f32[3,256,128]{2,1,0:T(8,128)S(1)}) custom-call(f32[3,128,128]{2,1,0:T(8,128)S(1)} %get-tuple-element.31.refs_0_.core_1, f32[3,128,128]{2,1,0:T(8,128)S(1)} %get-tuple-element.35.refs_1_.margin_1, ...), custom_call_target="tpu_custom_call" | custom-call | tf_op jit(solution)/shard_map/step_kernel/pallas_call | solution.py:233
  41.3 0.1 collective-permute-start.6
  41.4 4.7 %collective-permute-start.7 = (f32[3,256,128]{2,1,0:T(8,128)S(1)}, f32[3,256,128]{2,1,0:T(8,128)S(1)}, u32[]{:S(2)}, u32[]{:S(2)}) collective-permute-start(f32[3,256,128]{2,1,0:T(8,128)S(1)} %get-tuple-element.43), channel_id=1, source_target_pairs={{1,2},{3,4},{5,6},{7,8},{9,10},{11,12},{13,14},{2,1},{4,3},{6,5},{... | collective-permute-start | bytes 1179656 | tf_op jit(solution)/shard_map/ppermute | solution.py:385
  46.1 0.0 collective-permute-done.6.came_1
  46.1 11.9 %collective-permute-done.7.came_2 = f32[3,256,128]{2,1,0:T(8,128)S(1)} collective-permute-done((f32[3,256,128]{2,1,0:T(8,128)S(1)}, f32[3,256,128]{2,1,0:T(8,128)S(1)}, u32[]{:S(2)}, u32[]{:S(2)}) %collective-permute-start.7) | collective-permute-done | bytes 393248 | tf_op jit(solution)/shard_map/ppermute | solution.py:385
  58.0 0.1 share_kernel.1
  58.1 4.1 %collective-permute-start.8 = (f32[2,3,128,128]{3,2,1,0:T(8,128)S(1)}, f32[2,3,128,128]{3,2,1,0:T(8,128)S(1)}, u32[]{:S(2)}, u32[]{:S(2)}) collective-permute-start(f32[2,3,128,128]{3,2,1,0:T(8,128)S(1)} %get-tuple-element.45), channel_id=1, source_target_pairs={{0,16},{32,48},{64,80},{96,112},{128,144},{160,176},{192,208},{224... | collective-permute-start | bytes 1179656 | tf_op jit(solution)/shard_map/ppermute | solution.py:385
  62.2 12.1 %collective-permute-start.9 = (f32[2,3,128,128]{3,2,1,0:T(8,128)S(1)}, f32[2,3,128,128]{3,2,1,0:T(8,128)S(1)}, u32[]{:S(2)}, u32[]{:S(2)}) collective-permute-start(f32[2,3,128,128]{3,2,1,0:T(8,128)S(1)} %get-tuple-element.46), channel_id=1, source_target_pairs={{16,32},{48,64},{80,96},{112,128},{144,160},{176,192},{208,224},{3... | collective-permute-start | bytes 1179656 | tf_op jit(solution)/shard_map/ppermute | solution.py:385
  74.3 0.0 collective-permute-done.8.near
  74.3 7.6 %collective-permute-done.9.far = f32[2,3,128,128]{3,2,1,0:T(8,128)S(1)} collective-permute-done((f32[2,3,128,128]{3,2,1,0:T(8,128)S(1)}, f32[2,3,128,128]{3,2,1,0:T(8,128)S(1)}, u32[]{:S(2)}, u32[]{:S(2)}) %collective-permute-start.9) | collective-permute-done | bytes 393248 | tf_op jit(solution)/shard_map/ppermute | solution.py:385
  81.9 0.1 update_kernel.1
  82.0 0.1 collective-permute-start.10
  82.1 3.1 %collective-permute-start.11 = (f32[3,256,128]{2,1,0:T(8,128)S(1)}, f32[3,256,128]{2,1,0:T(8,128)S(1)}, u32[]{:S(2)}, u32[]{:S(2)}) collective-permute-start(f32[3,256,128]{2,1,0:T(8,128)S(1)} %get-tuple-element.48.refs_1_.mid_2), channel_id=1, source_target_pairs={{1,2},{3,4},{5,6},{7,8},{9,10},{11,12},{13,14},{2,1},{4,3},{6,5},{... | collective-permute-start | bytes 1179656 | tf_op jit(solution)/shard_map/ppermute | solution.py:385
  85.2 0.0 collective-permute-done.10.refs_2_
  85.2 12.1 %collective-permute-done.11.refs_3_ = f32[3,256,128]{2,1,0:T(8,128)S(1)} collective-permute-done((f32[3,256,128]{2,1,0:T(8,128)S(1)}, f32[3,256,128]{2,1,0:T(8,128)S(1)}, u32[]{:S(2)}, u32[]{:S(2)}) %collective-permute-start.11) | collective-permute-done | bytes 393248 | tf_op jit(solution)/shard_map/ppermute | solution.py:385
  97.3 7.2 %step_kernel.3 = (f32[3,256,128]{2,1,0:T(8,128)S(1)}, f32[3,256,128]{2,1,0:T(8,128)S(1)}, f32[3,128,128]{2,1,0:T(8,128)S(1)}, f32[3,128,128]{2,1,0:T(8,128)S(1)}...) custom-call(f32[3,256,128]{2,1,0:T(8,128)S(1)} %get-tuple-element.47.refs_0_.mid_1, ...), custom_call_target="tpu_custom_call" | custom-call | tf_op jit(solution)/shard_map/step_kernel/pallas_call | solution.py:233
  104.5 0.1 collective-permute-start.14
  104.6 2.9 %collective-permute-start.15 = (f32[3,128,128]{2,1,0:T(8,128)S(1)}, f32[3,128,128]{2,1,0:T(8,128)S(1)}, u32[]{:S(2)}, u32[]{:S(2)}) collective-permute-start(f32[3,128,128]{2,1,0:T(8,128)S(1)} %get-tuple-element.54), channel_id=1, source_target_pairs={{1,2},{3,4},{5,6},{7,8},{9,10},{11,12},{13,14},{2,1},{4,3},{6,5},{... | collective-permute-start | bytes 589832 | tf_op jit(solution)/shard_map/ppermute | solution.py:385
  107.5 0.1 collective-permute-start.12
  107.6 8.7 %collective-permute-start.13 = (f32[3,128,128]{2,1,0:T(8,128)S(1)}, f32[3,128,128]{2,1,0:T(8,128)S(1)}, u32[]{:S(2)}, u32[]{:S(2)}) collective-permute-start(f32[3,128,128]{2,1,0:T(8,128)S(1)} %get-tuple-element.52), channel_id=1, source_target_pairs={{1,2},{3,4},{5,6},{7,8},{9,10},{11,12},{13,14},{2,1},{4,3},{6,5},{... | collective-permute-start | bytes 589832 | tf_op jit(solution)/shard_map/ppermute | solution.py:385
  116.3 0.0 collective-permute-done.14.came_1
  116.3 1.3 collective-permute-done.15.came_2
  117.7 0.1 collective-permute-start.16
  117.8 15.0 %collective-permute-start.17 = (f32[2,3,64,128]{3,2,1,0:T(8,128)S(1)}, f32[2,3,64,128]{3,2,1,0:T(8,128)S(1)}, u32[]{:S(2)}, u32[]{:S(2)}) collective-permute-start(f32[2,3,64,128]{3,2,1,0:T(8,128)S(1)} %get-tuple-element.56), channel_id=1, source_target_pairs={{16,32},{48,64},{80,96},{112,128},{144,160},{176,192},{208,224},{3... | collective-permute-start | bytes 589832 | tf_op jit(solution)/shard_map/ppermute | solution.py:385
  132.9 0.0 collective-permute-done.12.came_1
  132.9 0.0 collective-permute-done.13.came_2
  132.9 0.0 collective-permute-done.16.near
  132.9 3.3 %collective-permute-done.17.far = f32[2,3,64,128]{3,2,1,0:T(8,128)S(1)} collective-permute-done((f32[2,3,64,128]{3,2,1,0:T(8,128)S(1)}, f32[2,3,64,128]{3,2,1,0:T(8,128)S(1)}, u32[]{:S(2)}, u32[]{:S(2)}) %collective-permute-start.17) | collective-permute-done | bytes 196640 | tf_op jit(solution)/shard_map/ppermute | solution.py:385
  136.2 0.9 finish_kernel.1
  (2 shorter events, 0.1 us)
Async XLA Ops:
  0.0 1.0 copy-start.2
  1.0 14.7 %copy-start.3 = (f32[256,256]{1,0:T(8,128)S(1)}, f32[256,256]{1,0:T(8,128)}, u32[]{:S(2)}) copy-start(f32[256,256]{1,0:T(8,128)} %phase.1) | copy-start | bytes 786436
  1.1 19.5 %collective-permute-start = (f32[2,3,64,128]{3,2,1,0:T(8,128)S(1)}, f32[2,3,64,128]{3,2,1,0:T(8,128)S(1)}, u32[]{:S(2)}, u32[]{:S(2)}) collective-permute-start(f32[2,3,64,128]{3,2,1,0:T(8,128)S(1)} %get-tuple-element.33), channel_id=1, source_target_pairs={{0,16},{32,48},{64,80},{96,112},{128,144},{160,176},{192,208},{224... | collective-permute-start | bytes 589832 | tf_op jit(solution)/shard_map/ppermute | solution.py:385
  2.9 17.8 %collective-permute-start.1 = (f32[2,3,64,128]{3,2,1,0:T(8,128)S(1)}, f32[2,3,64,128]{3,2,1,0:T(8,128)S(1)}, u32[]{:S(2)}, u32[]{:S(2)}) collective-permute-start(f32[2,3,64,128]{3,2,1,0:T(8,128)S(1)} %get-tuple-element.34), channel_id=1, source_target_pairs={{16,32},{48,64},{80,96},{112,128},{144,160},{176,192},{208,224},{3... | collective-permute-start | bytes 589832 | tf_op jit(solution)/shard_map/ppermute | solution.py:385
  7.7 19.1 %collective-permute-start.2 = (f32[3,128,128]{2,1,0:T(8,128)S(1)}, f32[3,128,128]{2,1,0:T(8,128)S(1)}, u32[]{:S(2)}, u32[]{:S(2)}) collective-permute-start(f32[3,128,128]{2,1,0:T(8,128)S(1)} %get-tuple-element.31.refs_0_.core_1), channel_id=1, source_target_pairs={{0,1},{2,3},{4,5},{6,7},{8,9},{10,11},{12,13},{14,15},{1,0},{3,2},... | collective-permute-start | bytes 589832 | tf_op jit(solution)/shard_map/ppermute | solution.py:385
  8.8 17.9 %collective-permute-start.4 = (f32[3,128,128]{2,1,0:T(8,128)S(1)}, f32[3,128,128]{2,1,0:T(8,128)S(1)}, u32[]{:S(2)}, u32[]{:S(2)}) collective-permute-start(f32[3,128,128]{2,1,0:T(8,128)S(1)} %get-tuple-element.32.refs_2_.core_2), channel_id=1, source_target_pairs={{1,2},{3,4},{5,6},{7,8},{9,10},{11,12},{13,14},{2,1},{4,3},{6,5},{... | collective-permute-start | bytes 589832 | tf_op jit(solution)/shard_map/ppermute | solution.py:385
  15.6 0.7 copy-start.6
  16.3 1.0 copy-start.1
  17.3 0.9 copy-start.4
  18.3 0.9 copy-start.5
  20.6 13.4 %copy-start = (bf16[4,2,256,256]{3,2,1,0:T(8,128)(2,1)S(1)}, bf16[4,2,256,256]{3,2,1,0:T(8,128)(2,1)}, u32[]{:S(2)}) copy-start(bf16[4,2,256,256]{3,2,1,0:T(8,128)(2,1)} %constant.5.clone.refs_11_.refs_7_) | copy-start | bytes 3145732
  20.7 6.0 %collective-permute-start.3 = (f32[3,128,128]{2,1,0:T(8,128)S(1)}, f32[3,128,128]{2,1,0:T(8,128)S(1)}, u32[]{:S(2)}, u32[]{:S(2)}) collective-permute-start(f32[3,128,128]{2,1,0:T(8,128)S(1)} %get-tuple-element.35.refs_1_.margin_1), channel_id=1, source_target_pairs={{0,1},{2,3},{4,5},{6,7},{8,9},{10,11},{12,13},{14,15},{1,0},{3,2},... | collective-permute-start | bytes 589832 | tf_op jit(solution)/shard_map/ppermute | solution.py:385
  20.8 13.2 %collective-permute-start.5 = (f32[3,128,128]{2,1,0:T(8,128)S(1)}, f32[3,128,128]{2,1,0:T(8,128)S(1)}, u32[]{:S(2)}, u32[]{:S(2)}) collective-permute-start(f32[3,128,128]{2,1,0:T(8,128)S(1)} %get-tuple-element.36.refs_3_.margin_2), channel_id=1, source_target_pairs={{1,2},{3,4},{5,6},{7,8},{9,10},{11,12},{13,14},{2,1},{4,3},{6,5},{... | collective-permute-start | bytes 589832 | tf_op jit(solution)/shard_map/ppermute | solution.py:385
  41.3 4.8 %collective-permute-start.6 = (f32[3,256,128]{2,1,0:T(8,128)S(1)}, f32[3,256,128]{2,1,0:T(8,128)S(1)}, u32[]{:S(2)}, u32[]{:S(2)}) collective-permute-start(f32[3,256,128]{2,1,0:T(8,128)S(1)} %get-tuple-element.42), channel_id=1, source_target_pairs={{0,1},{2,3},{4,5},{6,7},{8,9},{10,11},{12,13},{14,15},{1,0},{3,2},... | collective-permute-start | bytes 1179656 | tf_op jit(solution)/shard_map/ppermute | solution.py:385
  41.4 16.6 %collective-permute-start.7 = (f32[3,256,128]{2,1,0:T(8,128)S(1)}, f32[3,256,128]{2,1,0:T(8,128)S(1)}, u32[]{:S(2)}, u32[]{:S(2)}) collective-permute-start(f32[3,256,128]{2,1,0:T(8,128)S(1)} %get-tuple-element.43), channel_id=1, source_target_pairs={{1,2},{3,4},{5,6},{7,8},{9,10},{11,12},{13,14},{2,1},{4,3},{6,5},{... | collective-permute-start | bytes 1179656 | tf_op jit(solution)/shard_map/ppermute | solution.py:385
  58.1 16.2 %collective-permute-start.8 = (f32[2,3,128,128]{3,2,1,0:T(8,128)S(1)}, f32[2,3,128,128]{3,2,1,0:T(8,128)S(1)}, u32[]{:S(2)}, u32[]{:S(2)}) collective-permute-start(f32[2,3,128,128]{3,2,1,0:T(8,128)S(1)} %get-tuple-element.45), channel_id=1, source_target_pairs={{0,16},{32,48},{64,80},{96,112},{128,144},{160,176},{192,208},{224... | collective-permute-start | bytes 1179656 | tf_op jit(solution)/shard_map/ppermute | solution.py:385
  62.2 19.7 %collective-permute-start.9 = (f32[2,3,128,128]{3,2,1,0:T(8,128)S(1)}, f32[2,3,128,128]{3,2,1,0:T(8,128)S(1)}, u32[]{:S(2)}, u32[]{:S(2)}) collective-permute-start(f32[2,3,128,128]{3,2,1,0:T(8,128)S(1)} %get-tuple-element.46), channel_id=1, source_target_pairs={{16,32},{48,64},{80,96},{112,128},{144,160},{176,192},{208,224},{3... | collective-permute-start | bytes 1179656 | tf_op jit(solution)/shard_map/ppermute | solution.py:385
  82.0 3.2 %collective-permute-start.10 = (f32[3,256,128]{2,1,0:T(8,128)S(1)}, f32[3,256,128]{2,1,0:T(8,128)S(1)}, u32[]{:S(2)}, u32[]{:S(2)}) collective-permute-start(f32[3,256,128]{2,1,0:T(8,128)S(1)} %get-tuple-element.47.refs_0_.mid_1), channel_id=1, source_target_pairs={{0,1},{2,3},{4,5},{6,7},{8,9},{10,11},{12,13},{14,15},{1,0},{3,2},... | collective-permute-start | bytes 1179656 | tf_op jit(solution)/shard_map/ppermute | solution.py:385
  82.1 15.2 %collective-permute-start.11 = (f32[3,256,128]{2,1,0:T(8,128)S(1)}, f32[3,256,128]{2,1,0:T(8,128)S(1)}, u32[]{:S(2)}, u32[]{:S(2)}) collective-permute-start(f32[3,256,128]{2,1,0:T(8,128)S(1)} %get-tuple-element.48.refs_1_.mid_2), channel_id=1, source_target_pairs={{1,2},{3,4},{5,6},{7,8},{9,10},{11,12},{13,14},{2,1},{4,3},{6,5},{... | collective-permute-start | bytes 1179656 | tf_op jit(solution)/shard_map/ppermute | solution.py:385
  104.5 11.8 %collective-permute-start.14 = (f32[3,128,128]{2,1,0:T(8,128)S(1)}, f32[3,128,128]{2,1,0:T(8,128)S(1)}, u32[]{:S(2)}, u32[]{:S(2)}) collective-permute-start(f32[3,128,128]{2,1,0:T(8,128)S(1)} %get-tuple-element.53), channel_id=1, source_target_pairs={{0,1},{2,3},{4,5},{6,7},{8,9},{10,11},{12,13},{14,15},{1,0},{3,2},... | collective-permute-start | bytes 589832 | tf_op jit(solution)/shard_map/ppermute | solution.py:385
  104.6 13.0 %collective-permute-start.15 = (f32[3,128,128]{2,1,0:T(8,128)S(1)}, f32[3,128,128]{2,1,0:T(8,128)S(1)}, u32[]{:S(2)}, u32[]{:S(2)}) collective-permute-start(f32[3,128,128]{2,1,0:T(8,128)S(1)} %get-tuple-element.54), channel_id=1, source_target_pairs={{1,2},{3,4},{5,6},{7,8},{9,10},{11,12},{13,14},{2,1},{4,3},{6,5},{... | collective-permute-start | bytes 589832 | tf_op jit(solution)/shard_map/ppermute | solution.py:385
  107.5 25.3 %collective-permute-start.12 = (f32[3,128,128]{2,1,0:T(8,128)S(1)}, f32[3,128,128]{2,1,0:T(8,128)S(1)}, u32[]{:S(2)}, u32[]{:S(2)}) collective-permute-start(f32[3,128,128]{2,1,0:T(8,128)S(1)} %get-tuple-element.51), channel_id=1, source_target_pairs={{0,1},{2,3},{4,5},{6,7},{8,9},{10,11},{12,13},{14,15},{1,0},{3,2},... | collective-permute-start | bytes 589832 | tf_op jit(solution)/shard_map/ppermute | solution.py:385
  107.6 25.3 %collective-permute-start.13 = (f32[3,128,128]{2,1,0:T(8,128)S(1)}, f32[3,128,128]{2,1,0:T(8,128)S(1)}, u32[]{:S(2)}, u32[]{:S(2)}) collective-permute-start(f32[3,128,128]{2,1,0:T(8,128)S(1)} %get-tuple-element.52), channel_id=1, source_target_pairs={{1,2},{3,4},{5,6},{7,8},{9,10},{11,12},{13,14},{2,1},{4,3},{6,5},{... | collective-permute-start | bytes 589832 | tf_op jit(solution)/shard_map/ppermute | solution.py:385
  117.7 15.2 %collective-permute-start.16 = (f32[2,3,64,128]{3,2,1,0:T(8,128)S(1)}, f32[2,3,64,128]{3,2,1,0:T(8,128)S(1)}, u32[]{:S(2)}, u32[]{:S(2)}) collective-permute-start(f32[2,3,64,128]{3,2,1,0:T(8,128)S(1)} %get-tuple-element.55), channel_id=1, source_target_pairs={{0,16},{32,48},{64,80},{96,112},{128,144},{160,176},{192,208},{224... | collective-permute-start | bytes 589832 | tf_op jit(solution)/shard_map/ppermute | solution.py:385
  117.8 18.4 %collective-permute-start.17 = (f32[2,3,64,128]{3,2,1,0:T(8,128)S(1)}, f32[2,3,64,128]{3,2,1,0:T(8,128)S(1)}, u32[]{:S(2)}, u32[]{:S(2)}) collective-permute-start(f32[2,3,64,128]{3,2,1,0:T(8,128)S(1)} %get-tuple-element.56), channel_id=1, source_target_pairs={{16,32},{48,64},{80,96},{112,128},{144,160},{176,192},{208,224},{3... | collective-permute-start | bytes 589832 | tf_op jit(solution)/shard_map/ppermute | solution.py:385

commit v6 on v4

--- a/solution.py
+++ b/solution.py
@@ -267,19 +267,44 @@
     return call(setup_kernel, shapes, smem=1, count=4)(positions, probe, phase, patterns, order)
 
 
-def open_kernel(core, first, second, near, far):
+def planes(source, target, sems):
+    return [
+        pltpu.make_async_copy(source.at[layer, c], target.at[layer, c], sems.at[layer, c])
+        for layer in range(SLICES)
+        for c in range(2)
+    ]
+
+
+def open_kernel(whole, first, second, near, far, core, sems):
+    copies = planes(whole, core, sems)
+    for copy in copies:
+        copy.start()
     even = even_row()
     nearby = near_lanes(CORE)
     for layer in range(SLICES):
+        copies[2 * layer].wait()
+        copies[2 * layer + 1].wait()
         packs = pack(nearby, core[layer, 0], core[layer, 1])
-        for k, (value, whole) in enumerate(zip(packs, (first, second))):
-            whole[layer] = value
+        for k, (value, kept) in enumerate(zip(packs, (first, second))):
+            kept[layer] = value
             near[k, layer] = jnp.where(even, value[MARGIN:], value[:MARGIN])
             far[k, layer] = jnp.where(even, value[:MARGIN], value[MARGIN:])
 
 
+BLOCK = (SLICES, 2, CORE, CORE)
+COPIES = (pltpu.VMEM(BLOCK, jnp.float32), pltpu.SemaphoreType.DMA((SLICES, 2)))
+
+
 def begin(core):
-    return call(open_kernel, (HALF, HALF, RIMS, RIMS), count=1)(core)
+    return pl.pallas_call(
+        open_kernel,
+        out_shape=[jax.ShapeDtypeStruct(s, jnp.float32) for s in (HALF, HALF, RIMS, RIMS)],
+        in_specs=[pl.BlockSpec(memory_space=pltpu.HBM)],
+        out_specs=[pl.BlockSpec(memory_space=pltpu.VMEM)] * 4,
+        scratch_shapes=list(COPIES),
+        compiler_params=pltpu.CompilerParams(vmem_limit_bytes=8 << 20),
+        name="open_kernel",
+    )(pltpu.with_memory_space_constraint(core, pltpu.HBM))
 
 
 def assemble_kernel(core_1, core_2, near, far, first, second):
@@ -353,7 +378,8 @@
     return call(close_kernel, ((2, *HALF), RIMS, RIMS), count=4)(*args)
 
 
-def finish_kernel(mid_1, mid_2, total, near, far, out):
+def finish_kernel(mid_1, mid_2, total, near, far, whole, out, sems):
+    copies = planes(out, whole, sems)
     even = even_row()
     nearby = near_lanes(MARGIN)
     for layer in range(SLICES):
@@ -365,10 +391,22 @@
                 added = jnp.where(even, o, e) if half == 0 else jnp.where(even, e, o)
                 packs.append(mid[layer, rows] - STEP_SIZE * (total[k, layer, rows] + added))
             out[layer, 0, rows], out[layer, 1, rows] = unpack(nearby, *packs)
+        copies[2 * layer].start()
+        copies[2 * layer + 1].start()
+    for copy in copies:
+        copy.wait()
 
 
 def finish(*args):
-    return call(finish_kernel, ((SLICES, 2, CORE, CORE),), count=5)(*args)[0]
+    return pl.pallas_call(
+        finish_kernel,
+        out_shape=jax.ShapeDtypeStruct(BLOCK, jnp.float32),
+        in_specs=[pl.BlockSpec(memory_space=pltpu.VMEM)] * 5,
+        out_specs=pl.BlockSpec(memory_space=pltpu.HBM),
+        scratch_shapes=list(COPIES),
+        compiler_params=pltpu.CompilerParams(vmem_limit_bytes=8 << 20),
+        name="finish_kernel",
+    )(*args)
 
 
 def swap(axis, first, block):

time: 131 us -> 131 us (level)
  no operation moved by 1% of the time
where the time goes in v6:
time: 131 us; the launch traced here: 130 us
  waiting for transfers between devices  62 us (47%)
  starting transfers between devices  46.9 us (36%)
  Pallas kernels  18.3 us (14%)
  local copies, waits for them, and re-layouts  2.56 us (2%)
    ppermute x14, waiting for transfers between devices, swap(): return lax.ppermute(block, axis, pairs + [(j, i) for i, j in pairs])  62 us
    ppermute x14, starting transfers between devices, swap(): return lax.ppermute(block, axis, pairs + [(j, i) for i, j in pairs])  46.9 us
    pallas_call x2, Pallas kernels, step(): call(step_kernel, (PACK, PACK, PACK, PACK), (pltpu.VMEM((SLICES, 2, TILE,...  14.4 us
  transfers between devices with their start and end apart: 14, of which 10 were waited for; matrix products, arithmetic and copies ran while one was open for 1% of the time, Pallas kernels for 1%

profile of v6, /device:TPU:232, one launch (start us, length us, event | category | flops | bytes accessed | tf_op | source)
XLA Modules:
  0.0 130.2 jit_solution(9626475650376653998)
XLA Ops:
  0.0 0.0 copy-start.1
  0.0 1.3 open_kernel.1
  1.3 1.1 collective-permute-start
  2.4 4.8 %collective-permute-start.1 = (f32[2,3,64,128]{3,2,1,0:T(8,128)S(1)}, f32[2,3,64,128]{3,2,1,0:T(8,128)S(1)}, u32[]{:S(2)}, u32[]{:S(2)}) collective-permute-start(f32[2,3,64,128]{3,2,1,0:T(8,128)S(1)} %get-tuple-element.33), channel_id=1, source_target_pairs={{16,32},{48,64},{80,96},{112,128},{144,160},{176,192},{208,224},{3... | collective-permute-start | bytes 589832 | tf_op jit(solution)/shard_map/ppermute | solution.py:415
  7.2 0.8 collective-permute-done.near
  8.0 6.2 %collective-permute-done.1.far = f32[2,3,64,128]{3,2,1,0:T(8,128)S(1)} collective-permute-done((f32[2,3,64,128]{3,2,1,0:T(8,128)S(1)}, f32[2,3,64,128]{3,2,1,0:T(8,128)S(1)}, u32[]{:S(2)}, u32[]{:S(2)}) %collective-permute-start.1) | collective-permute-done | bytes 196640 | tf_op jit(solution)/shard_map/ppermute | solution.py:415
  14.2 0.0 copy-start.2
  14.2 0.0 copy-start.3
  14.2 0.1 assemble_kernel.1
  14.3 0.1 collective-permute-start.2
  14.4 4.1 %collective-permute-start.3 = (f32[3,256,128]{2,1,0:T(8,128)S(1)}, f32[3,256,128]{2,1,0:T(8,128)S(1)}, u32[]{:S(2)}, u32[]{:S(2)}) collective-permute-start(f32[3,256,128]{2,1,0:T(8,128)S(1)} %get-tuple-element.35.second.mid_2), channel_id=1, source_target_pairs={{1,2},{3,4},{5,6},{7,8},{9,10},{11,12},{13,14},{2,1},{4,3},{6,5},{... | collective-permute-start | bytes 1179656 | tf_op jit(solution)/shard_map/ppermute | solution.py:415
  18.5 0.0 copy-start.5
  18.5 0.0 copy-done.1
  18.5 0.0 copy-done.2
  18.5 0.0 copy-done.3
  18.6 0.6 copy-done.5
  19.2 0.0 copy-start.4
  19.2 0.9 copy-done.4
  20.1 1.4 %setup_kernel.1 = (f32[2,256,256]{2,1,0:T(8,128)S(1)}, f32[256,256]{1,0:T(8,128)S(1)}, f32[256,256]{1,0:T(8,128)S(1)}) custom-call(s32[2]{0:T(128)S(1)} %bitcast.7, f32[2,256,256]{2,1,0:T(8,128)S(1)} %copy-done.1, f32[256,256]{1,0:T(8,128)S(1)} %copy-done.2, f32[256,256]{1,0:T(8,128)S(1)} %bitcast.6, bf16[2,256,256]{2,1,0:T(8,128)(2,1)S(1)} %copy-done.4), custom_call_target="tpu_custom_call" | custom-call | tf_op jit(solution)/shard_map/setup_kernel/pallas_call | solution.py:267
  21.5 0.0 copy-start
  21.5 1.0 cosine_bitcast_fusion
  22.6 0.0 collective-permute-done.2.near
  22.6 7.0 %collective-permute-done.3.far = f32[3,256,128]{2,1,0:T(8,128)S(1)} collective-permute-done((f32[3,256,128]{2,1,0:T(8,128)S(1)}, f32[3,256,128]{2,1,0:T(8,128)S(1)}, u32[]{:S(2)}, u32[]{:S(2)}) %collective-permute-start.3) | collective-permute-done | bytes 393248 | tf_op jit(solution)/shard_map/ppermute | solution.py:415
  29.6 0.0 copy-done
  29.6 7.2 %step_kernel.2 = (f32[3,256,128]{2,1,0:T(8,128)S(1)}, f32[3,256,128]{2,1,0:T(8,128)S(1)}, f32[3,256,128]{2,1,0:T(8,128)S(1)}, f32[3,256,128]{2,1,0:T(8,128)S(1)}) custom-call(f32[3,256,128]{2,1,0:T(8,128)S(1)} %get-tuple-element.34.first.mid_1, f32[3,256,128]{2,1,0:T(8,128)S(1)} %get-tuple-element.35.second.mid_2, ...), custom_call_target="tpu_custom_call" | custom-call | tf_op jit(solution)/shard_map/step_kernel/pallas_call | solution.py:229
  36.8 0.1 collective-permute-start.4
  36.9 4.1 %collective-permute-start.5 = (f32[3,256,128]{2,1,0:T(8,128)S(1)}, f32[3,256,128]{2,1,0:T(8,128)S(1)}, u32[]{:S(2)}, u32[]{:S(2)}) collective-permute-start(f32[3,256,128]{2,1,0:T(8,128)S(1)} %get-tuple-element.42), channel_id=1, source_target_pairs={{1,2},{3,4},{5,6},{7,8},{9,10},{11,12},{13,14},{2,1},{4,3},{6,5},{... | collective-permute-start | bytes 1179656 | tf_op jit(solution)/shard_map/ppermute | solution.py:415
  41.0 0.0 collective-permute-done.4.came_1
  41.0 11.0 %collective-permute-done.5.came_2 = f32[3,256,128]{2,1,0:T(8,128)S(1)} collective-permute-done((f32[3,256,128]{2,1,0:T(8,128)S(1)}, f32[3,256,128]{2,1,0:T(8,128)S(1)}, u32[]{:S(2)}, u32[]{:S(2)}) %collective-permute-start.5) | collective-permute-done | bytes 393248 | tf_op jit(solution)/shard_map/ppermute | solution.py:415
  52.1 0.1 share_kernel.1
  52.2 6.8 %collective-permute-start.6 = (f32[2,3,128,128]{3,2,1,0:T(8,128)S(1)}, f32[2,3,128,128]{3,2,1,0:T(8,128)S(1)}, u32[]{:S(2)}, u32[]{:S(2)}) collective-permute-start(f32[2,3,128,128]{3,2,1,0:T(8,128)S(1)} %get-tuple-element.44), channel_id=1, source_target_pairs={{0,16},{32,48},{64,80},{96,112},{128,144},{160,176},{192,208},{224... | collective-permute-start | bytes 1179656 | tf_op jit(solution)/shard_map/ppermute | solution.py:415
  59.0 5.4 %collective-permute-start.7 = (f32[2,3,128,128]{3,2,1,0:T(8,128)S(1)}, f32[2,3,128,128]{3,2,1,0:T(8,128)S(1)}, u32[]{:S(2)}, u32[]{:S(2)}) collective-permute-start(f32[2,3,128,128]{3,2,1,0:T(8,128)S(1)} %get-tuple-element.45), channel_id=1, source_target_pairs={{16,32},{48,64},{80,96},{112,128},{144,160},{176,192},{208,224},{3... | collective-permute-start | bytes 1179656 | tf_op jit(solution)/shard_map/ppermute | solution.py:415
  64.4 3.2 %collective-permute-done.6.near = f32[2,3,128,128]{3,2,1,0:T(8,128)S(1)} collective-permute-done((f32[2,3,128,128]{3,2,1,0:T(8,128)S(1)}, f32[2,3,128,128]{3,2,1,0:T(8,128)S(1)}, u32[]{:S(2)}, u32[]{:S(2)}) %collective-permute-start.6) | collective-permute-done | bytes 393248 | tf_op jit(solution)/shard_map/ppermute | solution.py:415
  67.6 5.3 %collective-permute-done.7.far = f32[2,3,128,128]{3,2,1,0:T(8,128)S(1)} collective-permute-done((f32[2,3,128,128]{3,2,1,0:T(8,128)S(1)}, f32[2,3,128,128]{3,2,1,0:T(8,128)S(1)}, u32[]{:S(2)}, u32[]{:S(2)}) %collective-permute-start.7) | collective-permute-done | bytes 393248 | tf_op jit(solution)/shard_map/ppermute | solution.py:415
  72.9 0.1 update_kernel.1
  73.0 0.1 collective-permute-start.8
  73.1 4.9 %collective-permute-start.9 = (f32[3,256,128]{2,1,0:T(8,128)S(1)}, f32[3,256,128]{2,1,0:T(8,128)S(1)}, u32[]{:S(2)}, u32[]{:S(2)}) collective-permute-start(f32[3,256,128]{2,1,0:T(8,128)S(1)} %get-tuple-element.47.second.mid_2), channel_id=1, source_target_pairs={{1,2},{3,4},{5,6},{7,8},{9,10},{11,12},{13,14},{2,1},{4,3},{6,5},{... | collective-permute-start | bytes 1179656 | tf_op jit(solution)/shard_map/ppermute | solution.py:415
  78.0 0.0 collective-permute-done.8.near
  78.0 10.3 %collective-permute-done.9.far = f32[3,256,128]{2,1,0:T(8,128)S(1)} collective-permute-done((f32[3,256,128]{2,1,0:T(8,128)S(1)}, f32[3,256,128]{2,1,0:T(8,128)S(1)}, u32[]{:S(2)}, u32[]{:S(2)}) %collective-permute-start.9) | collective-permute-done | bytes 393248 | tf_op jit(solution)/shard_map/ppermute | solution.py:415
  88.4 7.2 %step_kernel.3 = (f32[3,256,128]{2,1,0:T(8,128)S(1)}, f32[3,256,128]{2,1,0:T(8,128)S(1)}, f32[3,256,128]{2,1,0:T(8,128)S(1)}, f32[3,256,128]{2,1,0:T(8,128)S(1)}) custom-call(f32[3,256,128]{2,1,0:T(8,128)S(1)} %get-tuple-element.46.first.mid_1, f32[3,256,128]{2,1,0:T(8,128)S(1)} %get-tuple-element.47.second.mid_2, ...), custom_call_target="tpu_custom_call" | custom-call | tf_op jit(solution)/shard_map/step_kernel/pallas_call | solution.py:229
  95.6 0.1 collective-permute-start.10
  95.7 4.7 %collective-permute-start.11 = (f32[3,256,128]{2,1,0:T(8,128)S(1)}, f32[3,256,128]{2,1,0:T(8,128)S(1)}, u32[]{:S(2)}, u32[]{:S(2)}) collective-permute-start(f32[3,256,128]{2,1,0:T(8,128)S(1)} %get-tuple-element.51), channel_id=1, source_target_pairs={{1,2},{3,4},{5,6},{7,8},{9,10},{11,12},{13,14},{2,1},{4,3},{6,5},{... | collective-permute-start | bytes 1179656 | tf_op jit(solution)/shard_map/ppermute | solution.py:415
  100.4 0.0 collective-permute-done.10.came_1
  100.4 10.5 %collective-permute-done.11.came_2 = f32[3,256,128]{2,1,0:T(8,128)S(1)} collective-permute-done((f32[3,256,128]{2,1,0:T(8,128)S(1)}, f32[3,256,128]{2,1,0:T(8,128)S(1)}, u32[]{:S(2)}, u32[]{:S(2)}) %collective-permute-start.11) | collective-permute-done | bytes 393248 | tf_op jit(solution)/shard_map/ppermute | solution.py:415
  110.8 0.1 close_kernel.1
  110.9 8.0 %collective-permute-start.12 = (f32[2,3,64,128]{3,2,1,0:T(8,128)S(1)}, f32[2,3,64,128]{3,2,1,0:T(8,128)S(1)}, u32[]{:S(2)}, u32[]{:S(2)}) collective-permute-start(f32[2,3,64,128]{3,2,1,0:T(8,128)S(1)} %get-tuple-element.53), channel_id=1, source_target_pairs={{0,16},{32,48},{64,80},{96,112},{128,144},{160,176},{192,208},{224... | collective-permute-start | bytes 589832 | tf_op jit(solution)/shard_map/ppermute | solution.py:415
  118.9 2.6 %collective-permute-start.13 = (f32[2,3,64,128]{3,2,1,0:T(8,128)S(1)}, f32[2,3,64,128]{3,2,1,0:T(8,128)S(1)}, u32[]{:S(2)}, u32[]{:S(2)}) collective-permute-start(f32[2,3,64,128]{3,2,1,0:T(8,128)S(1)} %get-tuple-element.54), channel_id=1, source_target_pairs={{16,32},{48,64},{80,96},{112,128},{144,160},{176,192},{208,224},{3... | collective-permute-start | bytes 589832 | tf_op jit(solution)/shard_map/ppermute | solution.py:415
  121.6 1.0 collective-permute-done.12.near
  122.6 6.6 %collective-permute-done.13.far = f32[2,3,64,128]{3,2,1,0:T(8,128)S(1)} collective-permute-done((f32[2,3,64,128]{3,2,1,0:T(8,128)S(1)}, f32[2,3,64,128]{3,2,1,0:T(8,128)S(1)}, u32[]{:S(2)}, u32[]{:S(2)}) %collective-permute-start.13) | collective-permute-done | bytes 196640 | tf_op jit(solution)/shard_map/ppermute | solution.py:415
  129.2 0.9 finish_kernel.1
  (1 shorter events, 0.0 us)
Async XLA Ops:
  0.0 18.5 %copy-start.1 = (f32[2,256,256]{2,1,0:T(8,128)S(1)}, f32[2,256,256]{2,1,0:T(8,128)}, u32[]{:S(2)}) copy-start(f32[2,256,256]{2,1,0:T(8,128)} %probe.1) | copy-start | bytes 1572868
  1.3 6.7 %collective-permute-start = (f32[2,3,64,128]{3,2,1,0:T(8,128)S(1)}, f32[2,3,64,128]{3,2,1,0:T(8,128)S(1)}, u32[]{:S(2)}, u32[]{:S(2)}) collective-permute-start(f32[2,3,64,128]{3,2,1,0:T(8,128)S(1)} %get-tuple-element.32), channel_id=1, source_target_pairs={{0,16},{32,48},{64,80},{96,112},{128,144},{160,176},{192,208},{224... | collective-permute-start | bytes 589832 | tf_op jit(solution)/shard_map/ppermute | solution.py:415
  2.4 11.8 %collective-permute-start.1 = (f32[2,3,64,128]{3,2,1,0:T(8,128)S(1)}, f32[2,3,64,128]{3,2,1,0:T(8,128)S(1)}, u32[]{:S(2)}, u32[]{:S(2)}) collective-permute-start(f32[2,3,64,128]{3,2,1,0:T(8,128)S(1)} %get-tuple-element.33), channel_id=1, source_target_pairs={{16,32},{48,64},{80,96},{112,128},{144,160},{176,192},{208,224},{3... | collective-permute-start | bytes 589832 | tf_op jit(solution)/shard_map/ppermute | solution.py:415
  14.2 4.3 %copy-start.2 = (f32[256,256]{1,0:T(8,128)S(1)}, f32[256,256]{1,0:T(8,128)}, u32[]{:S(2)}) copy-start(f32[256,256]{1,0:T(8,128)} %phase.1) | copy-start | bytes 786436
  14.2 4.3 %copy-start.3 = (f32[1,1,1,256,256]{4,3,2,1,0:T(8,128)S(1)}, f32[1,1,1,256,256]{4,3,2,1,0:T(8,128)}, u32[]{:S(2)}) copy-start(f32[1,1,1,256,256]{4,3,2,1,0:T(8,128)} %param.10) | copy-start | bytes 786436
  14.3 8.3 %collective-permute-start.2 = (f32[3,256,128]{2,1,0:T(8,128)S(1)}, f32[3,256,128]{2,1,0:T(8,128)S(1)}, u32[]{:S(2)}, u32[]{:S(2)}) collective-permute-start(f32[3,256,128]{2,1,0:T(8,128)S(1)} %get-tuple-element.34.first.mid_1), channel_id=1, source_target_pairs={{0,1},{2,3},{4,5},{6,7},{8,9},{10,11},{12,13},{14,15},{1,0},{3,2},... | collective-permute-start | bytes 1179656 | tf_op jit(solution)/shard_map/ppermute | solution.py:415
  14.4 15.2 %collective-permute-start.3 = (f32[3,256,128]{2,1,0:T(8,128)S(1)}, f32[3,256,128]{2,1,0:T(8,128)S(1)}, u32[]{:S(2)}, u32[]{:S(2)}) collective-permute-start(f32[3,256,128]{2,1,0:T(8,128)S(1)} %get-tuple-element.35.second.mid_2), channel_id=1, source_target_pairs={{1,2},{3,4},{5,6},{7,8},{9,10},{11,12},{13,14},{2,1},{4,3},{6,5},{... | collective-permute-start | bytes 1179656 | tf_op jit(solution)/shard_map/ppermute | solution.py:415
  18.5 0.7 copy-start.5
  19.2 0.9 copy-start.4
  21.5 8.1 %copy-start = (bf16[4,2,256,256]{3,2,1,0:T(8,128)(2,1)S(1)}, bf16[4,2,256,256]{3,2,1,0:T(8,128)(2,1)}, u32[]{:S(2)}) copy-start(bf16[4,2,256,256]{3,2,1,0:T(8,128)(2,1)} %constant.5.clone.tables) | copy-start | bytes 3145732
  36.8 4.2 %collective-permute-start.4 = (f32[3,256,128]{2,1,0:T(8,128)S(1)}, f32[3,256,128]{2,1,0:T(8,128)S(1)}, u32[]{:S(2)}, u32[]{:S(2)}) collective-permute-start(f32[3,256,128]{2,1,0:T(8,128)S(1)} %get-tuple-element.41), channel_id=1, source_target_pairs={{0,1},{2,3},{4,5},{6,7},{8,9},{10,11},{12,13},{14,15},{1,0},{3,2},... | collective-permute-start | bytes 1179656 | tf_op jit(solution)/shard_map/ppermute | solution.py:415
  36.9 15.2 %collective-permute-start.5 = (f32[3,256,128]{2,1,0:T(8,128)S(1)}, f32[3,256,128]{2,1,0:T(8,128)S(1)}, u32[]{:S(2)}, u32[]{:S(2)}) collective-permute-start(f32[3,256,128]{2,1,0:T(8,128)S(1)} %get-tuple-element.42), channel_id=1, source_target_pairs={{1,2},{3,4},{5,6},{7,8},{9,10},{11,12},{13,14},{2,1},{4,3},{6,5},{... | collective-permute-start | bytes 1179656 | tf_op jit(solution)/shard_map/ppermute | solution.py:415
  52.2 15.4 %collective-permute-start.6 = (f32[2,3,128,128]{3,2,1,0:T(8,128)S(1)}, f32[2,3,128,128]{3,2,1,0:T(8,128)S(1)}, u32[]{:S(2)}, u32[]{:S(2)}) collective-permute-start(f32[2,3,128,128]{3,2,1,0:T(8,128)S(1)} %get-tuple-element.44), channel_id=1, source_target_pairs={{0,16},{32,48},{64,80},{96,112},{128,144},{160,176},{192,208},{224... | collective-permute-start | bytes 1179656 | tf_op jit(solution)/shard_map/ppermute | solution.py:415
  59.0 14.0 %collective-permute-start.7 = (f32[2,3,128,128]{3,2,1,0:T(8,128)S(1)}, f32[2,3,128,128]{3,2,1,0:T(8,128)S(1)}, u32[]{:S(2)}, u32[]{:S(2)}) collective-permute-start(f32[2,3,128,128]{3,2,1,0:T(8,128)S(1)} %get-tuple-element.45), channel_id=1, source_target_pairs={{16,32},{48,64},{80,96},{112,128},{144,160},{176,192},{208,224},{3... | collective-permute-start | bytes 1179656 | tf_op jit(solution)/shard_map/ppermute | solution.py:415
  73.0 5.0 %collective-permute-start.8 = (f32[3,256,128]{2,1,0:T(8,128)S(1)}, f32[3,256,128]{2,1,0:T(8,128)S(1)}, u32[]{:S(2)}, u32[]{:S(2)}) collective-permute-start(f32[3,256,128]{2,1,0:T(8,128)S(1)} %get-tuple-element.46.first.mid_1), channel_id=1, source_target_pairs={{0,1},{2,3},{4,5},{6,7},{8,9},{10,11},{12,13},{14,15},{1,0},{3,2},... | collective-permute-start | bytes 1179656 | tf_op jit(solution)/shard_map/ppermute | solution.py:415
  73.1 15.2 %collective-permute-start.9 = (f32[3,256,128]{2,1,0:T(8,128)S(1)}, f32[3,256,128]{2,1,0:T(8,128)S(1)}, u32[]{:S(2)}, u32[]{:S(2)}) collective-permute-start(f32[3,256,128]{2,1,0:T(8,128)S(1)} %get-tuple-element.47.second.mid_2), channel_id=1, source_target_pairs={{1,2},{3,4},{5,6},{7,8},{9,10},{11,12},{13,14},{2,1},{4,3},{6,5},{... | collective-permute-start | bytes 1179656 | tf_op jit(solution)/shard_map/ppermute | solution.py:415
  95.6 4.8 %collective-permute-start.10 = (f32[3,256,128]{2,1,0:T(8,128)S(1)}, f32[3,256,128]{2,1,0:T(8,128)S(1)}, u32[]{:S(2)}, u32[]{:S(2)}) collective-permute-start(f32[3,256,128]{2,1,0:T(8,128)S(1)} %get-tuple-element.50), channel_id=1, source_target_pairs={{0,1},{2,3},{4,5},{6,7},{8,9},{10,11},{12,13},{14,15},{1,0},{3,2},... | collective-permute-start | bytes 1179656 | tf_op jit(solution)/shard_map/ppermute | solution.py:415
  95.7 15.2 %collective-permute-start.11 = (f32[3,256,128]{2,1,0:T(8,128)S(1)}, f32[3,256,128]{2,1,0:T(8,128)S(1)}, u32[]{:S(2)}, u32[]{:S(2)}) collective-permute-start(f32[3,256,128]{2,1,0:T(8,128)S(1)} %get-tuple-element.51), channel_id=1, source_target_pairs={{1,2},{3,4},{5,6},{7,8},{9,10},{11,12},{13,14},{2,1},{4,3},{6,5},{... | collective-permute-start | bytes 1179656 | tf_op jit(solution)/shard_map/ppermute | solution.py:415
  110.9 11.7 %collective-permute-start.12 = (f32[2,3,64,128]{3,2,1,0:T(8,128)S(1)}, f32[2,3,64,128]{3,2,1,0:T(8,128)S(1)}, u32[]{:S(2)}, u32[]{:S(2)}) collective-permute-start(f32[2,3,64,128]{3,2,1,0:T(8,128)S(1)} %get-tuple-element.53), channel_id=1, source_target_pairs={{0,16},{32,48},{64,80},{96,112},{128,144},{160,176},{192,208},{224... | collective-permute-start | bytes 589832 | tf_op jit(solution)/shard_map/ppermute | solution.py:415
  118.9 10.2 %collective-permute-start.13 = (f32[2,3,64,128]{3,2,1,0:T(8,128)S(1)}, f32[2,3,64,128]{3,2,1,0:T(8,128)S(1)}, u32[]{:S(2)}, u32[]{:S(2)}) collective-permute-start(f32[2,3,64,128]{3,2,1,0:T(8,128)S(1)} %get-tuple-element.54), channel_id=1, source_target_pairs={{16,32},{48,64},{80,96},{112,128},{144,160},{176,192},{208,224},{3... | collective-permute-start | bytes 589832 | tf_op jit(solution)/shard_map/ppermute | solution.py:415

commit v7 on v5

--- a/solution.py
+++ b/solution.py
@@ -288,16 +288,17 @@
     return call(open_kernel, (HALF, HALF, RIMS, RIMS), count=1)(core)
 
 
-def margin_kernel(near, far, first, second):
-    even = even_row()
-    for k, margin in enumerate((first, second)):
+def assemble_kernel(core_1, core_2, near, far, first, second):
+    even = even_row()
+    for k, (core, mid) in enumerate(((core_1, first), (core_2, second))):
         for layer in range(SLICES):
-            margin[layer, :MARGIN] = jnp.where(even, near[k, layer], far[k, layer])
-            margin[layer, MARGIN:] = jnp.where(even, far[k, layer], near[k, layer])
-
-
-def margins(*args):
-    return call(margin_kernel, (HALF, HALF), count=2)(*args)
+            mid[layer, :CORE] = core[layer]
+            mid[layer, CORE : CORE + MARGIN] = jnp.where(even, near[k, layer], far[k, layer])
+            mid[layer, CORE + MARGIN :] = jnp.where(even, far[k, layer], near[k, layer])
+
+
+def assemble(*args):
+    return call(assemble_kernel, (PACK, PACK), count=4)(*args)
 
 
 def share_kernel(part_1, part_2, came_1, came_2, total, send_near, send_far):
@@ -317,12 +318,12 @@
     return call(share_kernel, ((2, *PACK), (2, *HALF), (2, *HALF)), count=4)(*args)
 
 
-def update_kernel(core_1, core_2, margin_1, margin_2, total, near, far, new_1, new_2):
+def update_kernel(mid_1, mid_2, total, near, far, new_1, new_2):
     even = even_row()
     row = lax.axis_index("ty")
     above = jnp.where(row == 0, 0.0, STEP_SIZE)
     below = jnp.where(row == lax.axis_size("ty") - 1, 0.0, STEP_SIZE)
-    for k, (mid, new) in enumerate((((core_1, margin_1), new_1), ((core_2, margin_2), new_2))):
+    for k, (mid, new) in enumerate(((mid_1, new_1), (mid_2, new_2))):
         for layer in range(SLICES):
             e, o = near[k, layer], far[k, layer]
             down = jnp.where(even, e, o)
@@ -336,12 +337,11 @@
                 )
             ):
                 rows = pl.ds(n * MARGIN, MARGIN)
-                old = mid[n // 2][layer, pl.ds(n % 2 * MARGIN, MARGIN)]
-                new[layer, rows] = old - scale * (total[k, layer, rows] + added)
+                new[layer, rows] = mid[layer, rows] - scale * (total[k, layer, rows] + added)
 
 
 def update(*args):
-    return call(update_kernel, (PACK, PACK), count=7)(*args)
+    return call(update_kernel, (PACK, PACK), count=5)(*args)
 
 
 def close_kernel(part_1, part_2, came_1, came_2, send_near, send_far):
@@ -399,22 +399,20 @@
 def shards(object_field, probe, propagator_phase, patterns, scan_positions):
     first, second, near, far = begin(object_field)
     near, far = swap_rows(near, far)
-    core_near, core_far = swap_cols(first, second)
     lit, phase, ordered = setup(
         scan_positions[0, 0, 0], probe, propagator_phase, patterns[0, 0, 0], order_table()
     )
     wave = jnp.stack([jnp.cos(phase), jnp.sin(phase)])
     tables = jnp.asarray(half_tables())
     shared = (lit, wave, ordered, tables)
-    margin_1, margin_2 = margins(near, far)
-    rim_near, rim_far = swap_cols(margin_1, margin_2)
-    taken = (first, margin_1, second, margin_2, core_near, rim_near, core_far, rim_far)
-    parts, (near,), (far,) = step(2, 1, *taken, *shared)
+    first, second = assemble(first, second, near, far)
+    near, far = swap_cols(first, second)
+    parts, (near,), (far,) = step(1, 1, first, second, near, far, *shared)
 
     near, far = swap_cols(near, far)
     total, near, far = share(*parts, near, far)
     near, far = swap_rows(near, far)
-    first, second = update(first, second, margin_1, margin_2, total, near, far)
+    first, second = update(first, second, total, near, far)
     near, far = swap_cols(first, second)
     parts, near, far = step(1, 2, first, second, near, far, *shared)
 

time: 138 us -> 129 us (0.935)
  the two profiles are of different devices: /device:TPU:31 before, /device:TPU:232 now
where the time goes in v7:
time: 129 us; the launch traced here: 127 us
  starting transfers between devices  55.5 us (43%)
  waiting for transfers between devices  50.4 us (39%)
  Pallas kernels  17.1 us (13%)
  local copies, waits for them, and re-layouts  3.55 us (3%)
    ppermute x16, starting transfers between devices, swap(): return lax.ppermute(block, axis, pairs + [(j, i) for i, j in pairs])  55.5 us
    ppermute x16, waiting for transfers between devices, swap(): return lax.ppermute(block, axis, pairs + [(j, i) for i, j in pairs])  50.4 us
    pallas_call x2, Pallas kernels, step(): call(functools.partial(step_kernel, blocks, cuts), (PACK, PACK) + ((PACK,...  14.4 us
    unnamed x14, local copies, waits for them, and re-layouts  2.58 us
  transfers between devices with their start and end apart: 16, of which 9 were waited for; matrix products, arithmetic and copies ran while one was open for 1% of the time, Pallas kernels for 1%

profile of v7, /device:TPU:232, one launch (start us, length us, event | category | flops | bytes accessed | tf_op | source)
XLA Modules:
  0.0 127.0 jit_solution(13122117417214209521)
XLA Ops:
  0.0 0.0 copy-start.2
  0.0 1.0 copy-done.2
  1.0 0.0 copy-start.1
  1.0 0.1 open_kernel.1
  1.1 1.1 collective-permute-start
  2.2 4.8 %collective-permute-start.1 = (f32[2,3,64,128]{3,2,1,0:T(8,128)S(1)}, f32[2,3,64,128]{3,2,1,0:T(8,128)S(1)}, u32[]{:S(2)}, u32[]{:S(2)}) collective-permute-start(f32[2,3,64,128]{3,2,1,0:T(8,128)S(1)} %get-tuple-element.34), channel_id=1, source_target_pairs={{16,32},{48,64},{80,96},{112,128},{144,160},{176,192},{208,224},{3... | collective-permute-start | bytes 589832 | tf_op jit(solution)/shard_map/ppermute | solution.py:385
  7.0 0.8 collective-permute-done.near
  7.9 6.2 %collective-permute-done.1.far = f32[2,3,64,128]{3,2,1,0:T(8,128)S(1)} collective-permute-done((f32[2,3,64,128]{3,2,1,0:T(8,128)S(1)}, f32[2,3,64,128]{3,2,1,0:T(8,128)S(1)}, u32[]{:S(2)}, u32[]{:S(2)}) %collective-permute-start.1) | collective-permute-done | bytes 196640 | tf_op jit(solution)/shard_map/ppermute | solution.py:385
  14.1 0.0 copy-start.3
  14.1 0.0 copy-start.4
  14.1 0.1 assemble_kernel.1
  14.1 0.1 collective-permute-start.2
  14.2 4.1 %collective-permute-start.3 = (f32[3,256,128]{2,1,0:T(8,128)S(1)}, f32[3,256,128]{2,1,0:T(8,128)S(1)}, u32[]{:S(2)}, u32[]{:S(2)}) collective-permute-start(f32[3,256,128]{2,1,0:T(8,128)S(1)} %get-tuple-element.36.refs_1_.mid_2), channel_id=1, source_target_pairs={{1,2},{3,4},{5,6},{7,8},{9,10},{11,12},{13,14},{2,1},{4,3},{6,5},{... | collective-permute-start | bytes 1179656 | tf_op jit(solution)/shard_map/ppermute | solution.py:385
  18.4 0.0 copy-start.6
  18.4 0.0 copy-done.1
  18.4 0.0 copy-done.3
  18.4 0.0 copy-done.4
  18.4 0.6 copy-done.6
  19.0 0.0 copy-start.5
  19.0 0.9 copy-done.5
  20.0 1.4 %setup_kernel.1 = (f32[2,256,256]{2,1,0:T(8,128)S(1)}, f32[256,256]{1,0:T(8,128)S(1)}, f32[256,256]{1,0:T(8,128)S(1)}) custom-call(s32[2]{0:T(128)S(1)} %bitcast.7, f32[2,256,256]{2,1,0:T(8,128)S(1)} %copy-done.1, f32[256,256]{1,0:T(8,128)S(1)} %copy-done.3, f32[256,256]{1,0:T(8,128)S(1)} %bitcast.6, bf16[2,256,256]{2,1,0:T(8,128)(2,1)S(1)} %copy-done.5), custom_call_target="tpu_custom_call" | custom-call | tf_op jit(solution)/shard_map/setup_kernel/pallas_call | solution.py:273
  21.4 0.0 copy-start
  21.4 1.0 cosine_bitcast_fusion
  22.4 0.0 collective-permute-done.2.refs_2_
  22.4 7.0 %collective-permute-done.3.refs_3_ = f32[3,256,128]{2,1,0:T(8,128)S(1)} collective-permute-done((f32[3,256,128]{2,1,0:T(8,128)S(1)}, f32[3,256,128]{2,1,0:T(8,128)S(1)}, u32[]{:S(2)}, u32[]{:S(2)}) %collective-permute-start.3) | collective-permute-done | bytes 393248 | tf_op jit(solution)/shard_map/ppermute | solution.py:385
  29.5 0.0 copy-done
  29.5 7.2 %step_kernel.2 = (f32[3,256,128]{2,1,0:T(8,128)S(1)}, f32[3,256,128]{2,1,0:T(8,128)S(1)}, f32[3,256,128]{2,1,0:T(8,128)S(1)}, f32[3,256,128]{2,1,0:T(8,128)S(1)}) custom-call(f32[3,256,128]{2,1,0:T(8,128)S(1)} %get-tuple-element.35.refs_0_.mid_1, f32[3,256,128]{2,1,0:T(8,128)S(1)} %get-tuple-element.36.refs_1_.mid_2, ...), custom_call_target="tpu_custom_call" | custom-call | tf_op jit(solution)/shard_map/step_kernel/pallas_call | solution.py:233
  36.7 0.1 collective-permute-start.4
  36.8 4.1 %collective-permute-start.5 = (f32[3,256,128]{2,1,0:T(8,128)S(1)}, f32[3,256,128]{2,1,0:T(8,128)S(1)}, u32[]{:S(2)}, u32[]{:S(2)}) collective-permute-start(f32[3,256,128]{2,1,0:T(8,128)S(1)} %get-tuple-element.43), channel_id=1, source_target_pairs={{1,2},{3,4},{5,6},{7,8},{9,10},{11,12},{13,14},{2,1},{4,3},{6,5},{... | collective-permute-start | bytes 1179656 | tf_op jit(solution)/shard_map/ppermute | solution.py:385
  40.9 0.0 collective-permute-done.4.came_1
  40.9 11.0 %collective-permute-done.5.came_2 = f32[3,256,128]{2,1,0:T(8,128)S(1)} collective-permute-done((f32[3,256,128]{2,1,0:T(8,128)S(1)}, f32[3,256,128]{2,1,0:T(8,128)S(1)}, u32[]{:S(2)}, u32[]{:S(2)}) %collective-permute-start.5) | collective-permute-done | bytes 393248 | tf_op jit(solution)/shard_map/ppermute | solution.py:385
  51.9 0.1 share_kernel.1
  52.0 6.8 %collective-permute-start.6 = (f32[2,3,128,128]{3,2,1,0:T(8,128)S(1)}, f32[2,3,128,128]{3,2,1,0:T(8,128)S(1)}, u32[]{:S(2)}, u32[]{:S(2)}) collective-permute-start(f32[2,3,128,128]{3,2,1,0:T(8,128)S(1)} %get-tuple-element.45), channel_id=1, source_target_pairs={{0,16},{32,48},{64,80},{96,112},{128,144},{160,176},{192,208},{224... | collective-permute-start | bytes 1179656 | tf_op jit(solution)/shard_map/ppermute | solution.py:385
  58.8 5.5 %collective-permute-start.7 = (f32[2,3,128,128]{3,2,1,0:T(8,128)S(1)}, f32[2,3,128,128]{3,2,1,0:T(8,128)S(1)}, u32[]{:S(2)}, u32[]{:S(2)}) collective-permute-start(f32[2,3,128,128]{3,2,1,0:T(8,128)S(1)} %get-tuple-element.46), channel_id=1, source_target_pairs={{16,32},{48,64},{80,96},{112,128},{144,160},{176,192},{208,224},{3... | collective-permute-start | bytes 1179656 | tf_op jit(solution)/shard_map/ppermute | solution.py:385
  64.3 3.2 %collective-permute-done.6.near = f32[2,3,128,128]{3,2,1,0:T(8,128)S(1)} collective-permute-done((f32[2,3,128,128]{3,2,1,0:T(8,128)S(1)}, f32[2,3,128,128]{3,2,1,0:T(8,128)S(1)}, u32[]{:S(2)}, u32[]{:S(2)}) %collective-permute-start.6) | collective-permute-done | bytes 393248 | tf_op jit(solution)/shard_map/ppermute | solution.py:385
  67.5 5.3 %collective-permute-done.7.far = f32[2,3,128,128]{3,2,1,0:T(8,128)S(1)} collective-permute-done((f32[2,3,128,128]{3,2,1,0:T(8,128)S(1)}, f32[2,3,128,128]{3,2,1,0:T(8,128)S(1)}, u32[]{:S(2)}, u32[]{:S(2)}) %collective-permute-start.7) | collective-permute-done | bytes 393248 | tf_op jit(solution)/shard_map/ppermute | solution.py:385
  72.8 0.1 update_kernel.1
  72.9 0.1 collective-permute-start.8
  73.0 4.9 %collective-permute-start.9 = (f32[3,256,128]{2,1,0:T(8,128)S(1)}, f32[3,256,128]{2,1,0:T(8,128)S(1)}, u32[]{:S(2)}, u32[]{:S(2)}) collective-permute-start(f32[3,256,128]{2,1,0:T(8,128)S(1)} %get-tuple-element.48.refs_1_.mid_2), channel_id=1, source_target_pairs={{1,2},{3,4},{5,6},{7,8},{9,10},{11,12},{13,14},{2,1},{4,3},{6,5},{... | collective-permute-start | bytes 1179656 | tf_op jit(solution)/shard_map/ppermute | solution.py:385
  77.9 0.0 collective-permute-done.8.refs_2_
  77.9 10.3 %collective-permute-done.9.refs_3_ = f32[3,256,128]{2,1,0:T(8,128)S(1)} collective-permute-done((f32[3,256,128]{2,1,0:T(8,128)S(1)}, f32[3,256,128]{2,1,0:T(8,128)S(1)}, u32[]{:S(2)}, u32[]{:S(2)}) %collective-permute-start.9) | collective-permute-done | bytes 393248 | tf_op jit(solution)/shard_map/ppermute | solution.py:385
  88.2 7.2 %step_kernel.3 = (f32[3,256,128]{2,1,0:T(8,128)S(1)}, f32[3,256,128]{2,1,0:T(8,128)S(1)}, f32[3,128,128]{2,1,0:T(8,128)S(1)}, f32[3,128,128]{2,1,0:T(8,128)S(1)}...) custom-call(f32[3,256,128]{2,1,0:T(8,128)S(1)} %get-tuple-element.47.refs_0_.mid_1, ...), custom_call_target="tpu_custom_call" | custom-call | tf_op jit(solution)/shard_map/step_kernel/pallas_call | solution.py:233
  95.4 0.1 collective-permute-start.12
  95.5 4.7 %collective-permute-start.13 = (f32[3,128,128]{2,1,0:T(8,128)S(1)}, f32[3,128,128]{2,1,0:T(8,128)S(1)}, u32[]{:S(2)}, u32[]{:S(2)}) collective-permute-start(f32[3,128,128]{2,1,0:T(8,128)S(1)} %get-tuple-element.54), channel_id=1, source_target_pairs={{1,2},{3,4},{5,6},{7,8},{9,10},{11,12},{13,14},{2,1},{4,3},{6,5},{... | collective-permute-start | bytes 589832 | tf_op jit(solution)/shard_map/ppermute | solution.py:385
  100.2 0.1 collective-permute-start.10
  100.3 6.9 %collective-permute-start.11 = (f32[3,128,128]{2,1,0:T(8,128)S(1)}, f32[3,128,128]{2,1,0:T(8,128)S(1)}, u32[]{:S(2)}, u32[]{:S(2)}) collective-permute-start(f32[3,128,128]{2,1,0:T(8,128)S(1)} %get-tuple-element.52), channel_id=1, source_target_pairs={{1,2},{3,4},{5,6},{7,8},{9,10},{11,12},{13,14},{2,1},{4,3},{6,5},{... | collective-permute-start | bytes 589832 | tf_op jit(solution)/shard_map/ppermute | solution.py:385
  107.2 0.0 collective-permute-done.12.came_1
  107.2 1.3 %collective-permute-done.13.came_2 = f32[3,128,128]{2,1,0:T(8,128)S(1)} collective-permute-done((f32[3,128,128]{2,1,0:T(8,128)S(1)}, f32[3,128,128]{2,1,0:T(8,128)S(1)}, u32[]{:S(2)}, u32[]{:S(2)}) %collective-permute-start.13) | collective-permute-done | bytes 196640 | tf_op jit(solution)/shard_map/ppermute | solution.py:385
  108.6 7.1 %collective-permute-start.14 = (f32[2,3,64,128]{3,2,1,0:T(8,128)S(1)}, f32[2,3,64,128]{3,2,1,0:T(8,128)S(1)}, u32[]{:S(2)}, u32[]{:S(2)}) collective-permute-start(f32[2,3,64,128]{3,2,1,0:T(8,128)S(1)} %get-tuple-element.55), channel_id=1, source_target_pairs={{0,16},{32,48},{64,80},{96,112},{128,144},{160,176},{192,208},{224... | collective-permute-start | bytes 589832 | tf_op jit(solution)/shard_map/ppermute | solution.py:385
  115.7 5.1 %collective-permute-start.15 = (f32[2,3,64,128]{3,2,1,0:T(8,128)S(1)}, f32[2,3,64,128]{3,2,1,0:T(8,128)S(1)}, u32[]{:S(2)}, u32[]{:S(2)}) collective-permute-start(f32[2,3,64,128]{3,2,1,0:T(8,128)S(1)} %get-tuple-element.56), channel_id=1, source_target_pairs={{16,32},{48,64},{80,96},{112,128},{144,160},{176,192},{208,224},{3... | collective-permute-start | bytes 589832 | tf_op jit(solution)/shard_map/ppermute | solution.py:385
  120.8 0.0 collective-permute-done.10.came_1
  120.8 0.0 collective-permute-done.11.came_2
  120.8 0.0 collective-permute-done.14.near
  120.8 5.2 %collective-permute-done.15.far = f32[2,3,64,128]{3,2,1,0:T(8,128)S(1)} collective-permute-done((f32[2,3,64,128]{3,2,1,0:T(8,128)S(1)}, f32[2,3,64,128]{3,2,1,0:T(8,128)S(1)}, u32[]{:S(2)}, u32[]{:S(2)}) %collective-permute-start.15) | collective-permute-done | bytes 196640 | tf_op jit(solution)/shard_map/ppermute | solution.py:385
  126.1 0.9 finish_kernel.1
  (2 shorter events, 0.1 us)
Async XLA Ops:
  0.0 1.0 copy-start.2
  1.0 17.4 %copy-start.1 = (f32[2,256,256]{2,1,0:T(8,128)S(1)}, f32[2,256,256]{2,1,0:T(8,128)}, u32[]{:S(2)}) copy-start(f32[2,256,256]{2,1,0:T(8,128)} %probe.1) | copy-start | bytes 1572868
  1.1 6.7 %collective-permute-start = (f32[2,3,64,128]{3,2,1,0:T(8,128)S(1)}, f32[2,3,64,128]{3,2,1,0:T(8,128)S(1)}, u32[]{:S(2)}, u32[]{:S(2)}) collective-permute-start(f32[2,3,64,128]{3,2,1,0:T(8,128)S(1)} %get-tuple-element.33), channel_id=1, source_target_pairs={{0,16},{32,48},{64,80},{96,112},{128,144},{160,176},{192,208},{224... | collective-permute-start | bytes 589832 | tf_op jit(solution)/shard_map/ppermute | solution.py:385
  2.2 11.8 %collective-permute-start.1 = (f32[2,3,64,128]{3,2,1,0:T(8,128)S(1)}, f32[2,3,64,128]{3,2,1,0:T(8,128)S(1)}, u32[]{:S(2)}, u32[]{:S(2)}) collective-permute-start(f32[2,3,64,128]{3,2,1,0:T(8,128)S(1)} %get-tuple-element.34), channel_id=1, source_target_pairs={{16,32},{48,64},{80,96},{112,128},{144,160},{176,192},{208,224},{3... | collective-permute-start | bytes 589832 | tf_op jit(solution)/shard_map/ppermute | solution.py:385
  14.1 4.3 %copy-start.3 = (f32[256,256]{1,0:T(8,128)S(1)}, f32[256,256]{1,0:T(8,128)}, u32[]{:S(2)}) copy-start(f32[256,256]{1,0:T(8,128)} %phase.1) | copy-start | bytes 786436
  14.1 4.3 %copy-start.4 = (f32[1,1,1,256,256]{4,3,2,1,0:T(8,128)S(1)}, f32[1,1,1,256,256]{4,3,2,1,0:T(8,128)}, u32[]{:S(2)}) copy-start(f32[1,1,1,256,256]{4,3,2,1,0:T(8,128)} %param.10) | copy-start | bytes 786436
  14.1 8.3 %collective-permute-start.2 = (f32[3,256,128]{2,1,0:T(8,128)S(1)}, f32[3,256,128]{2,1,0:T(8,128)S(1)}, u32[]{:S(2)}, u32[]{:S(2)}) collective-permute-start(f32[3,256,128]{2,1,0:T(8,128)S(1)} %get-tuple-element.35.refs_0_.mid_1), channel_id=1, source_target_pairs={{0,1},{2,3},{4,5},{6,7},{8,9},{10,11},{12,13},{14,15},{1,0},{3,2},... | collective-permute-start | bytes 1179656 | tf_op jit(solution)/shard_map/ppermute | solution.py:385
  14.2 15.2 %collective-permute-start.3 = (f32[3,256,128]{2,1,0:T(8,128)S(1)}, f32[3,256,128]{2,1,0:T(8,128)S(1)}, u32[]{:S(2)}, u32[]{:S(2)}) collective-permute-start(f32[3,256,128]{2,1,0:T(8,128)S(1)} %get-tuple-element.36.refs_1_.mid_2), channel_id=1, source_target_pairs={{1,2},{3,4},{5,6},{7,8},{9,10},{11,12},{13,14},{2,1},{4,3},{6,5},{... | collective-permute-start | bytes 1179656 | tf_op jit(solution)/shard_map/ppermute | solution.py:385
  18.4 0.7 copy-start.6
  19.0 0.9 copy-start.5
  21.4 8.1 %copy-start = (bf16[4,2,256,256]{3,2,1,0:T(8,128)(2,1)S(1)}, bf16[4,2,256,256]{3,2,1,0:T(8,128)(2,1)}, u32[]{:S(2)}) copy-start(bf16[4,2,256,256]{3,2,1,0:T(8,128)(2,1)} %constant.5.clone.refs_7_) | copy-start | bytes 3145732
  36.7 4.2 %collective-permute-start.4 = (f32[3,256,128]{2,1,0:T(8,128)S(1)}, f32[3,256,128]{2,1,0:T(8,128)S(1)}, u32[]{:S(2)}, u32[]{:S(2)}) collective-permute-start(f32[3,256,128]{2,1,0:T(8,128)S(1)} %get-tuple-element.42), channel_id=1, source_target_pairs={{0,1},{2,3},{4,5},{6,7},{8,9},{10,11},{12,13},{14,15},{1,0},{3,2},... | collective-permute-start | bytes 1179656 | tf_op jit(solution)/shard_map/ppermute | solution.py:385
  36.8 15.2 %collective-permute-start.5 = (f32[3,256,128]{2,1,0:T(8,128)S(1)}, f32[3,256,128]{2,1,0:T(8,128)S(1)}, u32[]{:S(2)}, u32[]{:S(2)}) collective-permute-start(f32[3,256,128]{2,1,0:T(8,128)S(1)} %get-tuple-element.43), channel_id=1, source_target_pairs={{1,2},{3,4},{5,6},{7,8},{9,10},{11,12},{13,14},{2,1},{4,3},{6,5},{... | collective-permute-start | bytes 1179656 | tf_op jit(solution)/shard_map/ppermute | solution.py:385
  52.0 15.5 %collective-permute-start.6 = (f32[2,3,128,128]{3,2,1,0:T(8,128)S(1)}, f32[2,3,128,128]{3,2,1,0:T(8,128)S(1)}, u32[]{:S(2)}, u32[]{:S(2)}) collective-permute-start(f32[2,3,128,128]{3,2,1,0:T(8,128)S(1)} %get-tuple-element.45), channel_id=1, source_target_pairs={{0,16},{32,48},{64,80},{96,112},{128,144},{160,176},{192,208},{224... | collective-permute-start | bytes 1179656 | tf_op jit(solution)/shard_map/ppermute | solution.py:385
  58.8 14.0 %collective-permute-start.7 = (f32[2,3,128,128]{3,2,1,0:T(8,128)S(1)}, f32[2,3,128,128]{3,2,1,0:T(8,128)S(1)}, u32[]{:S(2)}, u32[]{:S(2)}) collective-permute-start(f32[2,3,128,128]{3,2,1,0:T(8,128)S(1)} %get-tuple-element.46), channel_id=1, source_target_pairs={{16,32},{48,64},{80,96},{112,128},{144,160},{176,192},{208,224},{3... | collective-permute-start | bytes 1179656 | tf_op jit(solution)/shard_map/ppermute | solution.py:385
  72.9 5.0 %collective-permute-start.8 = (f32[3,256,128]{2,1,0:T(8,128)S(1)}, f32[3,256,128]{2,1,0:T(8,128)S(1)}, u32[]{:S(2)}, u32[]{:S(2)}) collective-permute-start(f32[3,256,128]{2,1,0:T(8,128)S(1)} %get-tuple-element.47.refs_0_.mid_1), channel_id=1, source_target_pairs={{0,1},{2,3},{4,5},{6,7},{8,9},{10,11},{12,13},{14,15},{1,0},{3,2},... | collective-permute-start | bytes 1179656 | tf_op jit(solution)/shard_map/ppermute | solution.py:385
  73.0 15.2 %collective-permute-start.9 = (f32[3,256,128]{2,1,0:T(8,128)S(1)}, f32[3,256,128]{2,1,0:T(8,128)S(1)}, u32[]{:S(2)}, u32[]{:S(2)}) collective-permute-start(f32[3,256,128]{2,1,0:T(8,128)S(1)} %get-tuple-element.48.refs_1_.mid_2), channel_id=1, source_target_pairs={{1,2},{3,4},{5,6},{7,8},{9,10},{11,12},{13,14},{2,1},{4,3},{6,5},{... | collective-permute-start | bytes 1179656 | tf_op jit(solution)/shard_map/ppermute | solution.py:385
  95.4 11.8 %collective-permute-start.12 = (f32[3,128,128]{2,1,0:T(8,128)S(1)}, f32[3,128,128]{2,1,0:T(8,128)S(1)}, u32[]{:S(2)}, u32[]{:S(2)}) collective-permute-start(f32[3,128,128]{2,1,0:T(8,128)S(1)} %get-tuple-element.53), channel_id=1, source_target_pairs={{0,1},{2,3},{4,5},{6,7},{8,9},{10,11},{12,13},{14,15},{1,0},{3,2},... | collective-permute-start | bytes 589832 | tf_op jit(solution)/shard_map/ppermute | solution.py:385
  95.5 13.0 %collective-permute-start.13 = (f32[3,128,128]{2,1,0:T(8,128)S(1)}, f32[3,128,128]{2,1,0:T(8,128)S(1)}, u32[]{:S(2)}, u32[]{:S(2)}) collective-permute-start(f32[3,128,128]{2,1,0:T(8,128)S(1)} %get-tuple-element.54), channel_id=1, source_target_pairs={{1,2},{3,4},{5,6},{7,8},{9,10},{11,12},{13,14},{2,1},{4,3},{6,5},{... | collective-permute-start | bytes 589832 | tf_op jit(solution)/shard_map/ppermute | solution.py:385
  100.2 20.6 %collective-permute-start.10 = (f32[3,128,128]{2,1,0:T(8,128)S(1)}, f32[3,128,128]{2,1,0:T(8,128)S(1)}, u32[]{:S(2)}, u32[]{:S(2)}) collective-permute-start(f32[3,128,128]{2,1,0:T(8,128)S(1)} %get-tuple-element.51), channel_id=1, source_target_pairs={{0,1},{2,3},{4,5},{6,7},{8,9},{10,11},{12,13},{14,15},{1,0},{3,2},... | collective-permute-start | bytes 589832 | tf_op jit(solution)/shard_map/ppermute | solution.py:385
  100.3 20.5 %collective-permute-start.11 = (f32[3,128,128]{2,1,0:T(8,128)S(1)}, f32[3,128,128]{2,1,0:T(8,128)S(1)}, u32[]{:S(2)}, u32[]{:S(2)}) collective-permute-start(f32[3,128,128]{2,1,0:T(8,128)S(1)} %get-tuple-element.52), channel_id=1, source_target_pairs={{1,2},{3,4},{5,6},{7,8},{9,10},{11,12},{13,14},{2,1},{4,3},{6,5},{... | collective-permute-start | bytes 589832 | tf_op jit(solution)/shard_map/ppermute | solution.py:385
  108.6 12.2 %collective-permute-start.14 = (f32[2,3,64,128]{3,2,1,0:T(8,128)S(1)}, f32[2,3,64,128]{3,2,1,0:T(8,128)S(1)}, u32[]{:S(2)}, u32[]{:S(2)}) collective-permute-start(f32[2,3,64,128]{3,2,1,0:T(8,128)S(1)} %get-tuple-element.55), channel_id=1, source_target_pairs={{0,16},{32,48},{64,80},{96,112},{128,144},{160,176},{192,208},{224... | collective-permute-start | bytes 589832 | tf_op jit(solution)/shard_map/ppermute | solution.py:385
  115.7 10.4 %collective-permute-start.15 = (f32[2,3,64,128]{3,2,1,0:T(8,128)S(1)}, f32[2,3,64,128]{3,2,1,0:T(8,128)S(1)}, u32[]{:S(2)}, u32[]{:S(2)}) collective-permute-start(f32[2,3,64,128]{3,2,1,0:T(8,128)S(1)} %get-tuple-element.56), channel_id=1, source_target_pairs={{16,32},{48,64},{80,96},{112,128},{144,160},{176,192},{208,224},{3... | collective-permute-start | bytes 589832 | tf_op jit(solution)/shard_map/ppermute | solution.py:385
